TPU v7x, 32 devices: a whole 2x2x4 slice. The times are simulated.
32 devices in a mesh: freq: 16 (over z, x, core), lat: 2 (over y).
Axes of the slice: x: 2, y: 2, z: 4, core: 2. Of those that a mesh axis runs over, the one named last changes fastest.
Arguments:
- frequencies: float32 [16], P('freq'), may hold values from 0.3 to 1.5
- slowness: float32 [2, 32, 1024], P(None, 'lat', 'freq'), may hold values from 0.5 to 1.5
- src_field: float32 [16, 2, 32, 1024], P('freq', None, 'lat'), may hold values from -6 to 6
- rec_field: float32 [16, 2, 32, 1024], P('freq', None, 'lat'), may hold values from -6 to 6
Outputs:
- depth_image: float32 [2, 32, 1024], P(None, 'lat', 'freq')
- src_final: float32 [16, 2, 32, 1024], P('freq', None, 'lat')
- rec_final: float32 [16, 2, 32, 1024], P('freq', None, 'lat')
All inputs are finite; a program needn't handle non-finite values.
Results may differ from a plain program's by a relative error of at most 0.0003.
Values sent between devices are 32-bit elements; how exact they have to be, the bound alone decides.
No kernel may reach another device: no remote copies, remote signals or barrier semaphores. Data moves between devices by JAX's collectives and lax.ppermute only.
A program may use at most 64 MiB of HBM per device.

v0:
```python
import functools
import math

import jax
import jax.numpy as jnp
from jax import lax
from jax.experimental import pallas as pl
from jax.experimental.pallas import tpu as pltpu
from jax.sharding import PartitionSpec as P

TERMS = 8
LANES = 128

damping = 0.1

SIN2 = (2.0, -0.3333333134651184, 0.01666657254099846, -0.0003966305812355131, 5.3452554311661515e-06)
COS = (1.0, -0.49999991059303284, 0.04166615381836891, -0.0013878209283575416, 2.3889762815088034e-05)


def horner(powers, x):
    total = powers[-1] * x + powers[-2]
    for power in powers[-3::-1]:
        total = total * x + power
    return total


def node_phases(wavenum):
    square = wavenum * wavenum
    absorb = damping * square
    absorb_square = absorb * absorb
    half_absorb = 0.5 * absorb
    phases = []
    for node in range(TERMS):
        angle = math.pi * (node + 0.5) / TERMS
        excess = square - angle * angle
        modulus_square = excess * excess + absorb_square
        modulus = modulus_square * lax.rsqrt(modulus_square)
        larger_square = 0.5 * (modulus + jnp.abs(excess))
        inverse = lax.rsqrt(larger_square)
        larger = larger_square * inverse
        smaller = half_absorb * inverse
        propagating = excess >= 0
        real_part = jnp.where(propagating, larger, smaller)
        imag_part = jnp.where(propagating, smaller, larger)
        attenuation = jnp.exp(-imag_part)
        half = 0.5 * real_part
        half_square = half * half
        sine2 = half * horner(SIN2, half_square)
        cosine = horner(COS, half_square)
        phases.append((attenuation * (1.0 - 0.5 * (sine2 * sine2)), attenuation * (sine2 * cosine)))
    return phases


def cosine_sums(values):
    half = TERMS // 2
    both = [values[j] + values[TERMS - 1 - j] for j in range(half)]
    apart = [values[j] - values[TERMS - 1 - j] for j in range(half)]
    outer, inner = both[0] + both[3], both[1] + both[2]
    outer_gap, inner_gap = both[0] - both[3], both[1] - both[2]
    scale = 2.0 / TERMS
    c1, c2, c3 = (scale * math.cos(math.pi * m / 8) for m in (1, 2, 3))
    sums = [None] * TERMS
    sums[0] = (1.0 / TERMS) * (outer + inner)
    sums[4] = c2 * (outer - inner)
    sums[2] = c1 * outer_gap + c3 * inner_gap
    sums[6] = c3 * outer_gap - c1 * inner_gap
    for order in range(1, TERMS, 2):
        row = [scale * math.cos(order * math.pi * (j + 0.5) / TERMS) for j in range(half)]
        sums[order] = (row[0] * apart[0] + row[1] * apart[1]) + (row[2] * apart[2] + row[3] * apart[3])
    return sums


def migrate_kernel(setup, place_ref, freq_ref, slow_ref, *refs):
    rows, tiles, depth_steps, two, packed, width = setup
    blocks = 2 if two else 3
    fields, refs = refs[: 2 * blocks], refs[2 * blocks :]
    image_ref, src_ref, rec_ref, levels, coefs = refs
    flip = place_ref[0]
    reach = TERMS - 1
    low_margin = 0 if two else reach
    lowest = -depth_steps * low_margin
    slow_rows = (blocks + depth_steps - 1) * rows if depth_steps > 1 else blocks * rows

    lane = lax.broadcasted_iota(jnp.int32, (tiles, LANES), 1)
    tile = lax.broadcasted_iota(jnp.int32, (tiles, LANES), 0)
    first_lane, last_lane = lane == 0, lane == LANES - 1
    first_tile, last_tile = tile == 0, tile == tiles - 1

    def spread(values):
        left = pltpu.roll(values, 1, 1)
        right = pltpu.roll(values, LANES - 1, 1)
        before = jnp.where(first_tile, 0.0, pltpu.roll(left, 1, 0))
        after = jnp.where(last_tile, 0.0, pltpu.roll(right, tiles - 1, 0))
        left = jnp.where(first_lane, before, left)
        right = jnp.where(last_lane, after, right)
        return (values + values) + (left + right)

    def strided(row):
        return (row // 8) * 8 * tiles + row % 8

    def local_start(row):
        if not two:
            return strided(row)
        here, there = strided(row), strided(rows - 1 - row)
        return here + flip * (there - here)

    def fetch(pair, part, row):
        if 0 <= row < rows:
            ref, start = fields[pair * blocks], local_start(row)
        elif two:
            here, there = strided(row - rows), strided(2 * rows - 1 - row)
            ref, start = fields[pair * blocks + 1], here + flip * (there - here)
        elif row < 0:
            ref, start = fields[pair * blocks + 1], strided(rows + row)
        else:
            ref, start = fields[pair * blocks + 2], strided(row - rows)
        return ref[part, pl.ds(start, tiles, stride=8), :]

    for pair in range(2):
        for row in range(lowest, rows + depth_steps * reach):
            real, imag = fetch(pair, 0, row), fetch(pair, 1, row)
            levels[0, 2 * pair, row - lowest] = real
            levels[0, 2 * pair + 1, row - lowest] = -imag if pair else imag

    images = []
    for step in range(depth_steps):
        later = depth_steps - 1 - step
        low, high = -low_margin * later, rows + reach * later

        def slow_row(row, step=step):
            own = row if not two else row + flip * (rows - 1 - 2 * row)
            if step:
                return (blocks + step - 1) * rows + own
            if two:
                other = row + flip * (3 * rows - 1 - 2 * row)
                return jnp.where(row < rows, own, other)
            return jnp.where(row < 0, 2 * rows + row, jnp.where(row < rows, row, row + rows))

        def coefficient_row(row, carry, step=step):
            slow = slow_ref[pl.ds(slow_row(row), tiles, stride=slow_rows), :]
            phases = node_phases(freq_ref[0] * slow)
            for part in range(2):
                for order, value in enumerate(cosine_sums([p[part] for p in phases])):
                    coefs[order, part, row - lowest] = value
            return carry

        lax.fori_loop(low, high, coefficient_row, 0)

        def chebyshev(field, carry, low=low, high=high):
            for order in range(1, TERMS):
                left = TERMS - 1 - order
                begin = low if two else low - left
                end = high + left
                above = None if two else spread(levels[order - 1, field, begin - 1 - lowest])
                here = spread(levels[order - 1, field, begin - lowest])
                for row in range(begin, end):
                    below = spread(levels[order - 1, field, row + 1 - lowest])
                    total = here + here + below
                    if above is not None:
                        total = total + above
                    centre = levels[order - 1, field, row - lowest]
                    if order == 1:
                        value = 0.125 * total - centre
                    else:
                        value = (0.25 * total - (centre + centre)) - levels[order - 2, field, row - lowest]
                    if not two and row < 0:
                        value = value * place_ref[1].astype(jnp.float32)
                    if not two and row >= rows:
                        value = value * place_ref[2].astype(jnp.float32)
                    levels[order, field, row - lowest] = value
                    above, here = here, below
            return carry

        lax.fori_loop(0, 4, chebyshev, 0)

        row_images = []
        for row in range(low, high):
            at = row - lowest
            outs = []
            for pair in range(2):
                real = imag = None
                for order in range(TERMS):
                    coef_re, coef_im = coefs[order, 0, at], coefs[order, 1, at]
                    field_re, field_im = levels[order, 2 * pair, at], levels[order, 2 * pair + 1, at]
                    term_re = coef_re * field_re - coef_im * field_im
                    term_im = coef_re * field_im + coef_im * field_re
                    real = term_re if real is None else real + term_re
                    imag = term_im if imag is None else imag + term_im
                outs += [real, imag]
            if later:
                for field in range(4):
                    levels[0, field, at] = outs[field]
            else:
                start = local_start(row)
                src_ref[0, pl.ds(start, tiles, stride=8), :] = outs[0]
                src_ref[1, pl.ds(start, tiles, stride=8), :] = outs[1]
                rec_ref[0, pl.ds(start, tiles, stride=8), :] = outs[2]
                rec_ref[1, pl.ds(start, tiles, stride=8), :] = -outs[3]
            if 0 <= row < rows:
                value = outs[0] * outs[2] - outs[1] * outs[3]
                if not packed:
                    image_ref[step, pl.ds(local_start(row), tiles, stride=8), :] = value
                elif not later:
                    first = images[0][row]
                    own = row if not two else row + flip * (rows - 1 - 2 * row)
                    in_low = lane < width
                    even = jnp.where(in_low, first, pltpu.roll(value, width, 1))
                    odd = jnp.where(in_low, pltpu.roll(first, width, 1), value)
                    image_ref[pl.ds(own, tiles, stride=2 * rows), :] = even
                    image_ref[pl.ds(rows + own, tiles, stride=2 * rows), :] = odd
                row_images.append(value)
        images.append(row_images)


def tiled(block):
    parts, rows, columns = block.shape
    split = block.reshape(parts, rows // 8, 8, columns // LANES, LANES)
    return split.transpose(0, 1, 3, 2, 4).reshape(parts, rows * columns // LANES, LANES)


def untiled(block, rows):
    parts, count, _ = block.shape
    tiles = count // rows
    split = block.reshape(parts, rows // 8, tiles, 8, LANES)
    return split.transpose(0, 1, 3, 2, 4).reshape(parts, rows, tiles * LANES)


def from_side(block, side):
    count = lax.axis_size("lat")
    links = [(i, i - side) for i in range(count) if 0 <= i - side < count]
    return lax.ppermute(block, "lat", links)


def from_sides(block):
    if lax.axis_size("lat") == 2:
        return [lax.ppermute(block, "lat", [(0, 1), (1, 0)])]
    return [from_side(block, -1), from_side(block, 1)]


def gather_columns(block):
    count = lax.axis_size("freq")
    me = lax.axis_index("freq")
    rows, width = block.shape
    bits = [1 << i for i in range(count.bit_length() - 1)]
    inner = [b for b in bits if b * width < LANES]
    outer = [b for b in bits if b * width >= LANES][::-1]

    def partner(held, bit):
        return lax.ppermute(held, "freq", [(i, i ^ bit) for i in range(count)])

    for bit in inner:
        other = partner(block, bit)
        upper = (me & bit) != 0
        block = jnp.concatenate([jnp.where(upper, other, block), jnp.where(upper, block, other)], axis=1)
    for depth, bit in enumerate(outer):
        other = partner(block, bit)
        upper = (me & bit) != 0
        block = jnp.stack([jnp.where(upper, other, block), jnp.where(upper, block, other)], axis=depth)
    return block.reshape((count * width // LANES) * rows, LANES)


def shards(frequencies, slowness, src_field, rec_field):
    depth_steps, rows, width = slowness.shape
    columns = src_field.shape[3]
    tiles = columns // LANES
    freq_count = lax.axis_size("freq")
    lat_count = lax.axis_size("lat")
    lat_index = lax.axis_index("lat")
    two = lat_count == 2
    packed = depth_steps == 2 and width * depth_steps == LANES
    norm_factor = 1.0 / math.sqrt(frequencies.shape[0] * freq_count)

    slow_sides = from_sides(slowness[0])
    src_sides, rec_sides = from_sides(src_field[0]), from_sides(rec_field[0])
    if two:
        slow_parts = [slowness[0], slow_sides[0]]
    else:
        slow_parts = [slowness[0], slow_sides[0], slow_sides[1]]
    slow_parts += [slowness[z] for z in range(1, depth_steps)]
    slow = gather_columns(jnp.concatenate(slow_parts, axis=0))

    place = jnp.stack(
        [lat_index if two else 0, (lat_index > 0).astype(jnp.int32), (lat_index < lat_count - 1).astype(jnp.int32)]
    ).astype(jnp.int32)
    fields = [tiled(x) for x in (src_field[0], *src_sides, rec_field[0], *rec_sides)]
    reach = TERMS - 1
    span = rows + depth_steps * reach * (1 if two else 2)
    image_shape = (freq_count * rows, LANES) if packed else (depth_steps, rows * tiles, LANES)
    field_shape = jax.ShapeDtypeStruct((2, rows * tiles, LANES), jnp.float32)
    setup = (rows, tiles, depth_steps, two, packed, width)
    image, src, rec = pl.pallas_call(
        functools.partial(migrate_kernel, setup),
        out_shape=(jax.ShapeDtypeStruct(image_shape, jnp.float32), field_shape, field_shape),
        in_specs=[pl.BlockSpec(memory_space=pltpu.SMEM)] * 2
        + [pl.BlockSpec(memory_space=pltpu.VMEM)] * (1 + len(fields)),
        out_specs=(pl.BlockSpec(memory_space=pltpu.VMEM),) * 3,
        scratch_shapes=[
            pltpu.VMEM((TERMS, 4, span, tiles, LANES), jnp.float32),
            pltpu.VMEM((TERMS, 2, span, tiles, LANES), jnp.float32),
        ],
        name="migrate",
    )(place, frequencies, slow, *fields)

    if packed:
        pieces = image.reshape(freq_count, rows, LANES)
        total = jnp.sum(lax.all_to_all(pieces, "freq", 0, 0, tiled=True), axis=0) * norm_factor
        depth_image = jnp.stack([total[:, z * width : (z + 1) * width] for z in range(depth_steps)])
    else:
        whole = untiled(image, rows).reshape(depth_steps, rows, freq_count, width)
        pieces = whole.transpose(2, 0, 1, 3)
        depth_image = jnp.sum(lax.all_to_all(pieces, "freq", 0, 0, tiled=True), axis=0) * norm_factor
    return (depth_image, untiled(src, rows)[None], untiled(rec, rows)[None])


def solution(mesh):
    placed = (
        P("freq"),
        P(None, "lat", "freq"),
        P("freq", None, "lat", None),
        P("freq", None, "lat", None),
    )
    return jax.shard_map(
        shards,
        mesh=mesh,
        in_specs=placed,
        out_specs=(
            P(None, "lat", "freq"),
            P("freq", None, "lat", None),
            P("freq", None, "lat", None),
        ),
        check_vma=False,
    )
```

profile of v0, /device:TPU:0, one launch (start us, length us, event | category | flops | bytes accessed | tf_op | source)
XLA Modules:
  0.0 48.3 jit_solution(9117788483697957263)
XLA Ops:
  0.6 0.7 %slice_bitcast_fusion.3 = (f32[16,64]{1,0:T(8,128)S(1)}, f32[16,64]{1,0:T(8,128)S(1)}) fusion(f32[2,16,64]{2,1,0:T(8,128)} %param.5), kind=kLoop, calls=%fused_computation.17 | loop fusion | bytes 16384 | tf_op jit(solution)/shard_map/squeeze | solution.py:276
  1.3 3.0 %collective-permute-start = (f32[16,64]{1,0:T(8,128)S(1)}, f32[16,64]{1,0:T(8,128)S(1)}, u32[]{:S(2)}, u32[]{:S(2)}) collective-permute-start(f32[16,64]{1,0:T(8,128)S(1)} %get-tuple-element.17), channel_id=1, source_target_pairs={{0,1},{1,0},{2,3},{3,2},{4,5},{5,4},{6,7},{7,6},{8,9},{9,8},{10,11... | collective-permute-start | bytes 12296 | tf_op jit(solution)/shard_map/ppermute | solution.py:236
  4.3 1.6 %collective-permute-done = f32[16,64]{1,0:T(8,128)S(1)} collective-permute-done((f32[16,64]{1,0:T(8,128)S(1)}, f32[16,64]{1,0:T(8,128)S(1)}, u32[]{:S(2)}, u32[]{:S(2)}) %collective-permute-start) | collective-permute-done | bytes 4128 | tf_op jit(solution)/shard_map/ppermute | solution.py:236
  6.0 0.0 collective-permute-start.1
  6.0 1.2 %collective-permute-done.1 = f32[48,64]{1,0:T(8,128)S(1)} collective-permute-done((f32[48,64]{1,0:T(8,128)S(1)}, f32[48,64]{1,0:T(8,128)S(1)}, u32[]{:S(2)}, u32[]{:S(2)}) %collective-permute-start.1) | collective-permute-done | bytes 12320 | tf_op jit(solution)/shard_map/ppermute | solution.py:249
  7.2 0.0 copy-start.1
  7.2 0.1 pad_maximum_fusion.4
  7.3 0.0 copy-start
  7.3 3.1 %collective-permute-start.2 = (f32[48,128]{1,0:T(8,128)S(1)}, f32[48,128]{1,0:T(8,128)S(1)}, u32[]{:S(2)}, u32[]{:S(2)}) collective-permute-start(f32[48,128]{1,0:T(8,128)S(1)} %pad_maximum_fusion.4), channel_id=1, source_target_pairs={{0,16},{2,18},{4,20},{6,22},{8,24},{10,26},{12,28},{14,30},{16,0},... | collective-permute-start | bytes 73736 | tf_op jit(solution)/shard_map/ppermute | solution.py:249
  10.4 1.8 %collective-permute-done.2 = f32[48,128]{1,0:T(8,128)S(1)} collective-permute-done((f32[48,128]{1,0:T(8,128)S(1)}, f32[48,128]{1,0:T(8,128)S(1)}, u32[]{:S(2)}, u32[]{:S(2)}) %collective-permute-start.2) | collective-permute-done | bytes 24608 | tf_op jit(solution)/shard_map/ppermute | solution.py:249
  12.2 0.1 select_bitcast_fusion.5
  12.3 2.0 %collective-permute-start.3 = (f32[2,48,128]{2,1,0:T(8,128)S(1)}, f32[2,48,128]{2,1,0:T(8,128)S(1)}, u32[]{:S(2)}, u32[]{:S(2)}) collective-permute-start(f32[2,48,128]{2,1,0:T(8,128)S(1)} %pad_maximum_fusion.2), channel_id=1, source_target_pairs={{0,8},{2,10},{4,12},{6,14},{8,0},{10,2},{12,4},{14,6},{16,24},{18,... | collective-permute-start | bytes 147464 | tf_op jit(solution)/shard_map/ppermute | solution.py:249
  14.3 0.0 copy-done.1
  14.3 1.5 %collective-permute-start.6 = (f32[2,16,1024]{2,1,0:T(8,128)S(1)}, f32[2,16,1024]{2,1,0:T(8,128)S(1)}, u32[]{:S(2)}, u32[]{:S(2)}) collective-permute-start(f32[2,16,1024]{2,1,0:T(8,128)S(1)} %bitcast.62), channel_id=1, source_target_pairs={{0,1},{1,0},{2,3},{3,2},{4,5},{5,4},{6,7},{7,6},{8,9},{9,8},{10,11... | collective-permute-start | bytes 393224 | tf_op jit(solution)/shard_map/ppermute | solution.py:236
  15.8 0.0 copy-done
  15.8 0.5 %collective-permute-start.5 = (f32[2,16,1024]{2,1,0:T(8,128)S(1)}, f32[2,16,1024]{2,1,0:T(8,128)S(1)}, u32[]{:S(2)}, u32[]{:S(2)}) collective-permute-start(f32[2,16,1024]{2,1,0:T(8,128)S(1)} %bitcast.60), channel_id=1, source_target_pairs={{0,1},{1,0},{2,3},{3,2},{4,5},{5,4},{6,7},{7,6},{8,9},{9,8},{10,11... | collective-permute-start | bytes 393224 | tf_op jit(solution)/shard_map/ppermute | solution.py:236
  16.9 0.0 collective-permute-done.3
  17.0 1.6 %collective-permute-start.4 = (f32[2,2,48,128]{3,2,0,1:T(8,128)S(1)}, f32[2,2,48,128]{3,2,0,1:T(8,128)S(1)}, u32[]{:S(2)}, u32[]{:S(2)}) collective-permute-start(f32[2,2,48,128]{3,2,0,1:T(8,128)S(1)} %pad_maximum_fusion.1), channel_id=1, source_target_pairs={{0,4},{2,6},{4,0},{6,2},{8,12},{10,14},{12,8},{14,10},{16,20},{18,... | collective-permute-start | bytes 294920 | tf_op jit(solution)/shard_map/ppermute | solution.py:249
  18.5 0.6 %pad_add_fusion.place_ref = s32[3]{0:T(128)} fusion(s32[1]{0:T(128)} %bitcast.2, s32[1]{0:T(128)} %bitcast.1, s32[1]{0:T(128)} %bitcast), kind=kLoop, calls=%fused_computation.19 | loop fusion | flops 6 | bytes 24 | tf_op jit(solution)/shard_map/stack | solution.py:282
  19.1 2.5 %collective-permute-done.4 = f32[2,2,48,128]{3,2,0,1:T(8,128)S(1)} collective-permute-done((f32[2,2,48,128]{3,2,0,1:T(8,128)S(1)}, f32[2,2,48,128]{3,2,0,1:T(8,128)S(1)}, u32[]{:S(2)}, u32[]{:S(2)}) %collective-permute-start.4) | collective-permute-done | bytes 98336 | tf_op jit(solution)/shard_map/ppermute | solution.py:249
  21.7 0.7 %copy.7 = f32[2,2,2,48,128]{4,3,2,1,0:T(8,128)} copy(f32[2,2,2,48,128]{4,3,0,1,2:T(8,128)S(1)} %pad_maximum_fusion) | data formatting | bytes 393216 | tf_op jit(solution)/shard_map/stack | solution.py:258
  22.4 0.0 collective-permute-done.6
  22.4 0.0 copy-start.2
  22.4 0.0 collective-permute-done.5
  22.4 0.0 copy-start.3
  22.4 0.6 %copy-done.2 = f32[2,16,1024]{2,1,0:T(8,128)} copy-done((f32[2,16,1024]{2,1,0:T(8,128)}, f32[2,16,1024]{2,1,0:T(8,128)S(1)}, u32[]{:S(2)}) %copy-start.2) | copy-done | bytes 131096
  23.0 0.1 copy-done.3
  23.1 10.7 %migrate.1 = (f32[256,128]{1,0:T(8,128)}, f32[2,128,128]{2,1,0:T(8,128)}, f32[2,128,128]{2,1,0:T(8,128)}) custom-call(s32[3]{0:T(128)} %pad_add_fusion.place_ref, f32[1]{0:T(128)S(6)} %copy.8.freq_ref, f32[384,128]{1,0:T(8,128)} %bitcast.57, f32[2,128,128]{2,1,0:T(8,128)} %bitcast.59, f32[2,128,128]{2,1,0:T(8,128)} %bitcast.64, f32[2,128,128]{2,1,0:T(8,128)} %bitcast.61, ...), custom_call_target="tpu_custom_call" | custom-call | tf_op jit(solution)/shard_map/migrate/pallas_call | solution.py:291
  33.8 13.8 %all_to_all.5 = f32[16,16,128]{2,1,0:T(8,128)S(1)} all-to-all(f32[16,16,128]{2,1,0:T(8,128)} %bitcast.58), channel_id=1, replica_groups=mesh['freq'=16,'lat'=2] {'freq'}, dimensions={0} | all-to-all | bytes 262144 | tf_op jit(solution)/shard_map/all_to_all | solution.py:306
  47.6 0.1 slice_bitcast_fusion.1
  47.7 0.6 %pad_maximum_fusion.5 = f32[2,16,64]{2,1,0:T(8,128)} fusion(f32[1,16,64]{2,1,0:T(8,128)S(1)} %get-tuple-element.20, f32[1,16,64]{2,1,0:T(8,128)S(1)} %get-tuple-element.19), kind=kLoop, calls=%fused_computation.11 | loop fusion | flops 2048 | bytes 16384 | tf_op jit(solution)/shard_map/stack | solution.py:307
  (9 shorter events, 0.1 us)
Async XLA Ops:
  1.3 4.6 %collective-permute-start = (f32[16,64]{1,0:T(8,128)S(1)}, f32[16,64]{1,0:T(8,128)S(1)}, u32[]{:S(2)}, u32[]{:S(2)}) collective-permute-start(f32[16,64]{1,0:T(8,128)S(1)} %get-tuple-element.17), channel_id=1, source_target_pairs={{0,1},{1,0},{2,3},{3,2},{4,5},{5,4},{6,7},{7,6},{8,9},{9,8},{10,11... | collective-permute-start | bytes 12296 | tf_op jit(solution)/shard_map/ppermute | solution.py:236
  6.0 1.2 %collective-permute-start.1 = (f32[48,64]{1,0:T(8,128)S(1)}, f32[48,64]{1,0:T(8,128)S(1)}, u32[]{:S(2)}, u32[]{:S(2)}) collective-permute-start(f32[48,64]{1,0:T(8,128)S(1)} %pad_maximum_fusion.3), channel_id=1, source_target_pairs={{0,2},{2,0},{4,6},{6,4},{8,10},{10,8},{12,14},{14,12},{16,18},{18,... | collective-permute-start | bytes 36872 | tf_op jit(solution)/shard_map/ppermute | solution.py:249
  7.2 7.1 %copy-start.1 = (f32[1,2,16,1024]{3,2,1,0:T(8,128)S(1)}, f32[1,2,16,1024]{3,2,1,0:T(8,128)}, u32[]{:S(2)}) copy-start(f32[1,2,16,1024]{3,2,1,0:T(8,128)} %param.7) | copy-start | bytes 393220
  7.3 8.5 %copy-start = (f32[1,2,16,1024]{3,2,1,0:T(8,128)S(1)}, f32[1,2,16,1024]{3,2,1,0:T(8,128)}, u32[]{:S(2)}) copy-start(f32[1,2,16,1024]{3,2,1,0:T(8,128)} %param.6) | copy-start | bytes 393220
  7.3 4.9 %collective-permute-start.2 = (f32[48,128]{1,0:T(8,128)S(1)}, f32[48,128]{1,0:T(8,128)S(1)}, u32[]{:S(2)}, u32[]{:S(2)}) collective-permute-start(f32[48,128]{1,0:T(8,128)S(1)} %pad_maximum_fusion.4), channel_id=1, source_target_pairs={{0,16},{2,18},{4,20},{6,22},{8,24},{10,26},{12,28},{14,30},{16,0},... | collective-permute-start | bytes 73736 | tf_op jit(solution)/shard_map/ppermute | solution.py:249
  12.3 4.7 %collective-permute-start.3 = (f32[2,48,128]{2,1,0:T(8,128)S(1)}, f32[2,48,128]{2,1,0:T(8,128)S(1)}, u32[]{:S(2)}, u32[]{:S(2)}) collective-permute-start(f32[2,48,128]{2,1,0:T(8,128)S(1)} %pad_maximum_fusion.2), channel_id=1, source_target_pairs={{0,8},{2,10},{4,12},{6,14},{8,0},{10,2},{12,4},{14,6},{16,24},{18,... | collective-permute-start | bytes 147464 | tf_op jit(solution)/shard_map/ppermute | solution.py:249
  14.3 8.2 %collective-permute-start.6 = (f32[2,16,1024]{2,1,0:T(8,128)S(1)}, f32[2,16,1024]{2,1,0:T(8,128)S(1)}, u32[]{:S(2)}, u32[]{:S(2)}) collective-permute-start(f32[2,16,1024]{2,1,0:T(8,128)S(1)} %bitcast.62), channel_id=1, source_target_pairs={{0,1},{1,0},{2,3},{3,2},{4,5},{5,4},{6,7},{7,6},{8,9},{9,8},{10,11... | collective-permute-start | bytes 393224 | tf_op jit(solution)/shard_map/ppermute | solution.py:236
  15.8 6.6 %collective-permute-start.5 = (f32[2,16,1024]{2,1,0:T(8,128)S(1)}, f32[2,16,1024]{2,1,0:T(8,128)S(1)}, u32[]{:S(2)}, u32[]{:S(2)}) collective-permute-start(f32[2,16,1024]{2,1,0:T(8,128)S(1)} %bitcast.60), channel_id=1, source_target_pairs={{0,1},{1,0},{2,3},{3,2},{4,5},{5,4},{6,7},{7,6},{8,9},{9,8},{10,11... | collective-permute-start | bytes 393224 | tf_op jit(solution)/shard_map/ppermute | solution.py:236
  17.0 4.7 %collective-permute-start.4 = (f32[2,2,48,128]{3,2,0,1:T(8,128)S(1)}, f32[2,2,48,128]{3,2,0,1:T(8,128)S(1)}, u32[]{:S(2)}, u32[]{:S(2)}) collective-permute-start(f32[2,2,48,128]{3,2,0,1:T(8,128)S(1)} %pad_maximum_fusion.1), channel_id=1, source_target_pairs={{0,4},{2,6},{4,0},{6,2},{8,12},{10,14},{12,8},{14,10},{16,20},{18,... | collective-permute-start | bytes 294920 | tf_op jit(solution)/shard_map/ppermute | solution.py:249
  22.4 0.6 %copy-start.2 = (f32[2,16,1024]{2,1,0:T(8,128)}, f32[2,16,1024]{2,1,0:T(8,128)S(1)}, u32[]{:S(2)}) copy-start(f32[2,16,1024]{2,1,0:T(8,128)S(1)} %collective-permute-done.6) | copy-start | bytes 393220
  22.4 0.7 %copy-start.3 = (f32[2,16,1024]{2,1,0:T(8,128)}, f32[2,16,1024]{2,1,0:T(8,128)S(1)}, u32[]{:S(2)}) copy-start(f32[2,16,1024]{2,1,0:T(8,128)S(1)} %collective-permute-done.5) | copy-start | bytes 393220
where the time goes:
time: 48.6 us; the launch traced here: 48.3 us
  blocking collectives  13.8 us (28%)
  starting transfers between devices  11.7 us (24%)
  Pallas kernels  10.7 us (22%)
  waiting for transfers between devices  7.14 us (15%)
  local copies, waits for them, and re-layouts  2.18 us (4%)
  other arithmetic  1.47 us (3%)
  between operations  1.38 us (3%)
    all_to_all x1, blocking collectives, shards(): lax.all_to_all(pieces, 'freq', 0, 0, tiled=True)  13.8 us
    pallas_call x1, Pallas kernels, shards(): pl.pallas_call(functools.partial(migrate_kernel, setup), out_shape=(jax.S...  10.7 us
    ppermute x4, starting transfers between devices, partner(): return lax.ppermute(held, 'freq', [(i, i ^ bit) for i in range(count)])  6.64 us
    ppermute x4, waiting for transfers between devices, partner(): return lax.ppermute(held, 'freq', [(i, i ^ bit) for i in range(count)])  5.51 us
    ppermute x3, starting transfers between devices, from_sides(): return [lax.ppermute(block, 'lat', [(0, 1), (1, 0)])]  5.02 us
    ppermute x3, waiting for transfers between devices, from_sides(): return [lax.ppermute(block, 'lat', [(0, 1), (1, 0)])]  1.63 us
  transfers between devices with their start and end apart: 7, of which 4 were waited for; matrix products, arithmetic and copies ran while one was open for 3% of the time, Pallas kernels for 0%

commit v1 on v0

v1 whole, which is shorter than its diff:
```python
import functools
import math

import jax
import jax.numpy as jnp
from jax import lax
from jax.experimental import pallas as pl
from jax.experimental.pallas import tpu as pltpu
from jax.sharding import PartitionSpec as P

TERMS = 8
REACH = TERMS - 1
LANES = 128
SUBLANES = 8

damping = 0.1

SINE = (0.5, -0.010416666045784950, 6.510379898820e-05, -1.9366727e-07, 3.26248263e-10)


def horner(powers, x):
    total = powers[-1] * x + powers[-2]
    for power in powers[-3::-1]:
        total = total * x + power
    return total


def node_phases(wavenum):
    square = wavenum * wavenum
    absorb = damping * square
    absorb_square = absorb * absorb
    phases = []
    for node in range(TERMS):
        angle = math.pi * (node + 0.5) / TERMS
        excess = square - angle * angle
        modulus_square = excess * excess + absorb_square
        doubled = modulus_square * lax.rsqrt(modulus_square) + jnp.abs(excess)
        inverse = lax.rsqrt(doubled)
        larger = doubled * inverse
        smaller = absorb * inverse
        propagating = excess >= 0
        real_part = jnp.where(propagating, larger, smaller)
        imag_part = jnp.where(propagating, smaller, larger)
        attenuation = jnp.exp(imag_part * -math.sqrt(0.5))
        sine = real_part * horner(SINE, real_part * real_part)
        sine_square = sine * sine
        rest = 2.0 - sine_square
        phase_re = attenuation * (1.0 - sine_square)
        phase_im = attenuation * (sine * (rest * lax.rsqrt(rest)))
        phases.append((phase_re, phase_im))
    return phases


def cosine_sums(values):
    half = TERMS // 2
    both = [values[j] + values[TERMS - 1 - j] for j in range(half)]
    apart = [values[j] - values[TERMS - 1 - j] for j in range(half)]
    outer, inner = both[0] + both[3], both[1] + both[2]
    outer_gap, inner_gap = both[0] - both[3], both[1] - both[2]
    scale = 2.0 / TERMS
    c1, c2, c3 = (scale * math.cos(math.pi * m / 8) for m in (1, 2, 3))
    sums = [None] * TERMS
    sums[0] = (1.0 / TERMS) * (outer + inner)
    sums[4] = c2 * (outer - inner)
    sums[2] = c1 * outer_gap + c3 * inner_gap
    sums[6] = c3 * outer_gap - c1 * inner_gap
    for order in range(1, TERMS, 2):
        row = [scale * math.cos(order * math.pi * (j + 0.5) / TERMS) for j in range(half)]
        sums[order] = (row[0] * apart[0] + row[1] * apart[1]) + (row[2] * apart[2] + row[3] * apart[3])
    return sums


def window(rows, later, two):
    return (0 if two else -REACH * later), rows + REACH * later


def strided(row, tiles):
    return (row // SUBLANES) * SUBLANES * tiles + row % SUBLANES


def either(flip, here, there):
    return here + flip * (there - here)


def spreader(tiles):
    lane = lax.broadcasted_iota(jnp.int32, (tiles, LANES), 1)
    tile = lax.broadcasted_iota(jnp.int32, (tiles, LANES), 0)
    first_lane, last_lane = lane == 0, lane == LANES - 1
    first_tile, last_tile = tile == 0, tile == tiles - 1

    def spread(values):
        left = pltpu.roll(values, 1, 1)
        right = pltpu.roll(values, LANES - 1, 1)
        before = jnp.where(first_tile, 0.0, pltpu.roll(left, 1, 0))
        after = jnp.where(last_tile, 0.0, pltpu.roll(right, tiles - 1, 0))
        left = jnp.where(first_lane, before, left)
        right = jnp.where(last_lane, after, right)
        return (values + values) + (left + right)

    return spread


def chebyshev(levels, fields, low, high, lowest, rows, two):
    spread = spreader(levels.shape[3])
    if not two:
        lat = lax.axis_index("lat")
        inside_low = (lat > 0).astype(jnp.float32)
        inside_high = (lat < lax.axis_size("lat") - 1).astype(jnp.float32)
    for order in range(1, TERMS):
        left = TERMS - 1 - order
        begin, end = (low if two else low - left), high + left
        above = [None if two else spread(levels[order - 1, f, begin - 1 - lowest]) for f in fields]
        here = [spread(levels[order - 1, f, begin - lowest]) for f in fields]
        for row in range(begin, end):
            for k, f in enumerate(fields):
                below = spread(levels[order - 1, f, row + 1 - lowest])
                total = (here[k] + here[k]) + below
                if above[k] is not None:
                    total = total + above[k]
                centre = levels[order - 1, f, row - lowest]
                if order == 1:
                    value = 0.125 * total - centre
                else:
                    value = (0.25 * total - (centre + centre)) - levels[order - 2, f, row - lowest]
                if not two and row < 0:
                    value = value * inside_low
                if not two and row >= rows:
                    value = value * inside_high
                levels[order, f, row - lowest] = value
                above[k], here[k] = here[k], below


def first_kernel(rows, depth_steps, two, conjugate, *refs):
    fields, levels = refs[:-1], refs[-1]
    tiles = levels.shape[3]
    flip = lax.axis_index("lat")
    low, high = window(rows, depth_steps - 1, two)
    lowest = low if two else low - REACH
    for row in range(lowest, high + REACH):
        if two:
            side = 0 if row < rows else 1
            ref, near = fields[side], row - side * rows
            start = either(flip, strided(near, tiles), strided(rows - 1 - near, tiles))
        else:
            side = 1 if row < 0 else 2 if row >= rows else 0
            ref, start = fields[side], strided(row + (0, rows, -rows)[side], tiles)
        for part in range(2):
            value = ref[part, pl.ds(start, tiles, stride=SUBLANES), :]
            levels[0, part, row - lowest] = -value if part and conjugate else value
    chebyshev(levels, (0, 1), low, high, lowest, rows, two)


def coefficient_kernel(bit, other, *refs):
    freq_ref, slow_ref, out_ref = refs[0], refs[1], refs[-1]
    count, rows, _ = slow_ref.shape
    slot = (lax.axis_index("freq") >> bit) & 1
    if other:
        slot = 1 - slot
    groups = rows // SUBLANES

    def body(index, carry):
        piece = index // groups
        start = pl.multiple_of((index % groups) * SUBLANES, SUBLANES)
        phases = node_phases(freq_ref[0] * slow_ref[piece, pl.ds(start, SUBLANES), :])
        for part in range(2):
            for order, value in enumerate(cosine_sums([p[part] for p in phases])):
                out_ref[order, part, 2 * piece + slot, pl.ds(start, SUBLANES), :] = value
        return carry

    lax.fori_loop(0, count * groups, body, 0)


def main_kernel(setup, coef_ref, src_levels, rec_levels, *refs):
    rows, halo, depth_steps, two, packed, width = setup
    image_refs, (src_ref, rec_ref, levels) = refs[:-3], refs[-3:]
    tiles = levels.shape[3]
    coef_rows = coef_ref.shape[2] // tiles
    flip = lax.axis_index("lat")
    lane = lax.broadcasted_iota(jnp.int32, (tiles, LANES), 1)
    tile = lax.broadcasted_iota(jnp.int32, (tiles, LANES), 0)
    in_low = lane < width
    if packed:
        parity, me, count = tile * 0, lax.axis_index("freq"), lax.axis_size("freq")
        for bit in range(count.bit_length() - 1):
            parity = parity ^ (tile >> bit) ^ (me >> bit)
        keeps_even = (parity & 1) == 0

    def own(row):
        return either(flip, row, rows - 1 - row) if two else row

    def own_start(row):
        return either(flip, strided(row, tiles), strided(rows - 1 - row, tiles)) if two else strided(row, tiles)

    def coef_row(step, row):
        sides = 1 if two else 2
        if step:
            return rows + sides * halo + (step - 1) * rows + own(row)
        if 0 <= row < rows:
            return own(row)
        if two:
            return rows + either(flip, row - rows, halo - 1 - (row - rows))
        return rows + halo + (row if row < 0 else row - rows)

    images = []
    for step in range(depth_steps):
        later = depth_steps - 1 - step
        low, high = window(rows, later, two)
        lowest = window(rows, max(later, 1), two)[0]
        if step:

            def pair_fields(pair, carry, low=low, high=high, lowest=lowest):
                chebyshev(levels, (2 * pair, 2 * pair + 1), low, high, lowest, rows, two)
                return carry

            lax.fori_loop(0, 2, pair_fields, 0)
        top = low if two else low - REACH
        next_lowest = window(rows, max(later - 1, 1), two)[0]
        row_images = []
        for row in range(low, high):
            start = coef_row(step, row)
            coefs = [
                [coef_ref[order, part, pl.ds(start, tiles, stride=coef_rows), :] for part in range(2)]
                for order in range(TERMS)
            ]
            outs = []
            for pair in range(2):
                real = imag = None
                for order, (coef_re, coef_im) in enumerate(coefs):
                    if step:
                        field_re = levels[order, 2 * pair, row - lowest]
                        field_im = levels[order, 2 * pair + 1, row - lowest]
                    else:
                        source = rec_levels if pair else src_levels
                        field_re, field_im = source[order, 0, row - top], source[order, 1, row - top]
                    term_re = coef_re * field_re - coef_im * field_im
                    term_im = coef_re * field_im + coef_im * field_re
                    real = term_re if real is None else real + term_re
                    imag = term_im if imag is None else imag + term_im
                outs += [real, imag]
            if later:
                for field in range(4):
                    levels[0, field, row - next_lowest] = outs[field]
            else:
                at = pl.ds(own_start(row), tiles, stride=SUBLANES)
                src_ref[0, at, :] = outs[0]
                src_ref[1, at, :] = outs[1]
                rec_ref[0, at, :] = outs[2]
                rec_ref[1, at, :] = -outs[3]
            if not 0 <= row < rows:
                continue
            value = outs[0] * outs[2] - outs[1] * outs[3]
            row_images.append(value)
            if not packed:
                image_refs[0][step, pl.ds(own_start(row), tiles, stride=SUBLANES), :] = value
            elif not later:
                first = images[0][row]
                even = jnp.where(in_low, first, pltpu.roll(value, width, 1))
                odd = jnp.where(in_low, pltpu.roll(first, width, 1), value)
                at = pl.ds(own(row), tiles, stride=rows)
                image_refs[0][at, :] = jnp.where(keeps_even, even, odd)
                image_refs[1][at, :] = jnp.where(keeps_even, odd, even)
        images.append(row_images)


def tiled(block):
    parts, rows, columns = block.shape
    split = block.reshape(parts, rows // SUBLANES, SUBLANES, columns // LANES, LANES)
    return split.transpose(0, 1, 3, 2, 4).reshape(parts, rows * columns // LANES, LANES)


def untiled(block, rows):
    parts, count, _ = block.shape
    tiles = count // rows
    split = block.reshape(parts, rows // SUBLANES, tiles, SUBLANES, LANES)
    return split.transpose(0, 1, 3, 2, 4).reshape(parts, rows, tiles * LANES)


def from_sides(block):
    count = lax.axis_size("lat")
    if count == 2:
        return [lax.ppermute(block, "lat", [(0, 1), (1, 0)])]
    return [
        lax.ppermute(block, "lat", [(i, i - side) for i in range(count) if 0 <= i - side < count]) for side in (-1, 1)
    ]


def partner(block, mask):
    return lax.ppermute(block, "freq", [(i, i ^ mask) for i in range(lax.axis_size("freq"))])


def gather_columns(block):
    count = lax.axis_size("freq")
    me = lax.axis_index("freq")
    width = block.shape[1]
    bits = range(count.bit_length() - 1)
    inner = [b for b in bits if width << b < LANES]
    outer = [b for b in bits if width << b >= LANES][::-1]
    for b in inner:
        other = partner(block, 1 << b)
        upper = (me >> b) & 1 != 0
        block = jnp.concatenate([jnp.where(upper, other, block), jnp.where(upper, block, other)], axis=1)
    block = block[None]
    for depth, b in enumerate(outer):
        other = partner(block, (1 << b) | (1 if inner else 0))
        if b == outer[-1]:
            return block, other, b
        upper = (me >> b) & 1 != 0
        low, high = jnp.where(upper, other, block), jnp.where(upper, block, other)
        block = jnp.stack([low, high], axis=1).reshape(2 * block.shape[0], *block.shape[1:])


def scatter_sum(keep, send, rows):
    count = lax.axis_size("freq")
    me = lax.axis_index("freq")
    held = (keep + partner(send, 1)).reshape(count // 2, rows, LANES)
    for b in range(1, count.bit_length() - 1):
        upper = (me >> b) & 1 != 0
        split = held.reshape(held.shape[0] // 2, 2, rows, LANES)
        low, high = split[:, 0], split[:, 1]
        held = jnp.where(upper, high, low) + partner(jnp.where(upper, low, high), (1 << b) | 1)
    return held[0]


def shards(frequencies, slowness, src_field, rec_field):
    depth_steps, rows, width = slowness.shape
    tiles = src_field.shape[3] // LANES
    freq_count = lax.axis_size("freq")
    flip = lax.axis_index("lat")
    two = lax.axis_size("lat") == 2
    packed = depth_steps == 2 and width * depth_steps == LANES
    norm_factor = 1.0 / math.sqrt(frequencies.shape[0] * freq_count)
    halo = -(-REACH * (depth_steps - 1) // SUBLANES) * SUBLANES
    low, high = window(rows, depth_steps - 1, two)
    span = high + REACH - (low if two else low - REACH)
    later_span = window(rows, 1, two)[1] - window(rows, 1, two)[0]

    slow_sides = from_sides(slowness)
    src_sides, rec_sides = from_sides(src_field), from_sides(rec_field)
    slow_parts = [slowness[0]]
    if two:
        slow_parts.append(jnp.where(flip == 0, slow_sides[0][0, :halo], slow_sides[0][0, rows - halo :]))
    else:
        slow_parts += [slow_sides[0][0, rows - halo :], slow_sides[1][0, :halo]]
    slow_parts += [slowness[z] for z in range(1, depth_steps)]
    mine, theirs, bit = gather_columns(jnp.concatenate(slow_parts, axis=0))
    coef_rows = mine.shape[1]

    smem, vmem = pl.BlockSpec(memory_space=pltpu.SMEM), pl.BlockSpec(memory_space=pltpu.VMEM)
    shape_of = functools.partial(jax.ShapeDtypeStruct, dtype=jnp.float32)

    def limit(mib):
        return pltpu.CompilerParams(vmem_limit_bytes=mib << 20)

    def first_levels(own, sides, conjugate):
        fields = [tiled(x[0]) for x in (own, *sides)]
        return pl.pallas_call(
            functools.partial(first_kernel, rows, depth_steps, two, conjugate),
            out_shape=shape_of((TERMS, 2, span, tiles, LANES)),
            in_specs=[vmem] * len(fields),
            out_specs=vmem,
            compiler_params=limit(4),
            cost_estimate=pl.CostEstimate(flops=1 << 26, bytes_accessed=1 << 22, transcendentals=0),
            name="first",
        )(*fields)

    src_levels = first_levels(src_field, src_sides, False)
    rec_levels = first_levels(rec_field, rec_sides, True)

    coef_shape = shape_of((TERMS, 2, tiles, coef_rows, LANES))

    def coefficients(other, *operands):
        return pl.pallas_call(
            functools.partial(coefficient_kernel, bit, other),
            out_shape=coef_shape,
            in_specs=[smem] + [vmem] * (len(operands) - 1),
            out_specs=vmem,
            input_output_aliases={2: 0} if other else {},
            compiler_params=limit(8),
            cost_estimate=pl.CostEstimate(flops=1 << 26, bytes_accessed=1 << 22, transcendentals=0),
            name="coefficients",
        )(*operands)

    coefs = coefficients(False, frequencies, mine)
    coefs = coefficients(True, frequencies, theirs, coefs)

    image_shape = shape_of((tiles * rows, LANES) if packed else (depth_steps, rows * tiles, LANES))
    field_shape = shape_of((2, rows * tiles, LANES))
    image_shapes = [image_shape] * (2 if packed else 1)
    setup = (rows, halo, depth_steps, two, packed, width)
    *image, src, rec = pl.pallas_call(
        functools.partial(main_kernel, setup),
        out_shape=(*image_shapes, field_shape, field_shape),
        in_specs=[vmem] * 3,
        out_specs=(vmem,) * (len(image_shapes) + 2),
        scratch_shapes=[pltpu.VMEM((TERMS, 4, later_span, tiles, LANES), jnp.float32)],
        compiler_params=limit(16),
        name="main",
    )(coefs.reshape(TERMS, 2, tiles * coef_rows, LANES), src_levels, rec_levels)

    if packed:
        total = scatter_sum(*image, rows) * norm_factor
        depth_image = jnp.stack([total[:, z * width : (z + 1) * width] for z in range(depth_steps)])
    else:
        whole = untiled(image[0], rows).reshape(depth_steps, rows, freq_count, width)
        pieces = whole.transpose(2, 0, 1, 3)
        depth_image = jnp.sum(lax.all_to_all(pieces, "freq", 0, 0, tiled=True), axis=0) * norm_factor
    return (depth_image, untiled(src, rows)[None], untiled(rec, rows)[None])


def solution(mesh):
    placed = (
        P("freq"),
        P(None, "lat", "freq"),
        P("freq", None, "lat", None),
        P("freq", None, "lat", None),
    )
    return jax.shard_map(
        shards,
        mesh=mesh,
        in_specs=placed,
        out_specs=(
            P(None, "lat", "freq"),
            P("freq", None, "lat", None),
            P("freq", None, "lat", None),
        ),
        check_vma=False,
    )
```

time: 48.6 us -> 40.5 us (0.83)
  blocking collectives: 13.8 us -> 0 us
  waiting for transfers between devices: 7.14 us -> 13.9 us
  starting transfers between devices: 11.7 us -> 15.4 us
  Pallas kernels: 10.7 us -> 7.9 us
  local copies, waits for them, and re-layouts: 2.18 us -> 0.83 us
  other arithmetic: 1.47 us -> 0.86 us
    all_to_all x1 -> x0, blocking collectives: 13.8 us -> none  [shards(): lax.all_to_all(pieces, 'freq', 0, 0, tiled=True)]
    ppermute x4 -> x8, waiting for transfers between devices: 5.51 us -> 10.5 us  [partner(): lax.ppermute(block, 'freq', [(i, i ^ mask) for i in range(lax.axis_size('...]
    ppermute x4 -> x8, starting transfers between devices: 6.64 us -> 10.3 us  [partner(): lax.ppermute(block, 'freq', [(i, i ^ mask) for i in range(lax.axis_size('...]
    pallas_call x1 -> x5, Pallas kernels: 10.7 us -> 7.9 us  [the longest x1 3.21 us: shards(): pl.pallas_call(functools.partial(main_kernel, setup), out_shape=(*image_s...]
    ppermute x3, waiting for transfers between devices: 1.63 us -> 3.39 us  [from_sides(): return [lax.ppermute(block, 'lat', [(0, 1), (1, 0)])]]
    another operation x1, local copies, waits for them, and re-layouts: 0.7 us -> 0.01 us  [gather_columns(): jnp.stack([low, high], axis=1).reshape(2 * block.shape[0], *block.shape[1:])]
    unnamed x8 -> x4, local copies, waits for them, and re-layouts: 0.69 us -> 0.01 us
    another operation x7 -> x3, other arithmetic: 0.75 us -> 0.1 us  [gather_columns(): jnp.stack([low, high], axis=1).reshape(2 * block.shape[0], *block.shape[1:])]
  transfers between devices with their start and end apart: 7 -> 11, of which waited for: 4 -> 9; matrix products, arithmetic and copies ran while one was open for 3% -> 2% of each run, Pallas kernels for 0% -> 8%
where the time goes in v1:
time: 40.5 us; the launch traced here: 40.3 us
  starting transfers between devices  15.4 us (38%)
  waiting for transfers between devices  13.9 us (34%)
  Pallas kernels  7.9 us (20%)
  between operations  1.4 us (3%)
  other arithmetic  0.86 us (2%)
  local copies, waits for them, and re-layouts  0.83 us (2%)
    ppermute x8, waiting for transfers between devices, partner(): lax.ppermute(block, 'freq', [(i, i ^ mask) for i in range(lax.axis_size('...  10.5 us
    ppermute x8, starting transfers between devices, partner(): lax.ppermute(block, 'freq', [(i, i ^ mask) for i in range(lax.axis_size('...  10.3 us
    ppermute x3, starting transfers between devices, from_sides(): return [lax.ppermute(block, 'lat', [(0, 1), (1, 0)])]  5.09 us
    ppermute x3, waiting for transfers between devices, from_sides(): return [lax.ppermute(block, 'lat', [(0, 1), (1, 0)])]  3.39 us
    pallas_call x1, Pallas kernels, shards(): pl.pallas_call(functools.partial(main_kernel, setup), out_shape=(*image_s...  3.21 us
    pallas_call x2, Pallas kernels, coefficients(): pl.pallas_call(functools.partial(coefficient_kernel, bit, other), out_sha...  2.95 us
    pallas_call x2, Pallas kernels, first_levels(): pl.pallas_call(functools.partial(first_kernel, rows, depth_steps, two, co...  1.75 us
  transfers between devices with their start and end apart: 11, of which 9 were waited for; matrix products, arithmetic and copies ran while one was open for 2% of the time, Pallas kernels for 8%

profile of v1, /device:TPU:0, one launch (start us, length us, event | category | flops | bytes accessed | tf_op | source)
XLA Modules:
  0.0 40.3 jit_solution(5001011164399068287)
XLA Ops:
  0.6 0.0 copy-start
  0.6 3.1 %collective-permute-start = (f32[2,16,64]{2,1,0:T(8,128)}, f32[2,16,64]{2,1,0:T(8,128)S(1)}, u32[]{:S(2)}, u32[]{:S(2)}) collective-permute-start(f32[2,16,64]{2,1,0:T(8,128)} %param.5), channel_id=1, source_target_pairs={{0,1},{1,0},{2,3},{3,2},{4,5},{5,4},{6,7},{7,6},{8,9},{9,8},{10,11... | collective-permute-start | bytes 24584 | tf_op jit(solution)/shard_map/ppermute | solution.py:281
  3.7 0.7 %slice_bitcast_fusion.5 = (f32[16,64]{1,0:T(8,128)S(1)}, f32[16,64]{1,0:T(8,128)S(1)}) fusion(f32[2,16,64]{2,1,0:T(8,128)} %param.5), kind=kLoop, calls=%fused_computation.27 | loop fusion | bytes 16384 | tf_op jit(solution)/shard_map/squeeze | solution.py:339
  4.4 1.2 %collective-permute-done = f32[2,16,64]{2,1,0:T(8,128)S(1)} collective-permute-done((f32[2,16,64]{2,1,0:T(8,128)}, f32[2,16,64]{2,1,0:T(8,128)S(1)}, u32[]{:S(2)}, u32[]{:S(2)}) %collective-permute-start) | collective-permute-done | bytes 8224 | tf_op jit(solution)/shard_map/ppermute | solution.py:281
  5.6 0.1 collective-permute-start.1
  5.7 1.2 %collective-permute-done.1 = f32[40,64]{1,0:T(8,128)S(1)} collective-permute-done((f32[40,64]{1,0:T(8,128)S(1)}, f32[40,64]{1,0:T(8,128)S(1)}, u32[]{:S(2)}, u32[]{:S(2)}) %collective-permute-start.1) | collective-permute-done | bytes 10272 | tf_op jit(solution)/shard_map/ppermute | solution.py:288
  6.9 0.1 maximum_bitcast_fusion.1
  7.0 2.9 %collective-permute-start.2 = (f32[1,40,128]{2,1,0:T(8,128)S(1)}, f32[1,40,128]{2,1,0:T(8,128)S(1)}, u32[]{:S(2)}, u32[]{:S(2)}) collective-permute-start(f32[1,40,128]{2,1,0:T(8,128)S(1)} %maximum_bitcast_fusion.1), channel_id=1, source_target_pairs={{0,18},{2,16},{4,22},{6,20},{8,26},{10,24},{12,30},{14,28},{16,2},... | collective-permute-start | bytes 61448 | tf_op jit(solution)/shard_map/ppermute | solution.py:288
  9.9 1.5 %collective-permute-done.2 = f32[1,40,128]{2,1,0:T(8,128)S(1)} collective-permute-done((f32[1,40,128]{2,1,0:T(8,128)S(1)}, f32[1,40,128]{2,1,0:T(8,128)S(1)}, u32[]{:S(2)}, u32[]{:S(2)}) %collective-permute-start.2) | collective-permute-done | bytes 20512 | tf_op jit(solution)/shard_map/ppermute | solution.py:288
  11.3 0.1 select_bitcast_fusion.4
  11.4 1.7 %collective-permute-start.3 = (f32[2,40,128]{2,1,0:T(8,128)S(1)}, f32[2,40,128]{2,1,0:T(8,128)S(1)}, u32[]{:S(2)}, u32[]{:S(2)}) collective-permute-start(f32[2,40,128]{2,1,0:T(8,128)S(1)} %maximum_bitcast_fusion), channel_id=1, source_target_pairs={{0,10},{2,8},{4,14},{6,12},{8,2},{10,0},{12,6},{14,4},{16,26},{18,... | collective-permute-start | bytes 122888 | tf_op jit(solution)/shard_map/ppermute | solution.py:288
  13.1 1.5 %collective-permute-start.5 = (f32[1,2,16,1024]{3,2,1,0:T(8,128)}, f32[1,2,16,1024]{3,2,1,0:T(8,128)S(1)}, u32[]{:S(2)}, u32[]{:S(2)}) collective-permute-start(f32[1,2,16,1024]{3,2,1,0:T(8,128)} %param.6), channel_id=1, source_target_pairs={{0,1},{1,0},{2,3},{3,2},{4,5},{5,4},{6,7},{7,6},{8,9},{9,8},{10,11... | collective-permute-start | bytes 393224 | tf_op jit(solution)/shard_map/ppermute | solution.py:281
  14.6 0.5 %collective-permute-start.6 = (f32[1,2,16,1024]{3,2,1,0:T(8,128)}, f32[1,2,16,1024]{3,2,1,0:T(8,128)S(1)}, u32[]{:S(2)}, u32[]{:S(2)}) collective-permute-start(f32[1,2,16,1024]{3,2,1,0:T(8,128)} %param.7), channel_id=1, source_target_pairs={{0,1},{1,0},{2,3},{3,2},{4,5},{5,4},{6,7},{7,6},{8,9},{9,8},{10,11... | collective-permute-start | bytes 393224 | tf_op jit(solution)/shard_map/ppermute | solution.py:281
  15.1 0.0 copy-start.1
  15.2 1.5 %collective-permute-start.4 = (f32[4,40,128]{2,1,0:T(8,128)S(1)}, f32[4,40,128]{2,1,0:T(8,128)S(1)}, u32[]{:S(2)}, u32[]{:S(2)}) collective-permute-start(f32[4,40,128]{2,1,0:T(8,128)S(1)} %bitcast.113), channel_id=1, source_target_pairs={{0,6},{2,4},{4,2},{6,0},{8,14},{10,12},{12,10},{14,8},{16,22},{18,... | collective-permute-start | bytes 245768 | tf_op jit(solution)/shard_map/ppermute | solution.py:288
  17.3 1.5 %coefficients.2.refs_2_ = f32[8,2,8,40,128]{4,3,2,1,0:T(8,128)S(1)} custom-call(f32[1]{0:T(128)S(6)} %copy.24.refs_0_, f32[4,40,128]{2,1,0:T(8,128)S(1)} %bitcast.114), custom_call_target="tpu_custom_call" | custom-call | flops 67108864 | bytes 4194304 | tf_op jit(solution)/shard_map/coefficients/pallas_call | solution.py:372
  18.8 0.9 %collective-permute-done.5 = f32[1,2,16,1024]{3,2,1,0:T(8,128)S(1)} collective-permute-done((f32[1,2,16,1024]{3,2,1,0:T(8,128)}, f32[1,2,16,1024]{3,2,1,0:T(8,128)S(1)}, u32[]{:S(2)}, u32[]{:S(2)}) %collective-permute-start.5) | collective-permute-done | bytes 131104 | tf_op jit(solution)/shard_map/ppermute | solution.py:281
  19.7 0.9 %first.2.src_levels = f32[8,2,30,8,128]{4,3,2,1,0:T(8,128)S(1)} custom-call(f32[2,128,128]{2,1,0:T(8,128)S(1)} %bitcast.115, f32[2,128,128]{2,1,0:T(8,128)S(1)} %bitcast.118), custom_call_target="tpu_custom_call" | custom-call | flops 67108864 | bytes 4194304 | tf_op jit(solution)/shard_map/first/pallas_call | solution.py:356
  20.6 1.3 %collective-permute-done.6 = f32[1,2,16,1024]{3,2,1,0:T(8,128)S(1)} collective-permute-done((f32[1,2,16,1024]{3,2,1,0:T(8,128)}, f32[1,2,16,1024]{3,2,1,0:T(8,128)S(1)}, u32[]{:S(2)}, u32[]{:S(2)}) %collective-permute-start.6) | collective-permute-done | bytes 131104 | tf_op jit(solution)/shard_map/ppermute | solution.py:281
  21.9 0.9 %first.3.rec_levels = f32[8,2,30,8,128]{4,3,2,1,0:T(8,128)S(1)} custom-call(f32[2,128,128]{2,1,0:T(8,128)S(1)} %bitcast.116, f32[2,128,128]{2,1,0:T(8,128)S(1)} %bitcast.117), custom_call_target="tpu_custom_call" | custom-call | flops 67108864 | bytes 4194304 | tf_op jit(solution)/shard_map/first/pallas_call | solution.py:356
  22.7 0.0 collective-permute-done.4.refs_1_
  22.8 1.5 %coefficients.3 = f32[8,2,8,40,128]{4,3,2,1,0:T(8,128)S(1)} custom-call(f32[1]{0:T(128)S(6)} %copy.24.refs_0_, f32[4,40,128]{2,1,0:T(8,128)S(1)} %collective-permute-done.4.refs_1_, f32[8,2,8,40,128]{4,3,2,1,0:T(8,128)S(1)} %coefficients.2.refs_2_), custom_call_target="tpu_custom_call", output_to_operand_aliasing={{}: (2, {})} | custom-call | flops 67108864 | bytes 4194304 | tf_op jit(solution)/shard_map/coefficients/pallas_call | solution.py:372
  24.2 3.2 %main.1 = (f32[128,128]{1,0:T(8,128)S(1)}, f32[128,128]{1,0:T(8,128)S(1)}, f32[2,128,128]{2,1,0:T(8,128)}, f32[2,128,128]{2,1,0:T(8,128)}) custom-call(f32[8,2,320,128]{3,2,1,0:T(8,128)S(1)} %bitcast.112, f32[8,2,30,8,128]{4,3,2,1,0:T(8,128)S(1)} %first.2.src_levels, f32[8,2,30,8,128]{4,3,2,1,0:T(8,128)S(1)} %first.3.rec_levels), custom_call_target="tpu_custom_call" | custom-call | tf_op jit(solution)/shard_map/main/pallas_call | solution.py:390
  27.4 1.3 %collective-permute-done.7 = f32[128,128]{1,0:T(8,128)S(1)} collective-permute-done((f32[128,128]{1,0:T(8,128)S(1)}, f32[128,128]{1,0:T(8,128)S(1)}, u32[]{:S(2)}, u32[]{:S(2)}) %collective-permute-start.7) | collective-permute-done | bytes 65568 | tf_op jit(solution)/shard_map/ppermute | solution.py:288
  28.7 1.3 %collective-permute-start.8 = (f32[4,16,128]{2,1,0:T(8,128)S(1)}, f32[4,16,128]{2,1,0:T(8,128)S(1)}, u32[]{:S(2)}, u32[]{:S(2)}) collective-permute-start(f32[4,16,128]{2,1,0:T(8,128)S(1)} %select_bitcast_fusion.2), channel_id=1, source_target_pairs={{0,6},{2,4},{4,2},{6,0},{8,14},{10,12},{12,10},{14,8},{16,22},{18,... | collective-permute-start | bytes 98312 | tf_op jit(solution)/shard_map/ppermute | solution.py:288
  30.0 2.1 %collective-permute-done.8 = f32[4,16,128]{2,1,0:T(8,128)S(1)} collective-permute-done((f32[4,16,128]{2,1,0:T(8,128)S(1)}, f32[4,16,128]{2,1,0:T(8,128)S(1)}, u32[]{:S(2)}, u32[]{:S(2)}) %collective-permute-start.8) | collective-permute-done | bytes 32800 | tf_op jit(solution)/shard_map/ppermute | solution.py:288
  32.2 0.1 collective-permute-start.9
  32.2 3.2 %collective-permute-done.9 = f32[2,16,128]{2,1,0:T(8,128)S(1)} collective-permute-done((f32[2,16,128]{2,1,0:T(8,128)S(1)}, f32[2,16,128]{2,1,0:T(8,128)S(1)}, u32[]{:S(2)}, u32[]{:S(2)}) %collective-permute-start.9) | collective-permute-done | bytes 16416 | tf_op jit(solution)/shard_map/ppermute | solution.py:288
  35.4 2.8 %collective-permute-start.10 = (f32[1,16,128]{2,1,0:T(8,128)S(1)}, f32[1,16,128]{2,1,0:T(8,128)S(1)}, u32[]{:S(2)}, u32[]{:S(2)}) collective-permute-start(f32[1,16,128]{2,1,0:T(8,128)S(1)} %select_bitcast_fusion.6), channel_id=1, source_target_pairs={{0,18},{2,16},{4,22},{6,20},{8,26},{10,24},{12,30},{14,28},{16,2},... | collective-permute-start | bytes 24584 | tf_op jit(solution)/shard_map/ppermute | solution.py:288
  38.2 1.4 %collective-permute-done.10 = f32[1,16,128]{2,1,0:T(8,128)S(1)} collective-permute-done((f32[1,16,128]{2,1,0:T(8,128)S(1)}, f32[1,16,128]{2,1,0:T(8,128)S(1)}, u32[]{:S(2)}, u32[]{:S(2)}) %collective-permute-start.10) | collective-permute-done | bytes 8224 | tf_op jit(solution)/shard_map/ppermute | solution.py:288
  39.6 0.1 slice_bitcast_fusion.3
  39.7 0.6 %pad_maximum_fusion.2 = f32[2,16,64]{2,1,0:T(8,128)} fusion(f32[1,16,64]{2,1,0:T(8,128)S(1)} %get-tuple-element.20, f32[1,16,64]{2,1,0:T(8,128)S(1)} %get-tuple-element.19), kind=kLoop, calls=%fused_computation.12 | loop fusion | flops 2048 | bytes 16384 | tf_op jit(solution)/shard_map/stack | solution.py:402
  (18 shorter events, 0.1 us)
Async XLA Ops:
  0.6 19.0 %copy-start = (f32[1,2,16,1024]{3,2,1,0:T(8,128)S(1)}, f32[1,2,16,1024]{3,2,1,0:T(8,128)}, u32[]{:S(2)}) copy-start(f32[1,2,16,1024]{3,2,1,0:T(8,128)} %param.6) | copy-start | bytes 393220
  0.6 5.0 %collective-permute-start = (f32[2,16,64]{2,1,0:T(8,128)}, f32[2,16,64]{2,1,0:T(8,128)S(1)}, u32[]{:S(2)}, u32[]{:S(2)}) collective-permute-start(f32[2,16,64]{2,1,0:T(8,128)} %param.5), channel_id=1, source_target_pairs={{0,1},{1,0},{2,3},{3,2},{4,5},{5,4},{6,7},{7,6},{8,9},{9,8},{10,11... | collective-permute-start | bytes 24584 | tf_op jit(solution)/shard_map/ppermute | solution.py:281
  5.6 1.3 %collective-permute-start.1 = (f32[40,64]{1,0:T(8,128)S(1)}, f32[40,64]{1,0:T(8,128)S(1)}, u32[]{:S(2)}, u32[]{:S(2)}) collective-permute-start(f32[40,64]{1,0:T(8,128)S(1)} %pad_maximum_fusion.1), channel_id=1, source_target_pairs={{0,2},{2,0},{4,6},{6,4},{8,10},{10,8},{12,14},{14,12},{16,18},{18,... | collective-permute-start | bytes 30728 | tf_op jit(solution)/shard_map/ppermute | solution.py:288
  7.0 4.3 %collective-permute-start.2 = (f32[1,40,128]{2,1,0:T(8,128)S(1)}, f32[1,40,128]{2,1,0:T(8,128)S(1)}, u32[]{:S(2)}, u32[]{:S(2)}) collective-permute-start(f32[1,40,128]{2,1,0:T(8,128)S(1)} %maximum_bitcast_fusion.1), channel_id=1, source_target_pairs={{0,18},{2,16},{4,22},{6,20},{8,26},{10,24},{12,30},{14,28},{16,2},... | collective-permute-start | bytes 61448 | tf_op jit(solution)/shard_map/ppermute | solution.py:288
  11.4 3.7 %collective-permute-start.3 = (f32[2,40,128]{2,1,0:T(8,128)S(1)}, f32[2,40,128]{2,1,0:T(8,128)S(1)}, u32[]{:S(2)}, u32[]{:S(2)}) collective-permute-start(f32[2,40,128]{2,1,0:T(8,128)S(1)} %maximum_bitcast_fusion), channel_id=1, source_target_pairs={{0,10},{2,8},{4,14},{6,12},{8,2},{10,0},{12,6},{14,4},{16,26},{18,... | collective-permute-start | bytes 122888 | tf_op jit(solution)/shard_map/ppermute | solution.py:288
  13.1 6.6 %collective-permute-start.5 = (f32[1,2,16,1024]{3,2,1,0:T(8,128)}, f32[1,2,16,1024]{3,2,1,0:T(8,128)S(1)}, u32[]{:S(2)}, u32[]{:S(2)}) collective-permute-start(f32[1,2,16,1024]{3,2,1,0:T(8,128)} %param.6), channel_id=1, source_target_pairs={{0,1},{1,0},{2,3},{3,2},{4,5},{5,4},{6,7},{7,6},{8,9},{9,8},{10,11... | collective-permute-start | bytes 393224 | tf_op jit(solution)/shard_map/ppermute | solution.py:281
  14.6 7.2 %collective-permute-start.6 = (f32[1,2,16,1024]{3,2,1,0:T(8,128)}, f32[1,2,16,1024]{3,2,1,0:T(8,128)S(1)}, u32[]{:S(2)}, u32[]{:S(2)}) collective-permute-start(f32[1,2,16,1024]{3,2,1,0:T(8,128)} %param.7), channel_id=1, source_target_pairs={{0,1},{1,0},{2,3},{3,2},{4,5},{5,4},{6,7},{7,6},{8,9},{9,8},{10,11... | collective-permute-start | bytes 393224 | tf_op jit(solution)/shard_map/ppermute | solution.py:281
  15.1 6.7 %copy-start.1 = (f32[1,2,16,1024]{3,2,1,0:T(8,128)S(1)}, f32[1,2,16,1024]{3,2,1,0:T(8,128)}, u32[]{:S(2)}) copy-start(f32[1,2,16,1024]{3,2,1,0:T(8,128)} %param.7) | copy-start | bytes 393220
  15.2 7.6 %collective-permute-start.4 = (f32[4,40,128]{2,1,0:T(8,128)S(1)}, f32[4,40,128]{2,1,0:T(8,128)S(1)}, u32[]{:S(2)}, u32[]{:S(2)}) collective-permute-start(f32[4,40,128]{2,1,0:T(8,128)S(1)} %bitcast.113), channel_id=1, source_target_pairs={{0,6},{2,4},{4,2},{6,0},{8,14},{10,12},{12,10},{14,8},{16,22},{18,... | collective-permute-start | bytes 245768 | tf_op jit(solution)/shard_map/ppermute | solution.py:288
  27.4 1.3 %collective-permute-start.7 = (f32[128,128]{1,0:T(8,128)S(1)}, f32[128,128]{1,0:T(8,128)S(1)}, u32[]{:S(2)}, u32[]{:S(2)}) collective-permute-start(f32[128,128]{1,0:T(8,128)S(1)} %get-tuple-element.8), channel_id=1, source_target_pairs={{0,2},{2,0},{4,6},{6,4},{8,10},{10,8},{12,14},{14,12},{16,18},{18,... | collective-permute-start | bytes 196616 | tf_op jit(solution)/shard_map/ppermute | solution.py:288
  28.7 3.4 %collective-permute-start.8 = (f32[4,16,128]{2,1,0:T(8,128)S(1)}, f32[4,16,128]{2,1,0:T(8,128)S(1)}, u32[]{:S(2)}, u32[]{:S(2)}) collective-permute-start(f32[4,16,128]{2,1,0:T(8,128)S(1)} %select_bitcast_fusion.2), channel_id=1, source_target_pairs={{0,6},{2,4},{4,2},{6,0},{8,14},{10,12},{12,10},{14,8},{16,22},{18,... | collective-permute-start | bytes 98312 | tf_op jit(solution)/shard_map/ppermute | solution.py:288
  32.2 3.2 %collective-permute-start.9 = (f32[2,16,128]{2,1,0:T(8,128)S(1)}, f32[2,16,128]{2,1,0:T(8,128)S(1)}, u32[]{:S(2)}, u32[]{:S(2)}) collective-permute-start(f32[2,16,128]{2,1,0:T(8,128)S(1)} %select_bitcast_fusion.5), channel_id=1, source_target_pairs={{0,10},{2,8},{4,14},{6,12},{8,2},{10,0},{12,6},{14,4},{16,26},{18,... | collective-permute-start | bytes 49160 | tf_op jit(solution)/shard_map/ppermute | solution.py:288
  35.4 4.2 %collective-permute-start.10 = (f32[1,16,128]{2,1,0:T(8,128)S(1)}, f32[1,16,128]{2,1,0:T(8,128)S(1)}, u32[]{:S(2)}, u32[]{:S(2)}) collective-permute-start(f32[1,16,128]{2,1,0:T(8,128)S(1)} %select_bitcast_fusion.6), channel_id=1, source_target_pairs={{0,18},{2,16},{4,22},{6,20},{8,26},{10,24},{12,30},{14,28},{16,2},... | collective-permute-start | bytes 24584 | tf_op jit(solution)/shard_map/ppermute | solution.py:288

commit v2 on v1

--- a/solution.py
+++ b/solution.py
@@ -150,21 +150,23 @@
     chebyshev(levels, (0, 1), low, high, lowest, rows, two)
 
 
-def coefficient_kernel(bit, other, *refs):
+def coefficient_kernel(shared, *refs):
     freq_ref, slow_ref, out_ref = refs[0], refs[1], refs[-1]
     count, rows, _ = slow_ref.shape
-    slot = (lax.axis_index("freq") >> bit) & 1
-    if other:
-        slot = 1 - slot
+    slot = 0
+    for bit, other in shared:
+        own = (lax.axis_index("freq") >> bit) & 1
+        slot = 2 * slot + (1 - own if other else own)
     groups = rows // SUBLANES
+    freq = jnp.broadcast_to(freq_ref[...], (SUBLANES, LANES))
 
     def body(index, carry):
         piece = index // groups
         start = pl.multiple_of((index % groups) * SUBLANES, SUBLANES)
-        phases = node_phases(freq_ref[0] * slow_ref[piece, pl.ds(start, SUBLANES), :])
+        phases = node_phases(freq * slow_ref[piece, pl.ds(start, SUBLANES), :])
         for part in range(2):
             for order, value in enumerate(cosine_sums([p[part] for p in phases])):
-                out_ref[order, part, 2 * piece + slot, pl.ds(start, SUBLANES), :] = value
+                out_ref[order, part, (piece << len(shared)) + slot, pl.ds(start, SUBLANES), :] = value
         return carry
 
     lax.fori_loop(0, count * groups, body, 0)
@@ -288,44 +290,107 @@
     return lax.ppermute(block, "freq", [(i, i ^ mask) for i in range(lax.axis_size("freq"))])
 
 
+VMEM = pl.BlockSpec(memory_space=pltpu.VMEM)
+COST = pl.CostEstimate(flops=1 << 26, bytes_accessed=1 << 22, transcendentals=0)
+
+
+def call(kernel, shapes, *operands, mib=2, **options):
+    single = not isinstance(shapes, list)
+    outs = [jax.ShapeDtypeStruct(shape, jnp.float32) for shape in ([shapes] if single else shapes)]
+    options.setdefault("in_specs", [VMEM] * len(operands))
+    return pl.pallas_call(
+        kernel,
+        out_shape=outs[0] if single else outs,
+        out_specs=VMEM if single else [VMEM] * len(outs),
+        compiler_params=pltpu.CompilerParams(vmem_limit_bytes=mib << 20),
+        **options,
+    )(*operands)
+
+
+def bundle_kernel(halo, two, *refs):
+    layers, sides, out = refs[: -2 if two else -3], refs[-2 if two else -3 : -1], refs[-1]
+    rows = layers[0].shape[0]
+    out[:rows, :] = layers[0][...]
+    if two:
+        start = pl.multiple_of(lax.axis_index("lat") * (rows - halo), SUBLANES)
+        out[rows : rows + halo, :] = sides[0][0, pl.ds(start, halo), :]
+    else:
+        out[rows : rows + halo, :] = sides[0][0, rows - halo :, :]
+        out[rows + halo : rows + 2 * halo, :] = sides[1][0, :halo, :]
+    after = rows + halo * len(sides)
+    for step, layer in enumerate(layers[1:]):
+        out[after + step * rows : after + (step + 1) * rows, :] = layer[...]
+
+
+def beside_kernel(bit, mine, other, out):
+    upper = ((lax.axis_index("freq") >> bit) & 1) != 0
+    first, second = mine[...], other[...]
+    out[...] = jnp.concatenate([jnp.where(upper, second, first), jnp.where(upper, first, second)], axis=1)
+
+
+def stack_kernel(bit, mine, other, out):
+    slot = (lax.axis_index("freq") >> bit) & 1
+    for piece in range(mine.shape[0]):
+        out[2 * piece + slot] = mine[piece]
+        out[2 * piece + 1 - slot] = other[piece]
+
+
 def gather_columns(block):
     count = lax.axis_size("freq")
-    me = lax.axis_index("freq")
-    width = block.shape[1]
+    rows, width = block.shape
     bits = range(count.bit_length() - 1)
     inner = [b for b in bits if width << b < LANES]
     outer = [b for b in bits if width << b >= LANES][::-1]
     for b in inner:
         other = partner(block, 1 << b)
-        upper = (me >> b) & 1 != 0
-        block = jnp.concatenate([jnp.where(upper, other, block), jnp.where(upper, block, other)], axis=1)
+        shape = (rows, 2 * block.shape[1])
+        block = call(functools.partial(beside_kernel, b), shape, block, other, cost_estimate=COST)
     block = block[None]
-    for depth, b in enumerate(outer):
+    parts = []
+    for at, b in enumerate(outer):
         other = partner(block, (1 << b) | (1 if inner else 0))
+        if at == len(outer) - 2:
+            parts.append((block, ((b, False), (outer[-1], False))))
+            parts.append((other, ((b, True), (outer[-1], False))))
         if b == outer[-1]:
-            return block, other, b
-        upper = (me >> b) & 1 != 0
-        low, high = jnp.where(upper, other, block), jnp.where(upper, block, other)
-        block = jnp.stack([low, high], axis=1).reshape(2 * block.shape[0], *block.shape[1:])
-
-
-def scatter_sum(keep, send, rows):
+            parts.append((other, ((b, True),)))
+            return parts
+        shape = (2 * block.shape[0], *block.shape[1:])
+        block = call(functools.partial(stack_kernel, b), shape, block, other, cost_estimate=COST)
+
+
+def halve_kernel(bit, held, came, keep, send):
+    slot = (lax.axis_index("freq") >> bit) & 1
+    for piece in range(keep.shape[0]):
+        here, there = 2 * piece + slot, 2 * piece + 1 - slot
+        send[piece] = held[there] + came[there]
+        keep[piece] = held[here] + came[here]
+
+
+def last_kernel(scale, held, came, out):
+    total = (held[0] + came[0]) * scale
+    width = out.shape[2]
+    for step in range(out.shape[0]):
+        out[step] = total[:, step * width : (step + 1) * width]
+
+
+def scatter_sum(keep, send, rows, scale, out_shape):
     count = lax.axis_size("freq")
-    me = lax.axis_index("freq")
-    held = (keep + partner(send, 1)).reshape(count // 2, rows, LANES)
+    pieces = count // 2
+    held = keep.reshape(pieces, rows, LANES)
+    came = partner(send, 1).reshape(pieces, rows, LANES)
     for b in range(1, count.bit_length() - 1):
-        upper = (me >> b) & 1 != 0
-        split = held.reshape(held.shape[0] // 2, 2, rows, LANES)
-        low, high = split[:, 0], split[:, 1]
-        held = jnp.where(upper, high, low) + partner(jnp.where(upper, low, high), (1 << b) | 1)
-    return held[0]
+        pieces //= 2
+        shapes = [(pieces, rows, LANES)] * 2
+        held, send = call(functools.partial(halve_kernel, b), shapes, held, came)
+        came = partner(send, (1 << b) | 1)
+    return call(functools.partial(last_kernel, scale), out_shape, held, came)
 
 
 def shards(frequencies, slowness, src_field, rec_field):
     depth_steps, rows, width = slowness.shape
     tiles = src_field.shape[3] // LANES
     freq_count = lax.axis_size("freq")
-    flip = lax.axis_index("lat")
     two = lax.axis_size("lat") == 2
     packed = depth_steps == 2 and width * depth_steps == LANES
     norm_factor = 1.0 / math.sqrt(frequencies.shape[0] * freq_count)
@@ -335,71 +400,55 @@
     later_span = window(rows, 1, two)[1] - window(rows, 1, two)[0]
 
     slow_sides = from_sides(slowness)
-    src_sides, rec_sides = from_sides(src_field), from_sides(rec_field)
-    slow_parts = [slowness[0]]
-    if two:
-        slow_parts.append(jnp.where(flip == 0, slow_sides[0][0, :halo], slow_sides[0][0, rows - halo :]))
-    else:
-        slow_parts += [slow_sides[0][0, rows - halo :], slow_sides[1][0, :halo]]
-    slow_parts += [slowness[z] for z in range(1, depth_steps)]
-    mine, theirs, bit = gather_columns(jnp.concatenate(slow_parts, axis=0))
-    coef_rows = mine.shape[1]
-
-    smem, vmem = pl.BlockSpec(memory_space=pltpu.SMEM), pl.BlockSpec(memory_space=pltpu.VMEM)
-    shape_of = functools.partial(jax.ShapeDtypeStruct, dtype=jnp.float32)
-
-    def limit(mib):
-        return pltpu.CompilerParams(vmem_limit_bytes=mib << 20)
+    src_sides = from_sides(src_field)
+    rec_sides = from_sides(rec_field)
+    coef_rows = (rows + halo * len(slow_sides)) + (depth_steps - 1) * rows
+    layers = [slowness[z] for z in range(depth_steps)]
+    kernel = functools.partial(bundle_kernel, halo, two)
+    bundle = call(kernel, (coef_rows, width), *layers, *slow_sides)
+    parts = gather_columns(bundle)
 
     def first_levels(own, sides, conjugate):
         fields = [tiled(x[0]) for x in (own, *sides)]
-        return pl.pallas_call(
-            functools.partial(first_kernel, rows, depth_steps, two, conjugate),
-            out_shape=shape_of((TERMS, 2, span, tiles, LANES)),
-            in_specs=[vmem] * len(fields),
-            out_specs=vmem,
-            compiler_params=limit(4),
-            cost_estimate=pl.CostEstimate(flops=1 << 26, bytes_accessed=1 << 22, transcendentals=0),
-            name="first",
-        )(*fields)
+        kernel = functools.partial(first_kernel, rows, depth_steps, two, conjugate)
+        return call(kernel, (TERMS, 2, span, tiles, LANES), *fields, mib=4, cost_estimate=COST)
 
     src_levels = first_levels(src_field, src_sides, False)
     rec_levels = first_levels(rec_field, rec_sides, True)
 
-    coef_shape = shape_of((TERMS, 2, tiles, coef_rows, LANES))
-
-    def coefficients(other, *operands):
-        return pl.pallas_call(
-            functools.partial(coefficient_kernel, bit, other),
-            out_shape=coef_shape,
-            in_specs=[smem] + [vmem] * (len(operands) - 1),
-            out_specs=vmem,
-            input_output_aliases={2: 0} if other else {},
-            compiler_params=limit(8),
-            cost_estimate=pl.CostEstimate(flops=1 << 26, bytes_accessed=1 << 22, transcendentals=0),
-            name="coefficients",
-        )(*operands)
-
-    coefs = coefficients(False, frequencies, mine)
-    coefs = coefficients(True, frequencies, theirs, coefs)
-
-    image_shape = shape_of((tiles * rows, LANES) if packed else (depth_steps, rows * tiles, LANES))
-    field_shape = shape_of((2, rows * tiles, LANES))
+    coef_shape = (TERMS, 2, tiles, coef_rows, LANES)
+    freq = frequencies.reshape(1, 1)
+    coefs = []
+    for part, shared in parts:
+        coefs = [
+            call(
+                functools.partial(coefficient_kernel, shared),
+                coef_shape,
+                freq,
+                part,
+                *coefs,
+                mib=8,
+                input_output_aliases={2: 0} if coefs else {},
+                cost_estimate=COST,
+            )
+        ]
+
+    image_shape = (tiles * rows, LANES) if packed else (depth_steps, rows * tiles, LANES)
+    field_shape = (2, rows * tiles, LANES)
     image_shapes = [image_shape] * (2 if packed else 1)
     setup = (rows, halo, depth_steps, two, packed, width)
-    *image, src, rec = pl.pallas_call(
+    *image, src, rec = call(
         functools.partial(main_kernel, setup),
-        out_shape=(*image_shapes, field_shape, field_shape),
-        in_specs=[vmem] * 3,
-        out_specs=(vmem,) * (len(image_shapes) + 2),
+        [*image_shapes, field_shape, field_shape],
+        coefs[0].reshape(TERMS, 2, tiles * coef_rows, LANES),
+        src_levels,
+        rec_levels,
+        mib=16,
         scratch_shapes=[pltpu.VMEM((TERMS, 4, later_span, tiles, LANES), jnp.float32)],
-        compiler_params=limit(16),
-        name="main",
-    )(coefs.reshape(TERMS, 2, tiles * coef_rows, LANES), src_levels, rec_levels)
+    )
 
     if packed:
-        total = scatter_sum(*image, rows) * norm_factor
-        depth_image = jnp.stack([total[:, z * width : (z + 1) * width] for z in range(depth_steps)])
+        depth_image = scatter_sum(*image, rows, norm_factor, (depth_steps, rows, width))
     else:
         whole = untiled(image[0], rows).reshape(depth_steps, rows, freq_count, width)
         pieces = whole.transpose(2, 0, 1, 3)

time: 40.5 us -> 38.7 us (0.956)
  waiting for transfers between devices: 13.9 us -> 12.4 us
  Pallas kernels: 7.9 us -> 8.87 us
  other arithmetic: 0.86 us -> 0 us
    ppermute x3, waiting for transfers between devices: 3.39 us -> 1.2 us  [from_sides(): return [lax.ppermute(block, 'lat', [(0, 1), (1, 0)])]]
    pallas_call x5 -> x14, Pallas kernels: 7.9 us -> 8.87 us  [call(): pl.pallas_call(kernel, out_shape=outs[0] if single else outs, out_specs=V...]
    another operation x4 -> x0, other arithmetic: 0.71 us -> none  [the longest x1 0.61 us: shards(): jnp.stack([total[:, z * width:(z + 1) * width] for z in range(depth_steps)])]
    ppermute x8, waiting for transfers between devices: 10.5 us -> 11.2 us  [partner(): lax.ppermute(block, 'freq', [(i, i ^ mask) for i in range(lax.axis_size('...]
    ppermute x8, starting transfers between devices: 10.3 us -> 9.87 us  [partner(): lax.ppermute(block, 'freq', [(i, i ^ mask) for i in range(lax.axis_size('...]
  transfers between devices with their start and end apart: 11 -> 11, of which waited for: 9 -> 7; matrix products, arithmetic and copies ran while one was open for 2% -> 2% of each run, Pallas kernels for 8% -> 9%
where the time goes in v2:
time: 38.7 us; the launch traced here: 38.4 us
  starting transfers between devices  15 us (39%)
  waiting for transfers between devices  12.4 us (32%)
  Pallas kernels  8.87 us (23%)
  between operations  1.39 us (4%)
  local copies, waits for them, and re-layouts  0.81 us (2%)
    ppermute x8, waiting for transfers between devices, partner(): lax.ppermute(block, 'freq', [(i, i ^ mask) for i in range(lax.axis_size('...  11.2 us
    ppermute x8, starting transfers between devices, partner(): lax.ppermute(block, 'freq', [(i, i ^ mask) for i in range(lax.axis_size('...  9.87 us
    pallas_call x14, Pallas kernels, call(): pl.pallas_call(kernel, out_shape=outs[0] if single else outs, out_specs=V...  8.87 us
    ppermute x3, starting transfers between devices, from_sides(): return [lax.ppermute(block, 'lat', [(0, 1), (1, 0)])]  5.09 us
    ppermute x3, waiting for transfers between devices, from_sides(): return [lax.ppermute(block, 'lat', [(0, 1), (1, 0)])]  1.2 us
  transfers between devices with their start and end apart: 11, of which 7 were waited for; matrix products, arithmetic and copies ran while one was open for 2% of the time, Pallas kernels for 9%

profile of v2, /device:TPU:0, one launch (start us, length us, event | category | flops | bytes accessed | tf_op | source)
XLA Modules:
  0.0 38.4 jit_solution(965623031666955588)
XLA Ops:
  0.6 3.1 %collective-permute-start = (f32[2,16,64]{2,1,0:T(8,128)}, f32[2,16,64]{2,1,0:T(8,128)S(1)}, u32[]{:S(2)}, u32[]{:S(2)}) collective-permute-start(f32[2,16,64]{2,1,0:T(8,128)} %param.5), channel_id=1, source_target_pairs={{0,1},{1,0},{2,3},{3,2},{4,5},{5,4},{6,7},{7,6},{8,9},{9,8},{10,11... | collective-permute-start | bytes 24584 | tf_op jit(solution)/shard_map/ppermute | solution.py:283
  3.7 0.7 %slice_bitcast_fusion = (f32[16,64]{1,0:T(8,128)S(1)}, f32[16,64]{1,0:T(8,128)S(1)}) fusion(f32[2,16,64]{2,1,0:T(8,128)} %param.5), kind=kLoop, calls=%fused_computation | loop fusion | bytes 16384 | tf_op jit(solution)/shard_map/squeeze | solution.py:406
  4.4 1.2 %collective-permute-done.refs_2_ = f32[2,16,64]{2,1,0:T(8,128)S(1)} collective-permute-done((f32[2,16,64]{2,1,0:T(8,128)}, f32[2,16,64]{2,1,0:T(8,128)S(1)}, u32[]{:S(2)}, u32[]{:S(2)}) %collective-permute-start) | collective-permute-done | bytes 8224 | tf_op jit(solution)/shard_map/ppermute | solution.py:283
  5.6 0.0 collective-permute-start.1
  5.6 1.2 %collective-permute-done.1.other = f32[40,64]{1,0:T(8,128)S(1)} collective-permute-done((f32[40,64]{1,0:T(8,128)S(1)}, f32[40,64]{1,0:T(8,128)S(1)}, u32[]{:S(2)}, u32[]{:S(2)}) %collective-permute-start.1) | collective-permute-done | bytes 10272 | tf_op jit(solution)/shard_map/ppermute | solution.py:290
  6.8 0.1 shard_map.68
  6.9 2.9 %collective-permute-start.2 = (f32[1,40,128]{2,1,0:T(8,128)S(1)}, f32[1,40,128]{2,1,0:T(8,128)S(1)}, u32[]{:S(2)}, u32[]{:S(2)}) collective-permute-start(f32[1,40,128]{2,1,0:T(8,128)S(1)} %bitcast.49), channel_id=1, source_target_pairs={{0,18},{2,16},{4,22},{6,20},{8,26},{10,24},{12,30},{14,28},{16,2},... | collective-permute-start | bytes 61448 | tf_op jit(solution)/shard_map/ppermute | solution.py:290
  9.8 1.5 %collective-permute-start.5 = (f32[1,2,16,1024]{3,2,1,0:T(8,128)}, f32[1,2,16,1024]{3,2,1,0:T(8,128)S(1)}, u32[]{:S(2)}, u32[]{:S(2)}) collective-permute-start(f32[1,2,16,1024]{3,2,1,0:T(8,128)} %param.6), channel_id=1, source_target_pairs={{0,1},{1,0},{2,3},{3,2},{4,5},{5,4},{6,7},{7,6},{8,9},{9,8},{10,11... | collective-permute-start | bytes 393224 | tf_op jit(solution)/shard_map/ppermute | solution.py:283
  11.3 0.5 %collective-permute-start.6 = (f32[1,2,16,1024]{3,2,1,0:T(8,128)}, f32[1,2,16,1024]{3,2,1,0:T(8,128)S(1)}, u32[]{:S(2)}, u32[]{:S(2)}) collective-permute-start(f32[1,2,16,1024]{3,2,1,0:T(8,128)} %param.7), channel_id=1, source_target_pairs={{0,1},{1,0},{2,3},{3,2},{4,5},{5,4},{6,7},{7,6},{8,9},{9,8},{10,11... | collective-permute-start | bytes 393224 | tf_op jit(solution)/shard_map/ppermute | solution.py:283
  11.8 1.1 %collective-permute-start.3 = (f32[2,40,128]{2,1,0:T(8,128)S(1)}, f32[2,40,128]{2,1,0:T(8,128)S(1)}, u32[]{:S(2)}, u32[]{:S(2)}) collective-permute-start(f32[2,40,128]{2,1,0:T(8,128)S(1)} %shard_map.69.mine.refs_1_), channel_id=1, source_target_pairs={{0,10},{2,8},{4,14},{6,12},{8,2},{10,0},{12,6},{14,4},{16,26},{18,... | collective-permute-start | bytes 122888 | tf_op jit(solution)/shard_map/ppermute | solution.py:290
  12.9 2.7 %collective-permute-done.3.other.refs_1_ = f32[2,40,128]{2,1,0:T(8,128)S(1)} collective-permute-done((f32[2,40,128]{2,1,0:T(8,128)S(1)}, f32[2,40,128]{2,1,0:T(8,128)S(1)}, u32[]{:S(2)}, u32[]{:S(2)}) %collective-permute-start.3) | collective-permute-done | bytes 40992 | tf_op jit(solution)/shard_map/ppermute | solution.py:290
  15.6 1.4 %collective-permute-start.4 = (f32[4,40,128]{2,1,0:T(8,128)S(1)}, f32[4,40,128]{2,1,0:T(8,128)S(1)}, u32[]{:S(2)}, u32[]{:S(2)}) collective-permute-start(f32[4,40,128]{2,1,0:T(8,128)S(1)} %shard_map.70), channel_id=1, source_target_pairs={{0,6},{2,4},{4,2},{6,0},{8,14},{10,12},{12,10},{14,8},{16,22},{18,... | collective-permute-start | bytes 245768 | tf_op jit(solution)/shard_map/ppermute | solution.py:290
  17.7 0.8 %shard_map.71.refs_2_ = f32[8,2,8,40,128]{4,3,2,1,0:T(8,128)S(1)} custom-call(f32[1,1]{1,0:T(1,128)} %bitcast.39.refs_0_, f32[2,40,128]{2,1,0:T(8,128)S(1)} %shard_map.69.mine.refs_1_), custom_call_target="tpu_custom_call" | custom-call | flops 67108864 | bytes 4194304 | tf_op jit(solution)/shard_map/pallas_call | solution.py:301
  18.5 0.0 copy-start
  18.5 0.0 copy-start.1
  18.5 0.8 %shard_map.72.refs_2_ = f32[8,2,8,40,128]{4,3,2,1,0:T(8,128)S(1)} custom-call(f32[1,1]{1,0:T(1,128)} %bitcast.40.refs_0_, f32[2,40,128]{2,1,0:T(8,128)S(1)} %collective-permute-done.3.other.refs_1_, f32[8,2,8,40,128]{4,3,2,1,0:T(8,128)S(1)} %shard_map.71.refs_2_), custom_call_target="tpu_custom_call", output_to_operand_aliasing={{}: (2, {})} | custom-call | flops 67108864 | bytes 4194304 | tf_op jit(solution)/shard_map/pallas_call | solution.py:301
  19.3 0.0 collective-permute-done.5
  19.3 0.1 copy-done
  19.4 0.9 %shard_map.74.src_levels = f32[8,2,30,8,128]{4,3,2,1,0:T(8,128)S(1)} custom-call(f32[2,128,128]{2,1,0:T(8,128)S(1)} %bitcast.43, f32[2,128,128]{2,1,0:T(8,128)S(1)} %bitcast.46), custom_call_target="tpu_custom_call" | custom-call | flops 67108864 | bytes 4194304 | tf_op jit(solution)/shard_map/pallas_call | solution.py:301
  20.3 0.9 %shard_map.75.rec_levels = f32[8,2,30,8,128]{4,3,2,1,0:T(8,128)S(1)} custom-call(f32[2,128,128]{2,1,0:T(8,128)S(1)} %bitcast.44, f32[2,128,128]{2,1,0:T(8,128)S(1)} %bitcast.45), custom_call_target="tpu_custom_call" | custom-call | flops 67108864 | bytes 4194304 | tf_op jit(solution)/shard_map/pallas_call | solution.py:301
  21.2 0.0 collective-permute-done.4.refs_1_
  21.2 1.5 %shard_map.73 = f32[8,2,8,40,128]{4,3,2,1,0:T(8,128)S(1)} custom-call(f32[1,1]{1,0:T(1,128)} %bitcast.41.refs_0_, f32[4,40,128]{2,1,0:T(8,128)S(1)} %collective-permute-done.4.refs_1_, f32[8,2,8,40,128]{4,3,2,1,0:T(8,128)S(1)} %shard_map.72.refs_2_), custom_call_target="tpu_custom_call", output_to_operand_aliasing={{}: (2, {})} | custom-call | flops 67108864 | bytes 4194304 | tf_op jit(solution)/shard_map/pallas_call | solution.py:301
  22.7 3.2 %shard_map.76 = (f32[128,128]{1,0:T(8,128)S(1)}, f32[128,128]{1,0:T(8,128)S(1)}, f32[2,128,128]{2,1,0:T(8,128)}, f32[2,128,128]{2,1,0:T(8,128)}) custom-call(f32[8,2,320,128]{3,2,1,0:T(8,128)S(1)} %bitcast.42, f32[8,2,30,8,128]{4,3,2,1,0:T(8,128)S(1)} %shard_map.74.src_levels, f32[8,2,30,8,128]{4,3,2,1,0:T(8,128)S(1)} %shard_map.75.rec_levels), custom_call_target="tpu_custom_call" | custom-call | tf_op jit(solution)/shard_map/pallas_call | solution.py:301
  25.9 0.3 collective-permute-start.7
  26.2 1.0 %collective-permute-done.7 = f32[128,128]{1,0:T(8,128)S(1)} collective-permute-done((f32[128,128]{1,0:T(8,128)S(1)}, f32[128,128]{1,0:T(8,128)S(1)}, u32[]{:S(2)}, u32[]{:S(2)}) %collective-permute-start.7) | collective-permute-done | bytes 65568 | tf_op jit(solution)/shard_map/ppermute | solution.py:290
  27.2 0.5 %collective-permute-start.8 = (f32[4,16,128]{2,1,0:T(8,128)S(1)}, f32[4,16,128]{2,1,0:T(8,128)S(1)}, u32[]{:S(2)}, u32[]{:S(2)}) collective-permute-start(f32[4,16,128]{2,1,0:T(8,128)S(1)} %get-tuple-element.16), channel_id=1, source_target_pairs={{0,6},{2,4},{4,2},{6,0},{8,14},{10,12},{12,10},{14,8},{16,22},{18,... | collective-permute-start | bytes 98312 | tf_op jit(solution)/shard_map/ppermute | solution.py:290
  27.7 2.9 %collective-permute-done.8.came = f32[4,16,128]{2,1,0:T(8,128)S(1)} collective-permute-done((f32[4,16,128]{2,1,0:T(8,128)S(1)}, f32[4,16,128]{2,1,0:T(8,128)S(1)}, u32[]{:S(2)}, u32[]{:S(2)}) %collective-permute-start.8) | collective-permute-done | bytes 32800 | tf_op jit(solution)/shard_map/ppermute | solution.py:290
  30.6 1.6 %collective-permute-start.9 = (f32[2,16,128]{2,1,0:T(8,128)S(1)}, f32[2,16,128]{2,1,0:T(8,128)S(1)}, u32[]{:S(2)}, u32[]{:S(2)}) collective-permute-start(f32[2,16,128]{2,1,0:T(8,128)S(1)} %get-tuple-element.18), channel_id=1, source_target_pairs={{0,10},{2,8},{4,14},{6,12},{8,2},{10,0},{12,6},{14,4},{16,26},{18,... | collective-permute-start | bytes 49160 | tf_op jit(solution)/shard_map/ppermute | solution.py:290
  32.2 1.6 %collective-permute-done.9.came = f32[2,16,128]{2,1,0:T(8,128)S(1)} collective-permute-done((f32[2,16,128]{2,1,0:T(8,128)S(1)}, f32[2,16,128]{2,1,0:T(8,128)S(1)}, u32[]{:S(2)}, u32[]{:S(2)}) %collective-permute-start.9) | collective-permute-done | bytes 16416 | tf_op jit(solution)/shard_map/ppermute | solution.py:290
  33.8 2.2 %collective-permute-start.10 = (f32[1,16,128]{2,1,0:T(8,128)S(1)}, f32[1,16,128]{2,1,0:T(8,128)S(1)}, u32[]{:S(2)}, u32[]{:S(2)}) collective-permute-start(f32[1,16,128]{2,1,0:T(8,128)S(1)} %get-tuple-element.20), channel_id=1, source_target_pairs={{0,18},{2,16},{4,22},{6,20},{8,26},{10,24},{12,30},{14,28},{16,2},... | collective-permute-start | bytes 24584 | tf_op jit(solution)/shard_map/ppermute | solution.py:290
  36.0 1.8 %collective-permute-done.10.came = f32[1,16,128]{2,1,0:T(8,128)S(1)} collective-permute-done((f32[1,16,128]{2,1,0:T(8,128)S(1)}, f32[1,16,128]{2,1,0:T(8,128)S(1)}, u32[]{:S(2)}, u32[]{:S(2)}) %collective-permute-start.10) | collective-permute-done | bytes 8224 | tf_op jit(solution)/shard_map/ppermute | solution.py:290
  37.7 0.7 %shard_map.80 = f32[2,16,64]{2,1,0:T(8,128)} custom-call(f32[1,16,128]{2,1,0:T(8,128)S(1)} %get-tuple-element.19.held, f32[1,16,128]{2,1,0:T(8,128)S(1)} %collective-permute-done.10.came), custom_call_target="tpu_custom_call" | custom-call | tf_op jit(solution)/shard_map/pallas_call | solution.py:301
  (9 shorter events, 0.0 us)
Async XLA Ops:
  0.6 5.0 %collective-permute-start = (f32[2,16,64]{2,1,0:T(8,128)}, f32[2,16,64]{2,1,0:T(8,128)S(1)}, u32[]{:S(2)}, u32[]{:S(2)}) collective-permute-start(f32[2,16,64]{2,1,0:T(8,128)} %param.5), channel_id=1, source_target_pairs={{0,1},{1,0},{2,3},{3,2},{4,5},{5,4},{6,7},{7,6},{8,9},{9,8},{10,11... | collective-permute-start | bytes 24584 | tf_op jit(solution)/shard_map/ppermute | solution.py:283
  5.6 1.2 %collective-permute-start.1 = (f32[40,64]{1,0:T(8,128)S(1)}, f32[40,64]{1,0:T(8,128)S(1)}, u32[]{:S(2)}, u32[]{:S(2)}) collective-permute-start(f32[40,64]{1,0:T(8,128)S(1)} %shard_map.67.mine), channel_id=1, source_target_pairs={{0,2},{2,0},{4,6},{6,4},{8,10},{10,8},{12,14},{14,12},{16,18},{18,... | collective-permute-start | bytes 30728 | tf_op jit(solution)/shard_map/ppermute | solution.py:290
  6.9 4.9 %collective-permute-start.2 = (f32[1,40,128]{2,1,0:T(8,128)S(1)}, f32[1,40,128]{2,1,0:T(8,128)S(1)}, u32[]{:S(2)}, u32[]{:S(2)}) collective-permute-start(f32[1,40,128]{2,1,0:T(8,128)S(1)} %bitcast.49), channel_id=1, source_target_pairs={{0,18},{2,16},{4,22},{6,20},{8,26},{10,24},{12,30},{14,28},{16,2},... | collective-permute-start | bytes 61448 | tf_op jit(solution)/shard_map/ppermute | solution.py:290
  9.8 9.5 %collective-permute-start.5 = (f32[1,2,16,1024]{3,2,1,0:T(8,128)}, f32[1,2,16,1024]{3,2,1,0:T(8,128)S(1)}, u32[]{:S(2)}, u32[]{:S(2)}) collective-permute-start(f32[1,2,16,1024]{3,2,1,0:T(8,128)} %param.6), channel_id=1, source_target_pairs={{0,1},{1,0},{2,3},{3,2},{4,5},{5,4},{6,7},{7,6},{8,9},{9,8},{10,11... | collective-permute-start | bytes 393224 | tf_op jit(solution)/shard_map/ppermute | solution.py:283
  11.3 9.0 %collective-permute-start.6 = (f32[1,2,16,1024]{3,2,1,0:T(8,128)}, f32[1,2,16,1024]{3,2,1,0:T(8,128)S(1)}, u32[]{:S(2)}, u32[]{:S(2)}) collective-permute-start(f32[1,2,16,1024]{3,2,1,0:T(8,128)} %param.7), channel_id=1, source_target_pairs={{0,1},{1,0},{2,3},{3,2},{4,5},{5,4},{6,7},{7,6},{8,9},{9,8},{10,11... | collective-permute-start | bytes 393224 | tf_op jit(solution)/shard_map/ppermute | solution.py:283
  11.8 3.8 %collective-permute-start.3 = (f32[2,40,128]{2,1,0:T(8,128)S(1)}, f32[2,40,128]{2,1,0:T(8,128)S(1)}, u32[]{:S(2)}, u32[]{:S(2)}) collective-permute-start(f32[2,40,128]{2,1,0:T(8,128)S(1)} %shard_map.69.mine.refs_1_), channel_id=1, source_target_pairs={{0,10},{2,8},{4,14},{6,12},{8,2},{10,0},{12,6},{14,4},{16,26},{18,... | collective-permute-start | bytes 122888 | tf_op jit(solution)/shard_map/ppermute | solution.py:290
  15.6 5.6 %collective-permute-start.4 = (f32[4,40,128]{2,1,0:T(8,128)S(1)}, f32[4,40,128]{2,1,0:T(8,128)S(1)}, u32[]{:S(2)}, u32[]{:S(2)}) collective-permute-start(f32[4,40,128]{2,1,0:T(8,128)S(1)} %shard_map.70), channel_id=1, source_target_pairs={{0,6},{2,4},{4,2},{6,0},{8,14},{10,12},{12,10},{14,8},{16,22},{18,... | collective-permute-start | bytes 245768 | tf_op jit(solution)/shard_map/ppermute | solution.py:290
  18.5 0.9 %copy-start = (f32[1,2,16,1024]{3,2,1,0:T(8,128)S(1)}, f32[1,2,16,1024]{3,2,1,0:T(8,128)}, u32[]{:S(2)}) copy-start(f32[1,2,16,1024]{3,2,1,0:T(8,128)} %param.6) | copy-start | bytes 393220
  18.5 1.8 %copy-start.1 = (f32[1,2,16,1024]{3,2,1,0:T(8,128)S(1)}, f32[1,2,16,1024]{3,2,1,0:T(8,128)}, u32[]{:S(2)}) copy-start(f32[1,2,16,1024]{3,2,1,0:T(8,128)} %param.7) | copy-start | bytes 393220
  25.9 1.3 %collective-permute-start.7 = (f32[128,128]{1,0:T(8,128)S(1)}, f32[128,128]{1,0:T(8,128)S(1)}, u32[]{:S(2)}, u32[]{:S(2)}) collective-permute-start(f32[128,128]{1,0:T(8,128)S(1)} %get-tuple-element.14), channel_id=1, source_target_pairs={{0,2},{2,0},{4,6},{6,4},{8,10},{10,8},{12,14},{14,12},{16,18},{18,... | collective-permute-start | bytes 196616 | tf_op jit(solution)/shard_map/ppermute | solution.py:290
  27.2 3.4 %collective-permute-start.8 = (f32[4,16,128]{2,1,0:T(8,128)S(1)}, f32[4,16,128]{2,1,0:T(8,128)S(1)}, u32[]{:S(2)}, u32[]{:S(2)}) collective-permute-start(f32[4,16,128]{2,1,0:T(8,128)S(1)} %get-tuple-element.16), channel_id=1, source_target_pairs={{0,6},{2,4},{4,2},{6,0},{8,14},{10,12},{12,10},{14,8},{16,22},{18,... | collective-permute-start | bytes 98312 | tf_op jit(solution)/shard_map/ppermute | solution.py:290
  30.6 3.2 %collective-permute-start.9 = (f32[2,16,128]{2,1,0:T(8,128)S(1)}, f32[2,16,128]{2,1,0:T(8,128)S(1)}, u32[]{:S(2)}, u32[]{:S(2)}) collective-permute-start(f32[2,16,128]{2,1,0:T(8,128)S(1)} %get-tuple-element.18), channel_id=1, source_target_pairs={{0,10},{2,8},{4,14},{6,12},{8,2},{10,0},{12,6},{14,4},{16,26},{18,... | collective-permute-start | bytes 49160 | tf_op jit(solution)/shard_map/ppermute | solution.py:290
  33.8 4.0 %collective-permute-start.10 = (f32[1,16,128]{2,1,0:T(8,128)S(1)}, f32[1,16,128]{2,1,0:T(8,128)S(1)}, u32[]{:S(2)}, u32[]{:S(2)}) collective-permute-start(f32[1,16,128]{2,1,0:T(8,128)S(1)} %get-tuple-element.20), channel_id=1, source_target_pairs={{0,18},{2,16},{4,22},{6,20},{8,26},{10,24},{12,30},{14,28},{16,2},... | collective-permute-start | bytes 24584 | tf_op jit(solution)/shard_map/ppermute | solution.py:290

commit v3 on v2

--- a/solution.py
+++ b/solution.py
@@ -150,33 +150,31 @@
     chebyshev(levels, (0, 1), low, high, lowest, rows, two)
 
 
-def coefficient_kernel(shared, *refs):
+def coefficient_kernel(shared, tiles, *refs):
     freq_ref, slow_ref, out_ref = refs[0], refs[1], refs[-1]
     count, rows, _ = slow_ref.shape
     slot = 0
     for bit, other in shared:
         own = (lax.axis_index("freq") >> bit) & 1
         slot = 2 * slot + (1 - own if other else own)
-    groups = rows // SUBLANES
-    freq = jnp.broadcast_to(freq_ref[...], (SUBLANES, LANES))
-
-    def body(index, carry):
-        piece = index // groups
-        start = pl.multiple_of((index % groups) * SUBLANES, SUBLANES)
-        phases = node_phases(freq * slow_ref[piece, pl.ds(start, SUBLANES), :])
-        for part in range(2):
-            for order, value in enumerate(cosine_sums([p[part] for p in phases])):
-                out_ref[order, part, (piece << len(shared)) + slot, pl.ds(start, SUBLANES), :] = value
+    freq = freq_ref[...]
+
+    def body(piece, carry):
+        place = (piece << len(shared)) + slot
+        for start in range(0, rows, SUBLANES):
+            phases = node_phases(freq * slow_ref[piece, start : start + SUBLANES, :])
+            for part in range(2):
+                for order, value in enumerate(cosine_sums([p[part] for p in phases])):
+                    out_ref[order, part, pl.ds(start * tiles + place, SUBLANES, stride=tiles), :] = value
         return carry
 
-    lax.fori_loop(0, count * groups, body, 0)
+    lax.fori_loop(0, count, body, 0)
 
 
 def main_kernel(setup, coef_ref, src_levels, rec_levels, *refs):
     rows, halo, depth_steps, two, packed, width = setup
     image_refs, (src_ref, rec_ref, levels) = refs[:-3], refs[-3:]
     tiles = levels.shape[3]
-    coef_rows = coef_ref.shape[2] // tiles
     flip = lax.axis_index("lat")
     lane = lax.broadcasted_iota(jnp.int32, (tiles, LANES), 1)
     tile = lax.broadcasted_iota(jnp.int32, (tiles, LANES), 0)
@@ -219,9 +217,9 @@
         next_lowest = window(rows, max(later - 1, 1), two)[0]
         row_images = []
         for row in range(low, high):
-            start = coef_row(step, row)
+            start = pl.multiple_of(coef_row(step, row) * tiles, SUBLANES)
             coefs = [
-                [coef_ref[order, part, pl.ds(start, tiles, stride=coef_rows), :] for part in range(2)]
+                [coef_ref[order, part, pl.ds(start, tiles), :] for part in range(2)]
                 for order in range(TERMS)
             ]
             outs = []
@@ -322,6 +320,27 @@
         out[after + step * rows : after + (step + 1) * rows, :] = layer[...]
 
 
+def pair_kernel(halo, *refs):
+    layers, (core, out, edge) = refs[:-3], refs[-3:]
+    rows = layers[0].shape[0]
+    upper = (lax.axis_index("freq") & 1) != 0
+    for step, layer in enumerate(layers):
+        mine, other = layer[...], core[step]
+        pair = jnp.concatenate([jnp.where(upper, other, mine), jnp.where(upper, mine, other)], axis=1)
+        out[step * rows : (step + 1) * rows, :] = pair
+    start = pl.multiple_of((1 - lax.axis_index("lat")) * (rows - halo), SUBLANES)
+    edge[...] = out[pl.ds(start, halo), :]
+
+
+def tile_kernel(pair, edge, freq, out, freq_out):
+    halo, rows = edge.shape[0], out.shape[0] - edge.shape[0]
+    first = rows // 2
+    out[:first, :] = pair[:first, :]
+    out[first : first + halo, :] = edge[...]
+    out[first + halo :, :] = pair[first:, :]
+    freq_out[...] = freq[...]
+
+
 def beside_kernel(bit, mine, other, out):
     upper = ((lax.axis_index("freq") >> bit) & 1) != 0
     first, second = mine[...], other[...]
@@ -335,13 +354,14 @@
         out[2 * piece + 1 - slot] = other[piece]
 
 
-def gather_columns(block):
+def gather_columns(block, done=0):
     count = lax.axis_size("freq")
     rows, width = block.shape
+    width >>= done
     bits = range(count.bit_length() - 1)
     inner = [b for b in bits if width << b < LANES]
     outer = [b for b in bits if width << b >= LANES][::-1]
-    for b in inner:
+    for b in inner[done:]:
         other = partner(block, 1 << b)
         shape = (rows, 2 * block.shape[1])
         block = call(functools.partial(beside_kernel, b), shape, block, other, cost_estimate=COST)
@@ -399,14 +419,24 @@
     span = high + REACH - (low if two else low - REACH)
     later_span = window(rows, 1, two)[1] - window(rows, 1, two)[0]
 
-    slow_sides = from_sides(slowness)
     src_sides = from_sides(src_field)
     rec_sides = from_sides(rec_field)
-    coef_rows = (rows + halo * len(slow_sides)) + (depth_steps - 1) * rows
+    coef_rows = depth_steps * rows + halo * len(src_sides)
     layers = [slowness[z] for z in range(depth_steps)]
-    kernel = functools.partial(bundle_kernel, halo, two)
-    bundle = call(kernel, (coef_rows, width), *layers, *slow_sides)
-    parts = gather_columns(bundle)
+    freq = jnp.broadcast_to(frequencies, (SUBLANES, LANES))
+    if two and 2 * width == LANES and depth_steps == 2:
+        core = partner(slowness, 1)
+        shapes = [(depth_steps * rows, LANES), (halo, LANES)]
+        pair, edge = call(functools.partial(pair_kernel, halo), shapes, *layers, core, cost_estimate=COST)
+        (edge,) = from_sides(edge)
+        shapes = [(coef_rows, LANES), (SUBLANES, LANES)]
+        block, freq = call(tile_kernel, shapes, pair, edge, freq, cost_estimate=COST)
+        parts = gather_columns(block, done=1)
+    else:
+        slow_sides = from_sides(slowness)
+        kernel = functools.partial(bundle_kernel, halo, two)
+        bundle = call(kernel, (coef_rows, width), *layers, *slow_sides)
+        parts = gather_columns(bundle)
 
     def first_levels(own, sides, conjugate):
         fields = [tiled(x[0]) for x in (own, *sides)]
@@ -416,13 +446,12 @@
     src_levels = first_levels(src_field, src_sides, False)
     rec_levels = first_levels(rec_field, rec_sides, True)
 
-    coef_shape = (TERMS, 2, tiles, coef_rows, LANES)
-    freq = frequencies.reshape(1, 1)
+    coef_shape = (TERMS, 2, coef_rows * tiles, LANES)
     coefs = []
     for part, shared in parts:
         coefs = [
             call(
-                functools.partial(coefficient_kernel, shared),
+                functools.partial(coefficient_kernel, shared, tiles),
                 coef_shape,
                 freq,
                 part,
@@ -440,7 +469,7 @@
     *image, src, rec = call(
         functools.partial(main_kernel, setup),
         [*image_shapes, field_shape, field_shape],
-        coefs[0].reshape(TERMS, 2, tiles * coef_rows, LANES),
+        coefs[0],
         src_levels,
         rec_levels,
         mib=16,

time: 38.7 us -> 36.7 us (0.948)
  waiting for transfers between devices: 12.4 us -> 10.5 us
  Pallas kernels: 8.87 us -> 7.81 us
  starting transfers between devices: 15 us -> 15.7 us
    ppermute x8, waiting for transfers between devices: 11.2 us -> 9.59 us  [partner(): lax.ppermute(block, 'freq', [(i, i ^ mask) for i in range(lax.axis_size('...]
    pallas_call x14, Pallas kernels: 8.87 us -> 7.81 us  [call(): pl.pallas_call(kernel, out_shape=outs[0] if single else outs, out_specs=V...]
    ppermute x8, starting transfers between devices: 9.87 us -> 10.8 us  [partner(): lax.ppermute(block, 'freq', [(i, i ^ mask) for i in range(lax.axis_size('...]
  transfers between devices with their start and end apart: 11 -> 11, of which waited for: 7 -> 8; matrix products, arithmetic and copies ran while one was open for 2% -> 2% of each run, Pallas kernels for 9% -> 8%
where the time goes in v3:
time: 36.7 us; the launch traced here: 36.4 us
  starting transfers between devices  15.7 us (43%)
  waiting for transfers between devices  10.5 us (29%)
  Pallas kernels  7.81 us (21%)
  between operations  1.39 us (4%)
  local copies, waits for them, and re-layouts  0.97 us (3%)
    ppermute x8, starting transfers between devices, partner(): lax.ppermute(block, 'freq', [(i, i ^ mask) for i in range(lax.axis_size('...  10.8 us
    ppermute x8, waiting for transfers between devices, partner(): lax.ppermute(block, 'freq', [(i, i ^ mask) for i in range(lax.axis_size('...  9.59 us
    pallas_call x14, Pallas kernels, call(): pl.pallas_call(kernel, out_shape=outs[0] if single else outs, out_specs=V...  7.81 us
    ppermute x3, starting transfers between devices, from_sides(): return [lax.ppermute(block, 'lat', [(0, 1), (1, 0)])]  4.87 us
    ppermute x3, waiting for transfers between devices, from_sides(): return [lax.ppermute(block, 'lat', [(0, 1), (1, 0)])]  0.94 us
  transfers between devices with their start and end apart: 11, of which 8 were waited for; matrix products, arithmetic and copies ran while one was open for 2% of the time, Pallas kernels for 8%

profile of v3, /device:TPU:0, one launch (start us, length us, event | category | flops | bytes accessed | tf_op | source)
XLA Modules:
  0.0 36.4 jit_solution(8503738643645829987)
XLA Ops:
  0.6 0.6 %collective-permute-start = (f32[2,16,64]{2,1,0:T(8,128)}, f32[2,16,64]{2,1,0:T(8,128)S(1)}, u32[]{:S(2)}, u32[]{:S(2)}) collective-permute-start(f32[2,16,64]{2,1,0:T(8,128)} %param.5), channel_id=1, source_target_pairs={{0,2},{2,0},{4,6},{6,4},{8,10},{10,8},{12,14},{14,12},{16,18},{18,... | collective-permute-start | bytes 24584 | tf_op jit(solution)/shard_map/ppermute | solution.py:288
  1.2 0.7 %slice_bitcast_fusion = (f32[16,64]{1,0:T(8,128)S(1)}, f32[16,64]{1,0:T(8,128)S(1)}) fusion(f32[2,16,64]{2,1,0:T(8,128)} %param.5), kind=kLoop, calls=%fused_computation | loop fusion | bytes 16384 | tf_op jit(solution)/shard_map/squeeze | solution.py:425
  1.9 0.3 collective-permute-done.refs_2_
  2.2 0.1 shard_map.70
  2.3 2.8 %collective-permute-start.1 = (f32[8,128]{1,0:T(8,128)S(1)}, f32[8,128]{1,0:T(8,128)S(1)}, u32[]{:S(2)}, u32[]{:S(2)}) collective-permute-start(f32[8,128]{1,0:T(8,128)S(1)} %get-tuple-element.18), channel_id=1, source_target_pairs={{0,1},{1,0},{2,3},{3,2},{4,5},{5,4},{6,7},{7,6},{8,9},{9,8},{10,11... | collective-permute-start | bytes 12296 | tf_op jit(solution)/shard_map/ppermute | solution.py:281
  5.8 0.9 %collective-permute-done.1.edge = f32[8,128]{1,0:T(8,128)S(1)} collective-permute-done((f32[8,128]{1,0:T(8,128)S(1)}, f32[8,128]{1,0:T(8,128)S(1)}, u32[]{:S(2)}, u32[]{:S(2)}) %collective-permute-start.1) | collective-permute-done | bytes 4128 | tf_op jit(solution)/shard_map/ppermute | solution.py:281
  6.8 1.7 %collective-permute-start.2 = (f32[1,40,128]{2,1,0:T(8,128)S(1)}, f32[1,40,128]{2,1,0:T(8,128)S(1)}, u32[]{:S(2)}, u32[]{:S(2)}) collective-permute-start(f32[1,40,128]{2,1,0:T(8,128)S(1)} %bitcast.45), channel_id=1, source_target_pairs={{0,18},{2,16},{4,22},{6,20},{8,26},{10,24},{12,30},{14,28},{16,2},... | collective-permute-start | bytes 61448 | tf_op jit(solution)/shard_map/ppermute | solution.py:288
  8.5 1.5 %collective-permute-start.5 = (f32[1,2,16,1024]{3,2,1,0:T(8,128)}, f32[1,2,16,1024]{3,2,1,0:T(8,128)S(1)}, u32[]{:S(2)}, u32[]{:S(2)}) collective-permute-start(f32[1,2,16,1024]{3,2,1,0:T(8,128)} %param.6), channel_id=1, source_target_pairs={{0,1},{1,0},{2,3},{3,2},{4,5},{5,4},{6,7},{7,6},{8,9},{9,8},{10,11... | collective-permute-start | bytes 393224 | tf_op jit(solution)/shard_map/ppermute | solution.py:281
  10.0 0.5 %collective-permute-start.6 = (f32[1,2,16,1024]{3,2,1,0:T(8,128)}, f32[1,2,16,1024]{3,2,1,0:T(8,128)S(1)}, u32[]{:S(2)}, u32[]{:S(2)}) collective-permute-start(f32[1,2,16,1024]{3,2,1,0:T(8,128)} %param.7), channel_id=1, source_target_pairs={{0,1},{1,0},{2,3},{3,2},{4,5},{5,4},{6,7},{7,6},{8,9},{9,8},{10,11... | collective-permute-start | bytes 393224 | tf_op jit(solution)/shard_map/ppermute | solution.py:281
  10.5 0.4 %collective-permute-done.2.other = f32[1,40,128]{2,1,0:T(8,128)S(1)} collective-permute-done((f32[1,40,128]{2,1,0:T(8,128)S(1)}, f32[1,40,128]{2,1,0:T(8,128)S(1)}, u32[]{:S(2)}, u32[]{:S(2)}) %collective-permute-start.2) | collective-permute-done | bytes 20512 | tf_op jit(solution)/shard_map/ppermute | solution.py:288
  10.9 1.8 %collective-permute-start.3 = (f32[2,40,128]{2,1,0:T(8,128)S(1)}, f32[2,40,128]{2,1,0:T(8,128)S(1)}, u32[]{:S(2)}, u32[]{:S(2)}) collective-permute-start(f32[2,40,128]{2,1,0:T(8,128)S(1)} %shard_map.72.mine.refs_1_), channel_id=1, source_target_pairs={{0,10},{2,8},{4,14},{6,12},{8,2},{10,0},{12,6},{14,4},{16,26},{18,... | collective-permute-start | bytes 122888 | tf_op jit(solution)/shard_map/ppermute | solution.py:288
  12.7 1.7 %collective-permute-done.3.other.refs_1_ = f32[2,40,128]{2,1,0:T(8,128)S(1)} collective-permute-done((f32[2,40,128]{2,1,0:T(8,128)S(1)}, f32[2,40,128]{2,1,0:T(8,128)S(1)}, u32[]{:S(2)}, u32[]{:S(2)}) %collective-permute-start.3) | collective-permute-done | bytes 40992 | tf_op jit(solution)/shard_map/ppermute | solution.py:288
  14.4 2.1 %collective-permute-start.4 = (f32[4,40,128]{2,1,0:T(8,128)S(1)}, f32[4,40,128]{2,1,0:T(8,128)S(1)}, u32[]{:S(2)}, u32[]{:S(2)}) collective-permute-start(f32[4,40,128]{2,1,0:T(8,128)S(1)} %shard_map.73), channel_id=1, source_target_pairs={{0,6},{2,4},{4,2},{6,0},{8,14},{10,12},{12,10},{14,8},{16,22},{18,... | collective-permute-start | bytes 245768 | tf_op jit(solution)/shard_map/ppermute | solution.py:288
  16.5 0.6 %shard_map.74.refs_2_ = f32[8,2,320,128]{3,2,1,0:T(8,128)S(1)} custom-call(f32[8,128]{1,0:T(8,128)S(1)} %get-tuple-element.19.refs_0_, f32[2,40,128]{2,1,0:T(8,128)S(1)} %shard_map.72.mine.refs_1_), custom_call_target="tpu_custom_call" | custom-call | flops 67108864 | bytes 4194304 | tf_op jit(solution)/shard_map/pallas_call | solution.py:299
  17.2 0.0 copy-start
  17.2 0.0 copy-start.1
  17.2 0.6 %shard_map.75.refs_2_ = f32[8,2,320,128]{3,2,1,0:T(8,128)S(1)} custom-call(f32[8,128]{1,0:T(8,128)S(1)} %get-tuple-element.19.refs_0_, f32[2,40,128]{2,1,0:T(8,128)S(1)} %collective-permute-done.3.other.refs_1_, f32[8,2,320,128]{3,2,1,0:T(8,128)S(1)} %shard_map.74.refs_2_), custom_call_target="tpu_custom_call", output_to_operand_aliasing={{}: (2, {})} | custom-call | flops 67108864 | bytes 4194304 | tf_op jit(solution)/shard_map/pallas_call | solution.py:299
  17.8 0.0 collective-permute-done.5
  17.8 0.2 copy-done
  18.1 0.9 %shard_map.77.src_levels = f32[8,2,30,8,128]{4,3,2,1,0:T(8,128)S(1)} custom-call(f32[2,128,128]{2,1,0:T(8,128)S(1)} %bitcast.39, f32[2,128,128]{2,1,0:T(8,128)S(1)} %bitcast.42), custom_call_target="tpu_custom_call" | custom-call | flops 67108864 | bytes 4194304 | tf_op jit(solution)/shard_map/pallas_call | solution.py:299
  19.0 0.9 %shard_map.78.rec_levels = f32[8,2,30,8,128]{4,3,2,1,0:T(8,128)S(1)} custom-call(f32[2,128,128]{2,1,0:T(8,128)S(1)} %bitcast.40, f32[2,128,128]{2,1,0:T(8,128)S(1)} %bitcast.41), custom_call_target="tpu_custom_call" | custom-call | flops 67108864 | bytes 4194304 | tf_op jit(solution)/shard_map/pallas_call | solution.py:299
  19.9 1.2 %shard_map.76.coef_ref = f32[8,2,320,128]{3,2,1,0:T(8,128)S(1)} custom-call(f32[8,128]{1,0:T(8,128)S(1)} %get-tuple-element.19.refs_0_, f32[4,40,128]{2,1,0:T(8,128)S(1)} %collective-permute-done.4.refs_1_, f32[8,2,320,128]{3,2,1,0:T(8,128)S(1)} %shard_map.75.refs_2_), custom_call_target="tpu_custom_call", output_to_operand_aliasing={{}: (2, {})} | custom-call | flops 67108864 | bytes 4194304 | tf_op jit(solution)/shard_map/pallas_call | solution.py:299
  21.1 2.8 %shard_map.79 = (f32[128,128]{1,0:T(8,128)S(1)}, f32[128,128]{1,0:T(8,128)S(1)}, f32[2,128,128]{2,1,0:T(8,128)}, f32[2,128,128]{2,1,0:T(8,128)}) custom-call(f32[8,2,320,128]{3,2,1,0:T(8,128)S(1)} %shard_map.76.coef_ref, f32[8,2,30,8,128]{4,3,2,1,0:T(8,128)S(1)} %shard_map.77.src_levels, f32[8,2,30,8,128]{4,3,2,1,0:T(8,128)S(1)} %shard_map.78.rec_levels), custom_call_target="tpu_custom_call" | custom-call | tf_op jit(solution)/shard_map/pallas_call | solution.py:299
  23.9 0.1 collective-permute-start.7
  24.0 1.2 %collective-permute-done.7 = f32[128,128]{1,0:T(8,128)S(1)} collective-permute-done((f32[128,128]{1,0:T(8,128)S(1)}, f32[128,128]{1,0:T(8,128)S(1)}, u32[]{:S(2)}, u32[]{:S(2)}) %collective-permute-start.7) | collective-permute-done | bytes 65568 | tf_op jit(solution)/shard_map/ppermute | solution.py:288
  25.2 0.8 %collective-permute-start.8 = (f32[4,16,128]{2,1,0:T(8,128)S(1)}, f32[4,16,128]{2,1,0:T(8,128)S(1)}, u32[]{:S(2)}, u32[]{:S(2)}) collective-permute-start(f32[4,16,128]{2,1,0:T(8,128)S(1)} %get-tuple-element.24), channel_id=1, source_target_pairs={{0,6},{2,4},{4,2},{6,0},{8,14},{10,12},{12,10},{14,8},{16,22},{18,... | collective-permute-start | bytes 98312 | tf_op jit(solution)/shard_map/ppermute | solution.py:288
  26.0 2.6 %collective-permute-done.8.came = f32[4,16,128]{2,1,0:T(8,128)S(1)} collective-permute-done((f32[4,16,128]{2,1,0:T(8,128)S(1)}, f32[4,16,128]{2,1,0:T(8,128)S(1)}, u32[]{:S(2)}, u32[]{:S(2)}) %collective-permute-start.8) | collective-permute-done | bytes 32800 | tf_op jit(solution)/shard_map/ppermute | solution.py:288
  28.6 1.3 %collective-permute-start.9 = (f32[2,16,128]{2,1,0:T(8,128)S(1)}, f32[2,16,128]{2,1,0:T(8,128)S(1)}, u32[]{:S(2)}, u32[]{:S(2)}) collective-permute-start(f32[2,16,128]{2,1,0:T(8,128)S(1)} %get-tuple-element.26), channel_id=1, source_target_pairs={{0,10},{2,8},{4,14},{6,12},{8,2},{10,0},{12,6},{14,4},{16,26},{18,... | collective-permute-start | bytes 49160 | tf_op jit(solution)/shard_map/ppermute | solution.py:288
  29.9 1.8 %collective-permute-done.9.came = f32[2,16,128]{2,1,0:T(8,128)S(1)} collective-permute-done((f32[2,16,128]{2,1,0:T(8,128)S(1)}, f32[2,16,128]{2,1,0:T(8,128)S(1)}, u32[]{:S(2)}, u32[]{:S(2)}) %collective-permute-start.9) | collective-permute-done | bytes 16416 | tf_op jit(solution)/shard_map/ppermute | solution.py:288
  31.8 2.4 %collective-permute-start.10 = (f32[1,16,128]{2,1,0:T(8,128)S(1)}, f32[1,16,128]{2,1,0:T(8,128)S(1)}, u32[]{:S(2)}, u32[]{:S(2)}) collective-permute-start(f32[1,16,128]{2,1,0:T(8,128)S(1)} %get-tuple-element.28), channel_id=1, source_target_pairs={{0,18},{2,16},{4,22},{6,20},{8,26},{10,24},{12,30},{14,28},{16,2},... | collective-permute-start | bytes 24584 | tf_op jit(solution)/shard_map/ppermute | solution.py:288
  34.1 1.6 %collective-permute-done.10.came = f32[1,16,128]{2,1,0:T(8,128)S(1)} collective-permute-done((f32[1,16,128]{2,1,0:T(8,128)S(1)}, f32[1,16,128]{2,1,0:T(8,128)S(1)}, u32[]{:S(2)}, u32[]{:S(2)}) %collective-permute-start.10) | collective-permute-done | bytes 8224 | tf_op jit(solution)/shard_map/ppermute | solution.py:288
  35.7 0.7 %shard_map.83 = f32[2,16,64]{2,1,0:T(8,128)} custom-call(f32[1,16,128]{2,1,0:T(8,128)S(1)} %get-tuple-element.27.held, f32[1,16,128]{2,1,0:T(8,128)S(1)} %collective-permute-done.10.came), custom_call_target="tpu_custom_call" | custom-call | tf_op jit(solution)/shard_map/pallas_call | solution.py:299
  (10 shorter events, 0.1 us)
Async XLA Ops:
  0.6 1.6 %collective-permute-start = (f32[2,16,64]{2,1,0:T(8,128)}, f32[2,16,64]{2,1,0:T(8,128)S(1)}, u32[]{:S(2)}, u32[]{:S(2)}) collective-permute-start(f32[2,16,64]{2,1,0:T(8,128)} %param.5), channel_id=1, source_target_pairs={{0,2},{2,0},{4,6},{6,4},{8,10},{10,8},{12,14},{14,12},{16,18},{18,... | collective-permute-start | bytes 24584 | tf_op jit(solution)/shard_map/ppermute | solution.py:288
  2.3 4.4 %collective-permute-start.1 = (f32[8,128]{1,0:T(8,128)S(1)}, f32[8,128]{1,0:T(8,128)S(1)}, u32[]{:S(2)}, u32[]{:S(2)}) collective-permute-start(f32[8,128]{1,0:T(8,128)S(1)} %get-tuple-element.18), channel_id=1, source_target_pairs={{0,1},{1,0},{2,3},{3,2},{4,5},{5,4},{6,7},{7,6},{8,9},{9,8},{10,11... | collective-permute-start | bytes 12296 | tf_op jit(solution)/shard_map/ppermute | solution.py:281
  6.8 4.1 %collective-permute-start.2 = (f32[1,40,128]{2,1,0:T(8,128)S(1)}, f32[1,40,128]{2,1,0:T(8,128)S(1)}, u32[]{:S(2)}, u32[]{:S(2)}) collective-permute-start(f32[1,40,128]{2,1,0:T(8,128)S(1)} %bitcast.45), channel_id=1, source_target_pairs={{0,18},{2,16},{4,22},{6,20},{8,26},{10,24},{12,30},{14,28},{16,2},... | collective-permute-start | bytes 61448 | tf_op jit(solution)/shard_map/ppermute | solution.py:288
  8.5 9.3 %collective-permute-start.5 = (f32[1,2,16,1024]{3,2,1,0:T(8,128)}, f32[1,2,16,1024]{3,2,1,0:T(8,128)S(1)}, u32[]{:S(2)}, u32[]{:S(2)}) collective-permute-start(f32[1,2,16,1024]{3,2,1,0:T(8,128)} %param.6), channel_id=1, source_target_pairs={{0,1},{1,0},{2,3},{3,2},{4,5},{5,4},{6,7},{7,6},{8,9},{9,8},{10,11... | collective-permute-start | bytes 393224 | tf_op jit(solution)/shard_map/ppermute | solution.py:281
  10.0 9.0 %collective-permute-start.6 = (f32[1,2,16,1024]{3,2,1,0:T(8,128)}, f32[1,2,16,1024]{3,2,1,0:T(8,128)S(1)}, u32[]{:S(2)}, u32[]{:S(2)}) collective-permute-start(f32[1,2,16,1024]{3,2,1,0:T(8,128)} %param.7), channel_id=1, source_target_pairs={{0,1},{1,0},{2,3},{3,2},{4,5},{5,4},{6,7},{7,6},{8,9},{9,8},{10,11... | collective-permute-start | bytes 393224 | tf_op jit(solution)/shard_map/ppermute | solution.py:281
  10.9 3.5 %collective-permute-start.3 = (f32[2,40,128]{2,1,0:T(8,128)S(1)}, f32[2,40,128]{2,1,0:T(8,128)S(1)}, u32[]{:S(2)}, u32[]{:S(2)}) collective-permute-start(f32[2,40,128]{2,1,0:T(8,128)S(1)} %shard_map.72.mine.refs_1_), channel_id=1, source_target_pairs={{0,10},{2,8},{4,14},{6,12},{8,2},{10,0},{12,6},{14,4},{16,26},{18,... | collective-permute-start | bytes 122888 | tf_op jit(solution)/shard_map/ppermute | solution.py:288
  14.4 5.4 %collective-permute-start.4 = (f32[4,40,128]{2,1,0:T(8,128)S(1)}, f32[4,40,128]{2,1,0:T(8,128)S(1)}, u32[]{:S(2)}, u32[]{:S(2)}) collective-permute-start(f32[4,40,128]{2,1,0:T(8,128)S(1)} %shard_map.73), channel_id=1, source_target_pairs={{0,6},{2,4},{4,2},{6,0},{8,14},{10,12},{12,10},{14,8},{16,22},{18,... | collective-permute-start | bytes 245768 | tf_op jit(solution)/shard_map/ppermute | solution.py:288
  17.2 0.9 %copy-start = (f32[1,2,16,1024]{3,2,1,0:T(8,128)S(1)}, f32[1,2,16,1024]{3,2,1,0:T(8,128)}, u32[]{:S(2)}) copy-start(f32[1,2,16,1024]{3,2,1,0:T(8,128)} %param.6) | copy-start | bytes 393220
  17.2 1.8 %copy-start.1 = (f32[1,2,16,1024]{3,2,1,0:T(8,128)S(1)}, f32[1,2,16,1024]{3,2,1,0:T(8,128)}, u32[]{:S(2)}) copy-start(f32[1,2,16,1024]{3,2,1,0:T(8,128)} %param.7) | copy-start | bytes 393220
  23.9 1.3 %collective-permute-start.7 = (f32[128,128]{1,0:T(8,128)S(1)}, f32[128,128]{1,0:T(8,128)S(1)}, u32[]{:S(2)}, u32[]{:S(2)}) collective-permute-start(f32[128,128]{1,0:T(8,128)S(1)} %get-tuple-element.22), channel_id=1, source_target_pairs={{0,2},{2,0},{4,6},{6,4},{8,10},{10,8},{12,14},{14,12},{16,18},{18,... | collective-permute-start | bytes 196616 | tf_op jit(solution)/shard_map/ppermute | solution.py:288
  25.2 3.4 %collective-permute-start.8 = (f32[4,16,128]{2,1,0:T(8,128)S(1)}, f32[4,16,128]{2,1,0:T(8,128)S(1)}, u32[]{:S(2)}, u32[]{:S(2)}) collective-permute-start(f32[4,16,128]{2,1,0:T(8,128)S(1)} %get-tuple-element.24), channel_id=1, source_target_pairs={{0,6},{2,4},{4,2},{6,0},{8,14},{10,12},{12,10},{14,8},{16,22},{18,... | collective-permute-start | bytes 98312 | tf_op jit(solution)/shard_map/ppermute | solution.py:288
  28.6 3.2 %collective-permute-start.9 = (f32[2,16,128]{2,1,0:T(8,128)S(1)}, f32[2,16,128]{2,1,0:T(8,128)S(1)}, u32[]{:S(2)}, u32[]{:S(2)}) collective-permute-start(f32[2,16,128]{2,1,0:T(8,128)S(1)} %get-tuple-element.26), channel_id=1, source_target_pairs={{0,10},{2,8},{4,14},{6,12},{8,2},{10,0},{12,6},{14,4},{16,26},{18,... | collective-permute-start | bytes 49160 | tf_op jit(solution)/shard_map/ppermute | solution.py:288
  31.8 4.0 %collective-permute-start.10 = (f32[1,16,128]{2,1,0:T(8,128)S(1)}, f32[1,16,128]{2,1,0:T(8,128)S(1)}, u32[]{:S(2)}, u32[]{:S(2)}) collective-permute-start(f32[1,16,128]{2,1,0:T(8,128)S(1)} %get-tuple-element.28), channel_id=1, source_target_pairs={{0,18},{2,16},{4,22},{6,20},{8,26},{10,24},{12,30},{14,28},{16,2},... | collective-permute-start | bytes 24584 | tf_op jit(solution)/shard_map/ppermute | solution.py:288

commit v4 on v3

--- a/solution.py
+++ b/solution.py
@@ -41,7 +41,7 @@
         propagating = excess >= 0
         real_part = jnp.where(propagating, larger, smaller)
         imag_part = jnp.where(propagating, smaller, larger)
-        attenuation = jnp.exp(imag_part * -math.sqrt(0.5))
+        attenuation = jnp.exp2(imag_part * (-math.sqrt(0.5) / math.log(2.0)))
         sine = real_part * horner(SINE, real_part * real_part)
         sine_square = sine * sine
         rest = 2.0 - sine_square
@@ -173,7 +173,7 @@
 
 def main_kernel(setup, coef_ref, src_levels, rec_levels, *refs):
     rows, halo, depth_steps, two, packed, width = setup
-    image_refs, (src_ref, rec_ref, levels) = refs[:-3], refs[-3:]
+    image_refs, (final_ref, levels) = refs[:-2], refs[-2:]
     tiles = levels.shape[3]
     flip = lax.axis_index("lat")
     lane = lax.broadcasted_iota(jnp.int32, (tiles, LANES), 1)
@@ -241,11 +241,8 @@
                 for field in range(4):
                     levels[0, field, row - next_lowest] = outs[field]
             else:
-                at = pl.ds(own_start(row), tiles, stride=SUBLANES)
-                src_ref[0, at, :] = outs[0]
-                src_ref[1, at, :] = outs[1]
-                rec_ref[0, at, :] = outs[2]
-                rec_ref[1, at, :] = -outs[3]
+                for field in range(4):
+                    final_ref[field, row] = outs[field]
             if not 0 <= row < rows:
                 continue
             value = outs[0] * outs[2] - outs[1] * outs[3]
@@ -262,6 +259,20 @@
         images.append(row_images)
 
 
+def finish_kernel(two, final_ref, src_ref, rec_ref):
+    _, rows, tiles, _ = final_ref.shape
+    flip = lax.axis_index("lat")
+    for row in range(rows):
+        start = strided(row, tiles)
+        if two:
+            start = either(flip, start, strided(rows - 1 - row, tiles))
+        at = pl.ds(start, tiles, stride=SUBLANES)
+        src_ref[0, at, :] = final_ref[0, row]
+        src_ref[1, at, :] = final_ref[1, row]
+        rec_ref[0, at, :] = final_ref[2, row]
+        rec_ref[1, at, :] = -final_ref[3, row]
+
+
 def tiled(block):
     parts, rows, columns = block.shape
     split = block.reshape(parts, rows // SUBLANES, SUBLANES, columns // LANES, LANES)
@@ -366,17 +377,21 @@
         shape = (rows, 2 * block.shape[1])
         block = call(functools.partial(beside_kernel, b), shape, block, other, cost_estimate=COST)
     block = block[None]
-    parts = []
-    for at, b in enumerate(outer):
-        other = partner(block, (1 << b) | (1 if inner else 0))
-        if at == len(outer) - 2:
-            parts.append((block, ((b, False), (outer[-1], False))))
-            parts.append((other, ((b, True), (outer[-1], False))))
-        if b == outer[-1]:
-            parts.append((other, ((b, True),)))
-            return parts
+    cross = 1 if inner else 0
+    for b in outer[:-2]:
+        other = partner(block, (1 << b) | cross)
         shape = (2 * block.shape[0], *block.shape[1:])
         block = call(functools.partial(stack_kernel, b), shape, block, other, cost_estimate=COST)
+    high, low = outer[-2:]
+    other = partner(block, (1 << high) | cross)
+    near = partner(block, (1 << low) | cross)
+    far = partner(other, (1 << low) | cross)
+    return [
+        (block, ((high, False), (low, False))),
+        (other, ((high, True), (low, False))),
+        (near, ((high, False), (low, True))),
+        (far, ((high, True), (low, True))),
+    ]
 
 
 def halve_kernel(bit, held, came, keep, send):
@@ -466,15 +481,17 @@
     field_shape = (2, rows * tiles, LANES)
     image_shapes = [image_shape] * (2 if packed else 1)
     setup = (rows, halo, depth_steps, two, packed, width)
-    *image, src, rec = call(
+    *image, final = call(
         functools.partial(main_kernel, setup),
-        [*image_shapes, field_shape, field_shape],
+        [*image_shapes, (4, rows, tiles, LANES)],
         coefs[0],
         src_levels,
         rec_levels,
         mib=16,
         scratch_shapes=[pltpu.VMEM((TERMS, 4, later_span, tiles, LANES), jnp.float32)],
     )
+
+    src, rec = call(functools.partial(finish_kernel, two), [field_shape] * 2, final, mib=4, cost_estimate=COST)
 
     if packed:
         depth_image = scatter_sum(*image, rows, norm_factor, (depth_steps, rows, width))

time: 36.7 us -> 37.4 us (1.019)
  starting transfers between devices: 15.7 us -> 18.1 us
  waiting for transfers between devices: 10.5 us -> 8.81 us
    ppermute x8 -> x9, starting transfers between devices: 10.8 us -> 13.5 us  [partner(): lax.ppermute(block, 'freq', [(i, i ^ mask) for i in range(lax.axis_size('...]
    ppermute x8 -> x9, waiting for transfers between devices: 9.59 us -> 7.64 us  [partner(): lax.ppermute(block, 'freq', [(i, i ^ mask) for i in range(lax.axis_size('...]
    pallas_call x14 -> x15, Pallas kernels: 7.81 us -> 7.87 us  [call(): pl.pallas_call(kernel, out_shape=outs[0] if single else outs, out_specs=V...]
  transfers between devices with their start and end apart: 11 -> 12, of which waited for: 8 -> 7; matrix products, arithmetic and copies ran while one was open for 2% -> 2% of each run, Pallas kernels for 8% -> 11%
where the time goes in v4:
time: 37.4 us; the launch traced here: 37.1 us
  starting transfers between devices  18.1 us (48%)
  waiting for transfers between devices  8.81 us (24%)
  Pallas kernels  7.87 us (21%)
  between operations  1.4 us (4%)
  local copies, waits for them, and re-layouts  0.96 us (3%)
    ppermute x9, starting transfers between devices, partner(): lax.ppermute(block, 'freq', [(i, i ^ mask) for i in range(lax.axis_size('...  13.5 us
    pallas_call x15, Pallas kernels, call(): pl.pallas_call(kernel, out_shape=outs[0] if single else outs, out_specs=V...  7.87 us
    ppermute x9, waiting for transfers between devices, partner(): lax.ppermute(block, 'freq', [(i, i ^ mask) for i in range(lax.axis_size('...  7.64 us
    ppermute x3, starting transfers between devices, from_sides(): return [lax.ppermute(block, 'lat', [(0, 1), (1, 0)])]  4.61 us
    ppermute x3, waiting for transfers between devices, from_sides(): return [lax.ppermute(block, 'lat', [(0, 1), (1, 0)])]  1.17 us
  transfers between devices with their start and end apart: 12, of which 7 were waited for; matrix products, arithmetic and copies ran while one was open for 2% of the time, Pallas kernels for 11%

profile of v4, /device:TPU:0, one launch (start us, length us, event | category | flops | bytes accessed | tf_op | source)
XLA Modules:
  0.0 37.1 jit_solution(9022335713433857943)
XLA Ops:
  0.6 0.6 %collective-permute-start = (f32[2,16,64]{2,1,0:T(8,128)}, f32[2,16,64]{2,1,0:T(8,128)S(1)}, u32[]{:S(2)}, u32[]{:S(2)}) collective-permute-start(f32[2,16,64]{2,1,0:T(8,128)} %param.5), channel_id=1, source_target_pairs={{0,2},{2,0},{4,6},{6,4},{8,10},{10,8},{12,14},{14,12},{16,18},{18,... | collective-permute-start | bytes 24584 | tf_op jit(solution)/shard_map/ppermute | solution.py:299
  1.2 2.6 %collective-permute-start.6 = (f32[1,2,16,1024]{3,2,1,0:T(8,128)}, f32[1,2,16,1024]{3,2,1,0:T(8,128)S(1)}, u32[]{:S(2)}, u32[]{:S(2)}) collective-permute-start(f32[1,2,16,1024]{3,2,1,0:T(8,128)} %param.6), channel_id=1, source_target_pairs={{0,1},{1,0},{2,3},{3,2},{4,5},{5,4},{6,7},{7,6},{8,9},{9,8},{10,11... | collective-permute-start | bytes 393224 | tf_op jit(solution)/shard_map/ppermute | solution.py:292
  3.8 0.7 %slice_bitcast_fusion = (f32[16,64]{1,0:T(8,128)S(1)}, f32[16,64]{1,0:T(8,128)S(1)}) fusion(f32[2,16,64]{2,1,0:T(8,128)} %param.5), kind=kLoop, calls=%fused_computation | loop fusion | bytes 16384 | tf_op jit(solution)/shard_map/squeeze | solution.py:440
  4.5 0.1 shard_map.70
  4.6 0.6 %collective-permute-start.1 = (f32[8,128]{1,0:T(8,128)S(1)}, f32[8,128]{1,0:T(8,128)S(1)}, u32[]{:S(2)}, u32[]{:S(2)}) collective-permute-start(f32[8,128]{1,0:T(8,128)S(1)} %get-tuple-element.19), channel_id=1, source_target_pairs={{0,1},{1,0},{2,3},{3,2},{4,5},{5,4},{6,7},{7,6},{8,9},{9,8},{10,11... | collective-permute-start | bytes 12296 | tf_op jit(solution)/shard_map/ppermute | solution.py:292
  5.2 1.4 %collective-permute-start.7 = (f32[1,2,16,1024]{3,2,1,0:T(8,128)}, f32[1,2,16,1024]{3,2,1,0:T(8,128)S(1)}, u32[]{:S(2)}, u32[]{:S(2)}) collective-permute-start(f32[1,2,16,1024]{3,2,1,0:T(8,128)} %param.7), channel_id=1, source_target_pairs={{0,1},{1,0},{2,3},{3,2},{4,5},{5,4},{6,7},{7,6},{8,9},{9,8},{10,11... | collective-permute-start | bytes 393224 | tf_op jit(solution)/shard_map/ppermute | solution.py:292
  7.2 1.2 %collective-permute-done.1.edge = f32[8,128]{1,0:T(8,128)S(1)} collective-permute-done((f32[8,128]{1,0:T(8,128)S(1)}, f32[8,128]{1,0:T(8,128)S(1)}, u32[]{:S(2)}, u32[]{:S(2)}) %collective-permute-start.1) | collective-permute-done | bytes 4128 | tf_op jit(solution)/shard_map/ppermute | solution.py:292
  8.4 1.7 %collective-permute-start.2 = (f32[1,40,128]{2,1,0:T(8,128)S(1)}, f32[1,40,128]{2,1,0:T(8,128)S(1)}, u32[]{:S(2)}, u32[]{:S(2)}) collective-permute-start(f32[1,40,128]{2,1,0:T(8,128)S(1)} %bitcast.45), channel_id=1, source_target_pairs={{0,18},{2,16},{4,22},{6,20},{8,26},{10,24},{12,30},{14,28},{16,2},... | collective-permute-start | bytes 61448 | tf_op jit(solution)/shard_map/ppermute | solution.py:299
  10.2 2.4 %collective-permute-done.2.other = f32[1,40,128]{2,1,0:T(8,128)S(1)} collective-permute-done((f32[1,40,128]{2,1,0:T(8,128)S(1)}, f32[1,40,128]{2,1,0:T(8,128)S(1)}, u32[]{:S(2)}, u32[]{:S(2)}) %collective-permute-start.2) | collective-permute-done | bytes 20512 | tf_op jit(solution)/shard_map/ppermute | solution.py:299
  12.5 1.8 %collective-permute-start.3 = (f32[2,40,128]{2,1,0:T(8,128)S(1)}, f32[2,40,128]{2,1,0:T(8,128)S(1)}, u32[]{:S(2)}, u32[]{:S(2)}) collective-permute-start(f32[2,40,128]{2,1,0:T(8,128)S(1)} %shard_map.72.refs_1_), channel_id=1, source_target_pairs={{0,10},{2,8},{4,14},{6,12},{8,2},{10,0},{12,6},{14,4},{16,26},{18,... | collective-permute-start | bytes 122888 | tf_op jit(solution)/shard_map/ppermute | solution.py:299
  14.3 1.5 %collective-permute-start.5 = (f32[2,40,128]{2,1,0:T(8,128)S(1)}, f32[2,40,128]{2,1,0:T(8,128)S(1)}, u32[]{:S(2)}, u32[]{:S(2)}) collective-permute-start(f32[2,40,128]{2,1,0:T(8,128)S(1)} %shard_map.72.refs_1_), channel_id=1, source_target_pairs={{0,6},{2,4},{4,2},{6,0},{8,14},{10,12},{12,10},{14,8},{16,22},{18,... | collective-permute-start | bytes 122888 | tf_op jit(solution)/shard_map/ppermute | solution.py:299
  15.8 0.2 collective-permute-done.3.refs_1_
  16.0 1.8 %collective-permute-start.4 = (f32[2,40,128]{2,1,0:T(8,128)S(1)}, f32[2,40,128]{2,1,0:T(8,128)S(1)}, u32[]{:S(2)}, u32[]{:S(2)}) collective-permute-start(f32[2,40,128]{2,1,0:T(8,128)S(1)} %collective-permute-done.3.refs_1_), channel_id=1, source_target_pairs={{0,6},{2,4},{4,2},{6,0},{8,14},{10,12},{12,10},{14,8},{16,22},{18,... | collective-permute-start | bytes 122888 | tf_op jit(solution)/shard_map/ppermute | solution.py:299
  17.8 0.6 %shard_map.73.refs_2_ = f32[8,2,320,128]{3,2,1,0:T(8,128)S(1)} custom-call(f32[8,128]{1,0:T(8,128)S(1)} %get-tuple-element.20.refs_0_, f32[2,40,128]{2,1,0:T(8,128)S(1)} %shard_map.72.refs_1_), custom_call_target="tpu_custom_call" | custom-call | flops 67108864 | bytes 4194304 | tf_op jit(solution)/shard_map/pallas_call | solution.py:310
  18.4 0.6 %shard_map.74.refs_2_ = f32[8,2,320,128]{3,2,1,0:T(8,128)S(1)} custom-call(f32[8,128]{1,0:T(8,128)S(1)} %get-tuple-element.20.refs_0_, f32[2,40,128]{2,1,0:T(8,128)S(1)} %collective-permute-done.3.refs_1_, f32[8,2,320,128]{3,2,1,0:T(8,128)S(1)} %shard_map.73.refs_2_), custom_call_target="tpu_custom_call", output_to_operand_aliasing={{}: (2, {})} | custom-call | flops 67108864 | bytes 4194304 | tf_op jit(solution)/shard_map/pallas_call | solution.py:310
  19.1 0.6 %shard_map.75.refs_2_ = f32[8,2,320,128]{3,2,1,0:T(8,128)S(1)} custom-call(f32[8,128]{1,0:T(8,128)S(1)} %get-tuple-element.20.refs_0_, f32[2,40,128]{2,1,0:T(8,128)S(1)} %collective-permute-done.5.refs_1_, f32[8,2,320,128]{3,2,1,0:T(8,128)S(1)} %shard_map.74.refs_2_), custom_call_target="tpu_custom_call", output_to_operand_aliasing={{}: (2, {})} | custom-call | flops 67108864 | bytes 4194304 | tf_op jit(solution)/shard_map/pallas_call | solution.py:310
  19.7 0.0 copy-start.1
  19.7 0.6 %shard_map.76.coef_ref = f32[8,2,320,128]{3,2,1,0:T(8,128)S(1)} custom-call(f32[8,128]{1,0:T(8,128)S(1)} %get-tuple-element.20.refs_0_, f32[2,40,128]{2,1,0:T(8,128)S(1)} %collective-permute-done.4.refs_1_, f32[8,2,320,128]{3,2,1,0:T(8,128)S(1)} %shard_map.75.refs_2_), custom_call_target="tpu_custom_call", output_to_operand_aliasing={{}: (2, {})} | custom-call | flops 67108864 | bytes 4194304 | tf_op jit(solution)/shard_map/pallas_call | solution.py:310
  20.4 0.2 copy-done
  20.6 0.9 %shard_map.77.src_levels = f32[8,2,30,8,128]{4,3,2,1,0:T(8,128)S(1)} custom-call(f32[2,128,128]{2,1,0:T(8,128)S(1)} %bitcast.39, f32[2,128,128]{2,1,0:T(8,128)S(1)} %bitcast.41), custom_call_target="tpu_custom_call" | custom-call | flops 67108864 | bytes 4194304 | tf_op jit(solution)/shard_map/pallas_call | solution.py:310
  21.5 0.9 %shard_map.78.rec_levels = f32[8,2,30,8,128]{4,3,2,1,0:T(8,128)S(1)} custom-call(f32[2,128,128]{2,1,0:T(8,128)S(1)} %bitcast.40, f32[2,128,128]{2,1,0:T(8,128)S(1)} %bitcast.42), custom_call_target="tpu_custom_call" | custom-call | flops 67108864 | bytes 4194304 | tf_op jit(solution)/shard_map/pallas_call | solution.py:310
  22.4 2.1 %shard_map.79 = (f32[128,128]{1,0:T(8,128)S(1)}, f32[128,128]{1,0:T(8,128)S(1)}, f32[4,16,8,128]{3,2,1,0:T(8,128)S(1)}) custom-call(f32[8,2,320,128]{3,2,1,0:T(8,128)S(1)} %shard_map.76.coef_ref, f32[8,2,30,8,128]{4,3,2,1,0:T(8,128)S(1)} %shard_map.77.src_levels, f32[8,2,30,8,128]{4,3,2,1,0:T(8,128)S(1)} %shard_map.78.rec_levels), custom_call_target="tpu_custom_call" | custom-call | tf_op jit(solution)/shard_map/pallas_call | solution.py:310
  24.5 0.4 %collective-permute-start.8 = (f32[128,128]{1,0:T(8,128)S(1)}, f32[128,128]{1,0:T(8,128)S(1)}, u32[]{:S(2)}, u32[]{:S(2)}) collective-permute-start(f32[128,128]{1,0:T(8,128)S(1)} %get-tuple-element.23), channel_id=1, source_target_pairs={{0,2},{2,0},{4,6},{6,4},{8,10},{10,8},{12,14},{14,12},{16,18},{18,... | collective-permute-start | bytes 196616 | tf_op jit(solution)/shard_map/ppermute | solution.py:299
  24.9 0.9 %collective-permute-done.8 = f32[128,128]{1,0:T(8,128)S(1)} collective-permute-done((f32[128,128]{1,0:T(8,128)S(1)}, f32[128,128]{1,0:T(8,128)S(1)}, u32[]{:S(2)}, u32[]{:S(2)}) %collective-permute-start.8) | collective-permute-done | bytes 65568 | tf_op jit(solution)/shard_map/ppermute | solution.py:299
  25.9 1.5 %collective-permute-start.9 = (f32[4,16,128]{2,1,0:T(8,128)S(1)}, f32[4,16,128]{2,1,0:T(8,128)S(1)}, u32[]{:S(2)}, u32[]{:S(2)}) collective-permute-start(f32[4,16,128]{2,1,0:T(8,128)S(1)} %get-tuple-element.25), channel_id=1, source_target_pairs={{0,6},{2,4},{4,2},{6,0},{8,14},{10,12},{12,10},{14,8},{16,22},{18,... | collective-permute-start | bytes 98312 | tf_op jit(solution)/shard_map/ppermute | solution.py:299
  27.4 1.9 %collective-permute-done.9.came = f32[4,16,128]{2,1,0:T(8,128)S(1)} collective-permute-done((f32[4,16,128]{2,1,0:T(8,128)S(1)}, f32[4,16,128]{2,1,0:T(8,128)S(1)}, u32[]{:S(2)}, u32[]{:S(2)}) %collective-permute-start.9) | collective-permute-done | bytes 32800 | tf_op jit(solution)/shard_map/ppermute | solution.py:299
  29.3 1.5 %collective-permute-start.10 = (f32[2,16,128]{2,1,0:T(8,128)S(1)}, f32[2,16,128]{2,1,0:T(8,128)S(1)}, u32[]{:S(2)}, u32[]{:S(2)}) collective-permute-start(f32[2,16,128]{2,1,0:T(8,128)S(1)} %get-tuple-element.27), channel_id=1, source_target_pairs={{0,10},{2,8},{4,14},{6,12},{8,2},{10,0},{12,6},{14,4},{16,26},{18,... | collective-permute-start | bytes 49160 | tf_op jit(solution)/shard_map/ppermute | solution.py:299
  30.8 1.6 %collective-permute-done.10.came = f32[2,16,128]{2,1,0:T(8,128)S(1)} collective-permute-done((f32[2,16,128]{2,1,0:T(8,128)S(1)}, f32[2,16,128]{2,1,0:T(8,128)S(1)}, u32[]{:S(2)}, u32[]{:S(2)}) %collective-permute-start.10) | collective-permute-done | bytes 16416 | tf_op jit(solution)/shard_map/ppermute | solution.py:299
  32.4 2.6 %collective-permute-start.11 = (f32[1,16,128]{2,1,0:T(8,128)S(1)}, f32[1,16,128]{2,1,0:T(8,128)S(1)}, u32[]{:S(2)}, u32[]{:S(2)}) collective-permute-start(f32[1,16,128]{2,1,0:T(8,128)S(1)} %get-tuple-element.29), channel_id=1, source_target_pairs={{0,18},{2,16},{4,22},{6,20},{8,26},{10,24},{12,30},{14,28},{16,2},... | collective-permute-start | bytes 24584 | tf_op jit(solution)/shard_map/ppermute | solution.py:299
  35.1 0.7 %shard_map.84 = (f32[2,128,128]{2,1,0:T(8,128)}, f32[2,128,128]{2,1,0:T(8,128)}) custom-call(f32[4,16,8,128]{3,2,1,0:T(8,128)S(1)} %get-tuple-element.30.final_ref), custom_call_target="tpu_custom_call" | custom-call | flops 67108864 | bytes 4194304 | tf_op jit(solution)/shard_map/pallas_call | solution.py:310
  35.8 0.6 %collective-permute-done.11.came = f32[1,16,128]{2,1,0:T(8,128)S(1)} collective-permute-done((f32[1,16,128]{2,1,0:T(8,128)S(1)}, f32[1,16,128]{2,1,0:T(8,128)S(1)}, u32[]{:S(2)}, u32[]{:S(2)}) %collective-permute-start.11) | collective-permute-done | bytes 8224 | tf_op jit(solution)/shard_map/ppermute | solution.py:299
  36.4 0.7 %shard_map.83 = f32[2,16,64]{2,1,0:T(8,128)} custom-call(f32[1,16,128]{2,1,0:T(8,128)S(1)} %get-tuple-element.28.held, f32[1,16,128]{2,1,0:T(8,128)S(1)} %collective-permute-done.11.came), custom_call_target="tpu_custom_call" | custom-call | tf_op jit(solution)/shard_map/pallas_call | solution.py:310
  (13 shorter events, 0.1 us)
Async XLA Ops:
  0.6 3.9 %collective-permute-start = (f32[2,16,64]{2,1,0:T(8,128)}, f32[2,16,64]{2,1,0:T(8,128)S(1)}, u32[]{:S(2)}, u32[]{:S(2)}) collective-permute-start(f32[2,16,64]{2,1,0:T(8,128)} %param.5), channel_id=1, source_target_pairs={{0,2},{2,0},{4,6},{6,4},{8,10},{10,8},{12,14},{14,12},{16,18},{18,... | collective-permute-start | bytes 24584 | tf_op jit(solution)/shard_map/ppermute | solution.py:299
  1.2 19.2 %collective-permute-start.6 = (f32[1,2,16,1024]{3,2,1,0:T(8,128)}, f32[1,2,16,1024]{3,2,1,0:T(8,128)S(1)}, u32[]{:S(2)}, u32[]{:S(2)}) collective-permute-start(f32[1,2,16,1024]{3,2,1,0:T(8,128)} %param.6), channel_id=1, source_target_pairs={{0,1},{1,0},{2,3},{3,2},{4,5},{5,4},{6,7},{7,6},{8,9},{9,8},{10,11... | collective-permute-start | bytes 393224 | tf_op jit(solution)/shard_map/ppermute | solution.py:292
  4.6 3.8 %collective-permute-start.1 = (f32[8,128]{1,0:T(8,128)S(1)}, f32[8,128]{1,0:T(8,128)S(1)}, u32[]{:S(2)}, u32[]{:S(2)}) collective-permute-start(f32[8,128]{1,0:T(8,128)S(1)} %get-tuple-element.19), channel_id=1, source_target_pairs={{0,1},{1,0},{2,3},{3,2},{4,5},{5,4},{6,7},{7,6},{8,9},{9,8},{10,11... | collective-permute-start | bytes 12296 | tf_op jit(solution)/shard_map/ppermute | solution.py:292
  5.2 16.3 %collective-permute-start.7 = (f32[1,2,16,1024]{3,2,1,0:T(8,128)}, f32[1,2,16,1024]{3,2,1,0:T(8,128)S(1)}, u32[]{:S(2)}, u32[]{:S(2)}) collective-permute-start(f32[1,2,16,1024]{3,2,1,0:T(8,128)} %param.7), channel_id=1, source_target_pairs={{0,1},{1,0},{2,3},{3,2},{4,5},{5,4},{6,7},{7,6},{8,9},{9,8},{10,11... | collective-permute-start | bytes 393224 | tf_op jit(solution)/shard_map/ppermute | solution.py:292
  8.4 4.1 %collective-permute-start.2 = (f32[1,40,128]{2,1,0:T(8,128)S(1)}, f32[1,40,128]{2,1,0:T(8,128)S(1)}, u32[]{:S(2)}, u32[]{:S(2)}) collective-permute-start(f32[1,40,128]{2,1,0:T(8,128)S(1)} %bitcast.45), channel_id=1, source_target_pairs={{0,18},{2,16},{4,22},{6,20},{8,26},{10,24},{12,30},{14,28},{16,2},... | collective-permute-start | bytes 61448 | tf_op jit(solution)/shard_map/ppermute | solution.py:299
  12.5 3.5 %collective-permute-start.3 = (f32[2,40,128]{2,1,0:T(8,128)S(1)}, f32[2,40,128]{2,1,0:T(8,128)S(1)}, u32[]{:S(2)}, u32[]{:S(2)}) collective-permute-start(f32[2,40,128]{2,1,0:T(8,128)S(1)} %shard_map.72.refs_1_), channel_id=1, source_target_pairs={{0,10},{2,8},{4,14},{6,12},{8,2},{10,0},{12,6},{14,4},{16,26},{18,... | collective-permute-start | bytes 122888 | tf_op jit(solution)/shard_map/ppermute | solution.py:299
  14.3 4.7 %collective-permute-start.5 = (f32[2,40,128]{2,1,0:T(8,128)S(1)}, f32[2,40,128]{2,1,0:T(8,128)S(1)}, u32[]{:S(2)}, u32[]{:S(2)}) collective-permute-start(f32[2,40,128]{2,1,0:T(8,128)S(1)} %shard_map.72.refs_1_), channel_id=1, source_target_pairs={{0,6},{2,4},{4,2},{6,0},{8,14},{10,12},{12,10},{14,8},{16,22},{18,... | collective-permute-start | bytes 122888 | tf_op jit(solution)/shard_map/ppermute | solution.py:299
  16.0 3.7 %collective-permute-start.4 = (f32[2,40,128]{2,1,0:T(8,128)S(1)}, f32[2,40,128]{2,1,0:T(8,128)S(1)}, u32[]{:S(2)}, u32[]{:S(2)}) collective-permute-start(f32[2,40,128]{2,1,0:T(8,128)S(1)} %collective-permute-done.3.refs_1_), channel_id=1, source_target_pairs={{0,6},{2,4},{4,2},{6,0},{8,14},{10,12},{12,10},{14,8},{16,22},{18,... | collective-permute-start | bytes 122888 | tf_op jit(solution)/shard_map/ppermute | solution.py:299
  19.7 0.9 %copy-start = (f32[1,2,16,1024]{3,2,1,0:T(8,128)S(1)}, f32[1,2,16,1024]{3,2,1,0:T(8,128)}, u32[]{:S(2)}) copy-start(f32[1,2,16,1024]{3,2,1,0:T(8,128)} %param.6) | copy-start | bytes 393220
  19.7 1.8 %copy-start.1 = (f32[1,2,16,1024]{3,2,1,0:T(8,128)S(1)}, f32[1,2,16,1024]{3,2,1,0:T(8,128)}, u32[]{:S(2)}) copy-start(f32[1,2,16,1024]{3,2,1,0:T(8,128)} %param.7) | copy-start | bytes 393220
  24.5 1.3 %collective-permute-start.8 = (f32[128,128]{1,0:T(8,128)S(1)}, f32[128,128]{1,0:T(8,128)S(1)}, u32[]{:S(2)}, u32[]{:S(2)}) collective-permute-start(f32[128,128]{1,0:T(8,128)S(1)} %get-tuple-element.23), channel_id=1, source_target_pairs={{0,2},{2,0},{4,6},{6,4},{8,10},{10,8},{12,14},{14,12},{16,18},{18,... | collective-permute-start | bytes 196616 | tf_op jit(solution)/shard_map/ppermute | solution.py:299
  25.9 3.4 %collective-permute-start.9 = (f32[4,16,128]{2,1,0:T(8,128)S(1)}, f32[4,16,128]{2,1,0:T(8,128)S(1)}, u32[]{:S(2)}, u32[]{:S(2)}) collective-permute-start(f32[4,16,128]{2,1,0:T(8,128)S(1)} %get-tuple-element.25), channel_id=1, source_target_pairs={{0,6},{2,4},{4,2},{6,0},{8,14},{10,12},{12,10},{14,8},{16,22},{18,... | collective-permute-start | bytes 98312 | tf_op jit(solution)/shard_map/ppermute | solution.py:299
  29.3 3.2 %collective-permute-start.10 = (f32[2,16,128]{2,1,0:T(8,128)S(1)}, f32[2,16,128]{2,1,0:T(8,128)S(1)}, u32[]{:S(2)}, u32[]{:S(2)}) collective-permute-start(f32[2,16,128]{2,1,0:T(8,128)S(1)} %get-tuple-element.27), channel_id=1, source_target_pairs={{0,10},{2,8},{4,14},{6,12},{8,2},{10,0},{12,6},{14,4},{16,26},{18,... | collective-permute-start | bytes 49160 | tf_op jit(solution)/shard_map/ppermute | solution.py:299
  32.4 4.0 %collective-permute-start.11 = (f32[1,16,128]{2,1,0:T(8,128)S(1)}, f32[1,16,128]{2,1,0:T(8,128)S(1)}, u32[]{:S(2)}, u32[]{:S(2)}) collective-permute-start(f32[1,16,128]{2,1,0:T(8,128)S(1)} %get-tuple-element.29), channel_id=1, source_target_pairs={{0,18},{2,16},{4,22},{6,20},{8,26},{10,24},{12,30},{14,28},{16,2},... | collective-permute-start | bytes 24584 | tf_op jit(solution)/shard_map/ppermute | solution.py:299

commit v5 on v4

--- a/solution.py
+++ b/solution.py
@@ -154,9 +154,10 @@
     freq_ref, slow_ref, out_ref = refs[0], refs[1], refs[-1]
     count, rows, _ = slow_ref.shape
     slot = 0
+    core = lax.axis_index("freq") & 1
     for bit, other in shared:
-        own = (lax.axis_index("freq") >> bit) & 1
-        slot = 2 * slot + (1 - own if other else own)
+        change = {-1: core, -2: 1 - core}.get(other, other)
+        slot = 2 * slot + (((lax.axis_index("freq") >> bit) & 1) ^ change)
     freq = freq_ref[...]
 
     def body(piece, carry):
@@ -358,6 +359,10 @@
     out[...] = jnp.concatenate([jnp.where(upper, second, first), jnp.where(upper, first, second)], axis=1)
 
 
+def pick_kernel(first, second, out):
+    out[...] = jnp.where((lax.axis_index("freq") & 1) != 0, second[...], first[...])
+
+
 def stack_kernel(bit, mine, other, out):
     slot = (lax.axis_index("freq") >> bit) & 1
     for piece in range(mine.shape[0]):
@@ -384,14 +389,14 @@
         block = call(functools.partial(stack_kernel, b), shape, block, other, cost_estimate=COST)
     high, low = outer[-2:]
     other = partner(block, (1 << high) | cross)
-    near = partner(block, (1 << low) | cross)
-    far = partner(other, (1 << low) | cross)
-    return [
-        (block, ((high, False), (low, False))),
-        (other, ((high, True), (low, False))),
-        (near, ((high, False), (low, True))),
-        (far, ((high, True), (low, True))),
-    ]
+    mine = [(block, ((high, 0), (low, 0))), (other, ((high, 1), (low, 0)))]
+    if not cross:
+        theirs = [partner(part, 1 << low) for part in (block, other)]
+        return mine + [(theirs[0], ((high, 0), (low, 1))), (theirs[1], ((high, 1), (low, 1)))]
+    piece = call(pick_kernel, block.shape, block, other, cost_estimate=COST)
+    near = partner(piece, (1 << low) | 1)
+    far = partner(near, 1)
+    return mine + [(near, ((high, -2), (low, 1))), (far, ((high, -1), (low, 1)))]
 
 
 def halve_kernel(bit, held, came, keep, send):

time: 37.4 us -> 38.3 us (1.024)
  waiting for transfers between devices: 8.81 us -> 10.7 us
  starting transfers between devices: 18.1 us -> 17.1 us
    ppermute x9, waiting for transfers between devices: 7.64 us -> 9.73 us  [partner(): lax.ppermute(block, 'freq', [(i, i ^ mask) for i in range(lax.axis_size('...]
    ppermute x9, starting transfers between devices: 13.5 us -> 12.2 us  [partner(): lax.ppermute(block, 'freq', [(i, i ^ mask) for i in range(lax.axis_size('...]
    pallas_call x15 -> x16, Pallas kernels: 7.87 us -> 7.88 us  [call(): pl.pallas_call(kernel, out_shape=outs[0] if single else outs, out_specs=V...]
  transfers between devices with their start and end apart: 12 -> 12, of which waited for: 7 -> 9; matrix products, arithmetic and copies ran while one was open for 2% -> 2% of each run, Pallas kernels for 11% -> 11%
where the time goes in v5:
time: 38.3 us; the launch traced here: 38 us
  starting transfers between devices  17.1 us (45%)
  waiting for transfers between devices  10.7 us (28%)
  Pallas kernels  7.88 us (21%)
  between operations  1.4 us (4%)
  local copies, waits for them, and re-layouts  0.97 us (3%)
    ppermute x9, starting transfers between devices, partner(): lax.ppermute(block, 'freq', [(i, i ^ mask) for i in range(lax.axis_size('...  12.2 us
    ppermute x9, waiting for transfers between devices, partner(): lax.ppermute(block, 'freq', [(i, i ^ mask) for i in range(lax.axis_size('...  9.73 us
    pallas_call x16, Pallas kernels, call(): pl.pallas_call(kernel, out_shape=outs[0] if single else outs, out_specs=V...  7.88 us
    ppermute x3, starting transfers between devices, from_sides(): return [lax.ppermute(block, 'lat', [(0, 1), (1, 0)])]  4.87 us
    ppermute x3, waiting for transfers between devices, from_sides(): return [lax.ppermute(block, 'lat', [(0, 1), (1, 0)])]  0.94 us
  transfers between devices with their start and end apart: 12, of which 9 were waited for; matrix products, arithmetic and copies ran while one was open for 2% of the time, Pallas kernels for 11%

profile of v5, /device:TPU:0, one launch (start us, length us, event | category | flops | bytes accessed | tf_op | source)
XLA Modules:
  0.0 38.0 jit_solution(2350096751837998970)
XLA Ops:
  0.6 0.6 %collective-permute-start = (f32[2,16,64]{2,1,0:T(8,128)}, f32[2,16,64]{2,1,0:T(8,128)S(1)}, u32[]{:S(2)}, u32[]{:S(2)}) collective-permute-start(f32[2,16,64]{2,1,0:T(8,128)} %param.5), channel_id=1, source_target_pairs={{0,2},{2,0},{4,6},{6,4},{8,10},{10,8},{12,14},{14,12},{16,18},{18,... | collective-permute-start | bytes 24584 | tf_op jit(solution)/shard_map/ppermute | solution.py:300
  1.2 0.7 %slice_bitcast_fusion = (f32[16,64]{1,0:T(8,128)S(1)}, f32[16,64]{1,0:T(8,128)S(1)}) fusion(f32[2,16,64]{2,1,0:T(8,128)} %param.5), kind=kLoop, calls=%fused_computation | loop fusion | bytes 16384 | tf_op jit(solution)/shard_map/squeeze | solution.py:445
  1.9 0.3 collective-permute-done.refs_2_
  2.2 0.1 shard_map.70
  2.3 2.8 %collective-permute-start.1 = (f32[8,128]{1,0:T(8,128)S(1)}, f32[8,128]{1,0:T(8,128)S(1)}, u32[]{:S(2)}, u32[]{:S(2)}) collective-permute-start(f32[8,128]{1,0:T(8,128)S(1)} %get-tuple-element.19), channel_id=1, source_target_pairs={{0,1},{1,0},{2,3},{3,2},{4,5},{5,4},{6,7},{7,6},{8,9},{9,8},{10,11... | collective-permute-start | bytes 12296 | tf_op jit(solution)/shard_map/ppermute | solution.py:293
  5.8 0.9 %collective-permute-done.1.edge = f32[8,128]{1,0:T(8,128)S(1)} collective-permute-done((f32[8,128]{1,0:T(8,128)S(1)}, f32[8,128]{1,0:T(8,128)S(1)}, u32[]{:S(2)}, u32[]{:S(2)}) %collective-permute-start.1) | collective-permute-done | bytes 4128 | tf_op jit(solution)/shard_map/ppermute | solution.py:293
  6.8 1.7 %collective-permute-start.2 = (f32[1,40,128]{2,1,0:T(8,128)S(1)}, f32[1,40,128]{2,1,0:T(8,128)S(1)}, u32[]{:S(2)}, u32[]{:S(2)}) collective-permute-start(f32[1,40,128]{2,1,0:T(8,128)S(1)} %bitcast.45), channel_id=1, source_target_pairs={{0,18},{2,16},{4,22},{6,20},{8,26},{10,24},{12,30},{14,28},{16,2},... | collective-permute-start | bytes 61448 | tf_op jit(solution)/shard_map/ppermute | solution.py:300
  8.5 1.5 %collective-permute-start.6 = (f32[1,2,16,1024]{3,2,1,0:T(8,128)}, f32[1,2,16,1024]{3,2,1,0:T(8,128)S(1)}, u32[]{:S(2)}, u32[]{:S(2)}) collective-permute-start(f32[1,2,16,1024]{3,2,1,0:T(8,128)} %param.6), channel_id=1, source_target_pairs={{0,1},{1,0},{2,3},{3,2},{4,5},{5,4},{6,7},{7,6},{8,9},{9,8},{10,11... | collective-permute-start | bytes 393224 | tf_op jit(solution)/shard_map/ppermute | solution.py:293
  10.0 0.5 %collective-permute-start.7 = (f32[1,2,16,1024]{3,2,1,0:T(8,128)}, f32[1,2,16,1024]{3,2,1,0:T(8,128)S(1)}, u32[]{:S(2)}, u32[]{:S(2)}) collective-permute-start(f32[1,2,16,1024]{3,2,1,0:T(8,128)} %param.7), channel_id=1, source_target_pairs={{0,1},{1,0},{2,3},{3,2},{4,5},{5,4},{6,7},{7,6},{8,9},{9,8},{10,11... | collective-permute-start | bytes 393224 | tf_op jit(solution)/shard_map/ppermute | solution.py:293
  10.5 0.4 collective-permute-done.2.other
  10.9 1.8 %collective-permute-start.3 = (f32[2,40,128]{2,1,0:T(8,128)S(1)}, f32[2,40,128]{2,1,0:T(8,128)S(1)}, u32[]{:S(2)}, u32[]{:S(2)}) collective-permute-start(f32[2,40,128]{2,1,0:T(8,128)S(1)} %shard_map.72.first.refs_1_), channel_id=1, source_target_pairs={{0,10},{2,8},{4,14},{6,12},{8,2},{10,0},{12,6},{14,4},{16,26},{18,... | collective-permute-start | bytes 122888 | tf_op jit(solution)/shard_map/ppermute | solution.py:300
  12.7 1.7 %collective-permute-done.3.second.refs_1_ = f32[2,40,128]{2,1,0:T(8,128)S(1)} collective-permute-done((f32[2,40,128]{2,1,0:T(8,128)S(1)}, f32[2,40,128]{2,1,0:T(8,128)S(1)}, u32[]{:S(2)}, u32[]{:S(2)}) %collective-permute-start.3) | collective-permute-done | bytes 40992 | tf_op jit(solution)/shard_map/ppermute | solution.py:300
  14.4 2.1 %collective-permute-start.4 = (f32[2,40,128]{2,1,0:T(8,128)S(1)}, f32[2,40,128]{2,1,0:T(8,128)S(1)}, u32[]{:S(2)}, u32[]{:S(2)}) collective-permute-start(f32[2,40,128]{2,1,0:T(8,128)S(1)} %shard_map.73), channel_id=1, source_target_pairs={{0,6},{2,4},{4,2},{6,0},{8,14},{10,12},{12,10},{14,8},{16,22},{18,... | collective-permute-start | bytes 122888 | tf_op jit(solution)/shard_map/ppermute | solution.py:300
  16.5 1.7 %collective-permute-done.4.refs_1_ = f32[2,40,128]{2,1,0:T(8,128)S(1)} collective-permute-done((f32[2,40,128]{2,1,0:T(8,128)S(1)}, f32[2,40,128]{2,1,0:T(8,128)S(1)}, u32[]{:S(2)}, u32[]{:S(2)}) %collective-permute-start.4) | collective-permute-done | bytes 40992 | tf_op jit(solution)/shard_map/ppermute | solution.py:300
  18.2 0.5 %collective-permute-start.5 = (f32[2,40,128]{2,1,0:T(8,128)S(1)}, f32[2,40,128]{2,1,0:T(8,128)S(1)}, u32[]{:S(2)}, u32[]{:S(2)}) collective-permute-start(f32[2,40,128]{2,1,0:T(8,128)S(1)} %collective-permute-done.4.refs_1_), channel_id=1, source_target_pairs={{0,2},{2,0},{4,6},{6,4},{8,10},{10,8},{12,14},{14,12},{16,18},{18,... | collective-permute-start | bytes 122888 | tf_op jit(solution)/shard_map/ppermute | solution.py:300
  18.7 0.6 %shard_map.74.refs_2_ = f32[8,2,320,128]{3,2,1,0:T(8,128)S(1)} custom-call(f32[8,128]{1,0:T(8,128)S(1)} %get-tuple-element.20.refs_0_, f32[2,40,128]{2,1,0:T(8,128)S(1)} %shard_map.72.first.refs_1_), custom_call_target="tpu_custom_call" | custom-call | flops 67108864 | bytes 4194304 | tf_op jit(solution)/shard_map/pallas_call | solution.py:311
  19.4 0.6 %shard_map.75.refs_2_ = f32[8,2,320,128]{3,2,1,0:T(8,128)S(1)} custom-call(f32[8,128]{1,0:T(8,128)S(1)} %get-tuple-element.20.refs_0_, f32[2,40,128]{2,1,0:T(8,128)S(1)} %collective-permute-done.3.second.refs_1_, f32[8,2,320,128]{3,2,1,0:T(8,128)S(1)} %shard_map.74.refs_2_), custom_call_target="tpu_custom_call", output_to_operand_aliasing={{}: (2, {})} | custom-call | flops 67108864 | bytes 4194304 | tf_op jit(solution)/shard_map/pallas_call | solution.py:311
  20.0 0.6 %shard_map.76.refs_2_ = f32[8,2,320,128]{3,2,1,0:T(8,128)S(1)} custom-call(f32[8,128]{1,0:T(8,128)S(1)} %get-tuple-element.20.refs_0_, f32[2,40,128]{2,1,0:T(8,128)S(1)} %collective-permute-done.4.refs_1_, f32[8,2,320,128]{3,2,1,0:T(8,128)S(1)} %shard_map.75.refs_2_), custom_call_target="tpu_custom_call", output_to_operand_aliasing={{}: (2, {})} | custom-call | flops 67108864 | bytes 4194304 | tf_op jit(solution)/shard_map/pallas_call | solution.py:311
  20.6 0.2 copy-done
  20.9 0.9 %shard_map.78.src_levels = f32[8,2,30,8,128]{4,3,2,1,0:T(8,128)S(1)} custom-call(f32[2,128,128]{2,1,0:T(8,128)S(1)} %bitcast.39, f32[2,128,128]{2,1,0:T(8,128)S(1)} %bitcast.42), custom_call_target="tpu_custom_call" | custom-call | flops 67108864 | bytes 4194304 | tf_op jit(solution)/shard_map/pallas_call | solution.py:311
  21.8 0.9 %shard_map.79.rec_levels = f32[8,2,30,8,128]{4,3,2,1,0:T(8,128)S(1)} custom-call(f32[2,128,128]{2,1,0:T(8,128)S(1)} %bitcast.40, f32[2,128,128]{2,1,0:T(8,128)S(1)} %bitcast.41), custom_call_target="tpu_custom_call" | custom-call | flops 67108864 | bytes 4194304 | tf_op jit(solution)/shard_map/pallas_call | solution.py:311
  22.7 0.6 %shard_map.77.coef_ref = f32[8,2,320,128]{3,2,1,0:T(8,128)S(1)} custom-call(f32[8,128]{1,0:T(8,128)S(1)} %get-tuple-element.20.refs_0_, f32[2,40,128]{2,1,0:T(8,128)S(1)} %collective-permute-done.5.refs_1_, f32[8,2,320,128]{3,2,1,0:T(8,128)S(1)} %shard_map.76.refs_2_), custom_call_target="tpu_custom_call", output_to_operand_aliasing={{}: (2, {})} | custom-call | flops 67108864 | bytes 4194304 | tf_op jit(solution)/shard_map/pallas_call | solution.py:311
  23.3 2.1 %shard_map.80 = (f32[128,128]{1,0:T(8,128)S(1)}, f32[128,128]{1,0:T(8,128)S(1)}, f32[4,16,8,128]{3,2,1,0:T(8,128)S(1)}) custom-call(f32[8,2,320,128]{3,2,1,0:T(8,128)S(1)} %shard_map.77.coef_ref, f32[8,2,30,8,128]{4,3,2,1,0:T(8,128)S(1)} %shard_map.78.src_levels, f32[8,2,30,8,128]{4,3,2,1,0:T(8,128)S(1)} %shard_map.79.rec_levels), custom_call_target="tpu_custom_call" | custom-call | tf_op jit(solution)/shard_map/pallas_call | solution.py:311
  25.5 1.2 %collective-permute-done.8 = f32[128,128]{1,0:T(8,128)S(1)} collective-permute-done((f32[128,128]{1,0:T(8,128)S(1)}, f32[128,128]{1,0:T(8,128)S(1)}, u32[]{:S(2)}, u32[]{:S(2)}) %collective-permute-start.8) | collective-permute-done | bytes 65568 | tf_op jit(solution)/shard_map/ppermute | solution.py:300
  26.7 1.4 %collective-permute-start.9 = (f32[4,16,128]{2,1,0:T(8,128)S(1)}, f32[4,16,128]{2,1,0:T(8,128)S(1)}, u32[]{:S(2)}, u32[]{:S(2)}) collective-permute-start(f32[4,16,128]{2,1,0:T(8,128)S(1)} %get-tuple-element.25), channel_id=1, source_target_pairs={{0,6},{2,4},{4,2},{6,0},{8,14},{10,12},{12,10},{14,8},{16,22},{18,... | collective-permute-start | bytes 98312 | tf_op jit(solution)/shard_map/ppermute | solution.py:300
  28.2 2.0 %collective-permute-done.9.came = f32[4,16,128]{2,1,0:T(8,128)S(1)} collective-permute-done((f32[4,16,128]{2,1,0:T(8,128)S(1)}, f32[4,16,128]{2,1,0:T(8,128)S(1)}, u32[]{:S(2)}, u32[]{:S(2)}) %collective-permute-start.9) | collective-permute-done | bytes 32800 | tf_op jit(solution)/shard_map/ppermute | solution.py:300
  30.2 1.5 %collective-permute-start.10 = (f32[2,16,128]{2,1,0:T(8,128)S(1)}, f32[2,16,128]{2,1,0:T(8,128)S(1)}, u32[]{:S(2)}, u32[]{:S(2)}) collective-permute-start(f32[2,16,128]{2,1,0:T(8,128)S(1)} %get-tuple-element.27), channel_id=1, source_target_pairs={{0,10},{2,8},{4,14},{6,12},{8,2},{10,0},{12,6},{14,4},{16,26},{18,... | collective-permute-start | bytes 49160 | tf_op jit(solution)/shard_map/ppermute | solution.py:300
  31.6 1.7 %collective-permute-done.10.came = f32[2,16,128]{2,1,0:T(8,128)S(1)} collective-permute-done((f32[2,16,128]{2,1,0:T(8,128)S(1)}, f32[2,16,128]{2,1,0:T(8,128)S(1)}, u32[]{:S(2)}, u32[]{:S(2)}) %collective-permute-start.10) | collective-permute-done | bytes 16416 | tf_op jit(solution)/shard_map/ppermute | solution.py:300
  33.3 2.5 %collective-permute-start.11 = (f32[1,16,128]{2,1,0:T(8,128)S(1)}, f32[1,16,128]{2,1,0:T(8,128)S(1)}, u32[]{:S(2)}, u32[]{:S(2)}) collective-permute-start(f32[1,16,128]{2,1,0:T(8,128)S(1)} %get-tuple-element.29), channel_id=1, source_target_pairs={{0,18},{2,16},{4,22},{6,20},{8,26},{10,24},{12,30},{14,28},{16,2},... | collective-permute-start | bytes 24584 | tf_op jit(solution)/shard_map/ppermute | solution.py:300
  35.8 0.7 %shard_map.85 = (f32[2,128,128]{2,1,0:T(8,128)}, f32[2,128,128]{2,1,0:T(8,128)}) custom-call(f32[4,16,8,128]{3,2,1,0:T(8,128)S(1)} %get-tuple-element.30.final_ref), custom_call_target="tpu_custom_call" | custom-call | flops 67108864 | bytes 4194304 | tf_op jit(solution)/shard_map/pallas_call | solution.py:311
  36.6 0.7 %collective-permute-done.11.came = f32[1,16,128]{2,1,0:T(8,128)S(1)} collective-permute-done((f32[1,16,128]{2,1,0:T(8,128)S(1)}, f32[1,16,128]{2,1,0:T(8,128)S(1)}, u32[]{:S(2)}, u32[]{:S(2)}) %collective-permute-start.11) | collective-permute-done | bytes 8224 | tf_op jit(solution)/shard_map/ppermute | solution.py:300
  37.3 0.7 %shard_map.84 = f32[2,16,64]{2,1,0:T(8,128)} custom-call(f32[1,16,128]{2,1,0:T(8,128)S(1)} %get-tuple-element.28.held, f32[1,16,128]{2,1,0:T(8,128)S(1)} %collective-permute-done.11.came), custom_call_target="tpu_custom_call" | custom-call | tf_op jit(solution)/shard_map/pallas_call | solution.py:311
  (14 shorter events, 0.1 us)
Async XLA Ops:
  0.6 1.6 %collective-permute-start = (f32[2,16,64]{2,1,0:T(8,128)}, f32[2,16,64]{2,1,0:T(8,128)S(1)}, u32[]{:S(2)}, u32[]{:S(2)}) collective-permute-start(f32[2,16,64]{2,1,0:T(8,128)} %param.5), channel_id=1, source_target_pairs={{0,2},{2,0},{4,6},{6,4},{8,10},{10,8},{12,14},{14,12},{16,18},{18,... | collective-permute-start | bytes 24584 | tf_op jit(solution)/shard_map/ppermute | solution.py:300
  2.3 4.4 %collective-permute-start.1 = (f32[8,128]{1,0:T(8,128)S(1)}, f32[8,128]{1,0:T(8,128)S(1)}, u32[]{:S(2)}, u32[]{:S(2)}) collective-permute-start(f32[8,128]{1,0:T(8,128)S(1)} %get-tuple-element.19), channel_id=1, source_target_pairs={{0,1},{1,0},{2,3},{3,2},{4,5},{5,4},{6,7},{7,6},{8,9},{9,8},{10,11... | collective-permute-start | bytes 12296 | tf_op jit(solution)/shard_map/ppermute | solution.py:293
  6.8 4.1 %collective-permute-start.2 = (f32[1,40,128]{2,1,0:T(8,128)S(1)}, f32[1,40,128]{2,1,0:T(8,128)S(1)}, u32[]{:S(2)}, u32[]{:S(2)}) collective-permute-start(f32[1,40,128]{2,1,0:T(8,128)S(1)} %bitcast.45), channel_id=1, source_target_pairs={{0,18},{2,16},{4,22},{6,20},{8,26},{10,24},{12,30},{14,28},{16,2},... | collective-permute-start | bytes 61448 | tf_op jit(solution)/shard_map/ppermute | solution.py:300
  8.5 12.2 %collective-permute-start.6 = (f32[1,2,16,1024]{3,2,1,0:T(8,128)}, f32[1,2,16,1024]{3,2,1,0:T(8,128)S(1)}, u32[]{:S(2)}, u32[]{:S(2)}) collective-permute-start(f32[1,2,16,1024]{3,2,1,0:T(8,128)} %param.6), channel_id=1, source_target_pairs={{0,1},{1,0},{2,3},{3,2},{4,5},{5,4},{6,7},{7,6},{8,9},{9,8},{10,11... | collective-permute-start | bytes 393224 | tf_op jit(solution)/shard_map/ppermute | solution.py:293
  10.0 11.8 %collective-permute-start.7 = (f32[1,2,16,1024]{3,2,1,0:T(8,128)}, f32[1,2,16,1024]{3,2,1,0:T(8,128)S(1)}, u32[]{:S(2)}, u32[]{:S(2)}) collective-permute-start(f32[1,2,16,1024]{3,2,1,0:T(8,128)} %param.7), channel_id=1, source_target_pairs={{0,1},{1,0},{2,3},{3,2},{4,5},{5,4},{6,7},{7,6},{8,9},{9,8},{10,11... | collective-permute-start | bytes 393224 | tf_op jit(solution)/shard_map/ppermute | solution.py:293
  10.9 3.5 %collective-permute-start.3 = (f32[2,40,128]{2,1,0:T(8,128)S(1)}, f32[2,40,128]{2,1,0:T(8,128)S(1)}, u32[]{:S(2)}, u32[]{:S(2)}) collective-permute-start(f32[2,40,128]{2,1,0:T(8,128)S(1)} %shard_map.72.first.refs_1_), channel_id=1, source_target_pairs={{0,10},{2,8},{4,14},{6,12},{8,2},{10,0},{12,6},{14,4},{16,26},{18,... | collective-permute-start | bytes 122888 | tf_op jit(solution)/shard_map/ppermute | solution.py:300
  14.4 3.8 %collective-permute-start.4 = (f32[2,40,128]{2,1,0:T(8,128)S(1)}, f32[2,40,128]{2,1,0:T(8,128)S(1)}, u32[]{:S(2)}, u32[]{:S(2)}) collective-permute-start(f32[2,40,128]{2,1,0:T(8,128)S(1)} %shard_map.73), channel_id=1, source_target_pairs={{0,6},{2,4},{4,2},{6,0},{8,14},{10,12},{12,10},{14,8},{16,22},{18,... | collective-permute-start | bytes 122888 | tf_op jit(solution)/shard_map/ppermute | solution.py:300
  18.2 4.5 %collective-permute-start.5 = (f32[2,40,128]{2,1,0:T(8,128)S(1)}, f32[2,40,128]{2,1,0:T(8,128)S(1)}, u32[]{:S(2)}, u32[]{:S(2)}) collective-permute-start(f32[2,40,128]{2,1,0:T(8,128)S(1)} %collective-permute-done.4.refs_1_), channel_id=1, source_target_pairs={{0,2},{2,0},{4,6},{6,4},{8,10},{10,8},{12,14},{14,12},{16,18},{18,... | collective-permute-start | bytes 122888 | tf_op jit(solution)/shard_map/ppermute | solution.py:300
  20.0 0.9 %copy-start = (f32[1,2,16,1024]{3,2,1,0:T(8,128)S(1)}, f32[1,2,16,1024]{3,2,1,0:T(8,128)}, u32[]{:S(2)}) copy-start(f32[1,2,16,1024]{3,2,1,0:T(8,128)} %param.6) | copy-start | bytes 393220
  20.0 1.8 %copy-start.1 = (f32[1,2,16,1024]{3,2,1,0:T(8,128)S(1)}, f32[1,2,16,1024]{3,2,1,0:T(8,128)}, u32[]{:S(2)}) copy-start(f32[1,2,16,1024]{3,2,1,0:T(8,128)} %param.7) | copy-start | bytes 393220
  25.4 1.3 %collective-permute-start.8 = (f32[128,128]{1,0:T(8,128)S(1)}, f32[128,128]{1,0:T(8,128)S(1)}, u32[]{:S(2)}, u32[]{:S(2)}) collective-permute-start(f32[128,128]{1,0:T(8,128)S(1)} %get-tuple-element.23), channel_id=1, source_target_pairs={{0,2},{2,0},{4,6},{6,4},{8,10},{10,8},{12,14},{14,12},{16,18},{18,... | collective-permute-start | bytes 196616 | tf_op jit(solution)/shard_map/ppermute | solution.py:300
  26.7 3.4 %collective-permute-start.9 = (f32[4,16,128]{2,1,0:T(8,128)S(1)}, f32[4,16,128]{2,1,0:T(8,128)S(1)}, u32[]{:S(2)}, u32[]{:S(2)}) collective-permute-start(f32[4,16,128]{2,1,0:T(8,128)S(1)} %get-tuple-element.25), channel_id=1, source_target_pairs={{0,6},{2,4},{4,2},{6,0},{8,14},{10,12},{12,10},{14,8},{16,22},{18,... | collective-permute-start | bytes 98312 | tf_op jit(solution)/shard_map/ppermute | solution.py:300
  30.2 3.2 %collective-permute-start.10 = (f32[2,16,128]{2,1,0:T(8,128)S(1)}, f32[2,16,128]{2,1,0:T(8,128)S(1)}, u32[]{:S(2)}, u32[]{:S(2)}) collective-permute-start(f32[2,16,128]{2,1,0:T(8,128)S(1)} %get-tuple-element.27), channel_id=1, source_target_pairs={{0,10},{2,8},{4,14},{6,12},{8,2},{10,0},{12,6},{14,4},{16,26},{18,... | collective-permute-start | bytes 49160 | tf_op jit(solution)/shard_map/ppermute | solution.py:300
  33.3 4.0 %collective-permute-start.11 = (f32[1,16,128]{2,1,0:T(8,128)S(1)}, f32[1,16,128]{2,1,0:T(8,128)S(1)}, u32[]{:S(2)}, u32[]{:S(2)}) collective-permute-start(f32[1,16,128]{2,1,0:T(8,128)S(1)} %get-tuple-element.29), channel_id=1, source_target_pairs={{0,18},{2,16},{4,22},{6,20},{8,26},{10,24},{12,30},{14,28},{16,2},... | collective-permute-start | bytes 24584 | tf_op jit(solution)/shard_map/ppermute | solution.py:300

commit v6 on v5

--- a/solution.py
+++ b/solution.py
@@ -109,15 +109,16 @@
     for order in range(1, TERMS):
         left = TERMS - 1 - order
         begin, end = (low if two else low - left), high + left
-        above = [None if two else spread(levels[order - 1, f, begin - 1 - lowest]) for f in fields]
-        here = [spread(levels[order - 1, f, begin - lowest]) for f in fields]
+        above = [None if two else levels[order - 1, f, begin - 1 - lowest] for f in fields]
+        here = [levels[order - 1, f, begin - lowest] for f in fields]
         for row in range(begin, end):
             for k, f in enumerate(fields):
-                below = spread(levels[order - 1, f, row + 1 - lowest])
-                total = (here[k] + here[k]) + below
+                below = levels[order - 1, f, row + 1 - lowest]
+                centre = here[k]
+                total = (centre + centre) + below
                 if above[k] is not None:
                     total = total + above[k]
-                centre = levels[order - 1, f, row - lowest]
+                total = spread(total)
                 if order == 1:
                     value = 0.125 * total - centre
                 else:

time: 38.3 us -> 38.2 us (level)
  no operation moved by 1% of the time
where the time goes in v6:
time: 38.2 us; the launch traced here: 37.9 us
  starting transfers between devices  17.1 us (45%)
  waiting for transfers between devices  10.7 us (28%)
  Pallas kernels  7.79 us (20%)
  between operations  1.4 us (4%)
  local copies, waits for them, and re-layouts  0.97 us (3%)
    ppermute x9, starting transfers between devices, partner(): lax.ppermute(block, 'freq', [(i, i ^ mask) for i in range(lax.axis_size('...  12.2 us
    ppermute x9, waiting for transfers between devices, partner(): lax.ppermute(block, 'freq', [(i, i ^ mask) for i in range(lax.axis_size('...  9.73 us
    pallas_call x16, Pallas kernels, call(): pl.pallas_call(kernel, out_shape=outs[0] if single else outs, out_specs=V...  7.79 us
    ppermute x3, starting transfers between devices, from_sides(): return [lax.ppermute(block, 'lat', [(0, 1), (1, 0)])]  4.87 us
    ppermute x3, waiting for transfers between devices, from_sides(): return [lax.ppermute(block, 'lat', [(0, 1), (1, 0)])]  0.94 us
  transfers between devices with their start and end apart: 12, of which 9 were waited for; matrix products, arithmetic and copies ran while one was open for 2% of the time, Pallas kernels for 11%

profile of v6, /device:TPU:0, one launch (start us, length us, event | category | flops | bytes accessed | tf_op | source)
XLA Modules:
  0.0 37.9 jit_solution(11345174619081420799)
XLA Ops:
  0.6 0.6 %collective-permute-start = (f32[2,16,64]{2,1,0:T(8,128)}, f32[2,16,64]{2,1,0:T(8,128)S(1)}, u32[]{:S(2)}, u32[]{:S(2)}) collective-permute-start(f32[2,16,64]{2,1,0:T(8,128)} %param.5), channel_id=1, source_target_pairs={{0,2},{2,0},{4,6},{6,4},{8,10},{10,8},{12,14},{14,12},{16,18},{18,... | collective-permute-start | bytes 24584 | tf_op jit(solution)/shard_map/ppermute | solution.py:301
  1.2 0.7 %slice_bitcast_fusion = (f32[16,64]{1,0:T(8,128)S(1)}, f32[16,64]{1,0:T(8,128)S(1)}) fusion(f32[2,16,64]{2,1,0:T(8,128)} %param.5), kind=kLoop, calls=%fused_computation | loop fusion | bytes 16384 | tf_op jit(solution)/shard_map/squeeze | solution.py:446
  1.9 0.3 collective-permute-done.refs_2_
  2.2 0.1 shard_map.70
  2.3 2.8 %collective-permute-start.1 = (f32[8,128]{1,0:T(8,128)S(1)}, f32[8,128]{1,0:T(8,128)S(1)}, u32[]{:S(2)}, u32[]{:S(2)}) collective-permute-start(f32[8,128]{1,0:T(8,128)S(1)} %get-tuple-element.19), channel_id=1, source_target_pairs={{0,1},{1,0},{2,3},{3,2},{4,5},{5,4},{6,7},{7,6},{8,9},{9,8},{10,11... | collective-permute-start | bytes 12296 | tf_op jit(solution)/shard_map/ppermute | solution.py:294
  5.8 0.9 %collective-permute-done.1.edge = f32[8,128]{1,0:T(8,128)S(1)} collective-permute-done((f32[8,128]{1,0:T(8,128)S(1)}, f32[8,128]{1,0:T(8,128)S(1)}, u32[]{:S(2)}, u32[]{:S(2)}) %collective-permute-start.1) | collective-permute-done | bytes 4128 | tf_op jit(solution)/shard_map/ppermute | solution.py:294
  6.8 1.7 %collective-permute-start.2 = (f32[1,40,128]{2,1,0:T(8,128)S(1)}, f32[1,40,128]{2,1,0:T(8,128)S(1)}, u32[]{:S(2)}, u32[]{:S(2)}) collective-permute-start(f32[1,40,128]{2,1,0:T(8,128)S(1)} %bitcast.45), channel_id=1, source_target_pairs={{0,18},{2,16},{4,22},{6,20},{8,26},{10,24},{12,30},{14,28},{16,2},... | collective-permute-start | bytes 61448 | tf_op jit(solution)/shard_map/ppermute | solution.py:301
  8.5 1.5 %collective-permute-start.6 = (f32[1,2,16,1024]{3,2,1,0:T(8,128)}, f32[1,2,16,1024]{3,2,1,0:T(8,128)S(1)}, u32[]{:S(2)}, u32[]{:S(2)}) collective-permute-start(f32[1,2,16,1024]{3,2,1,0:T(8,128)} %param.6), channel_id=1, source_target_pairs={{0,1},{1,0},{2,3},{3,2},{4,5},{5,4},{6,7},{7,6},{8,9},{9,8},{10,11... | collective-permute-start | bytes 393224 | tf_op jit(solution)/shard_map/ppermute | solution.py:294
  10.0 0.5 %collective-permute-start.7 = (f32[1,2,16,1024]{3,2,1,0:T(8,128)}, f32[1,2,16,1024]{3,2,1,0:T(8,128)S(1)}, u32[]{:S(2)}, u32[]{:S(2)}) collective-permute-start(f32[1,2,16,1024]{3,2,1,0:T(8,128)} %param.7), channel_id=1, source_target_pairs={{0,1},{1,0},{2,3},{3,2},{4,5},{5,4},{6,7},{7,6},{8,9},{9,8},{10,11... | collective-permute-start | bytes 393224 | tf_op jit(solution)/shard_map/ppermute | solution.py:294
  10.5 0.4 collective-permute-done.2.other
  10.9 1.8 %collective-permute-start.3 = (f32[2,40,128]{2,1,0:T(8,128)S(1)}, f32[2,40,128]{2,1,0:T(8,128)S(1)}, u32[]{:S(2)}, u32[]{:S(2)}) collective-permute-start(f32[2,40,128]{2,1,0:T(8,128)S(1)} %shard_map.72.first.refs_1_), channel_id=1, source_target_pairs={{0,10},{2,8},{4,14},{6,12},{8,2},{10,0},{12,6},{14,4},{16,26},{18,... | collective-permute-start | bytes 122888 | tf_op jit(solution)/shard_map/ppermute | solution.py:301
  12.7 1.7 %collective-permute-done.3.second.refs_1_ = f32[2,40,128]{2,1,0:T(8,128)S(1)} collective-permute-done((f32[2,40,128]{2,1,0:T(8,128)S(1)}, f32[2,40,128]{2,1,0:T(8,128)S(1)}, u32[]{:S(2)}, u32[]{:S(2)}) %collective-permute-start.3) | collective-permute-done | bytes 40992 | tf_op jit(solution)/shard_map/ppermute | solution.py:301
  14.4 2.1 %collective-permute-start.4 = (f32[2,40,128]{2,1,0:T(8,128)S(1)}, f32[2,40,128]{2,1,0:T(8,128)S(1)}, u32[]{:S(2)}, u32[]{:S(2)}) collective-permute-start(f32[2,40,128]{2,1,0:T(8,128)S(1)} %shard_map.73), channel_id=1, source_target_pairs={{0,6},{2,4},{4,2},{6,0},{8,14},{10,12},{12,10},{14,8},{16,22},{18,... | collective-permute-start | bytes 122888 | tf_op jit(solution)/shard_map/ppermute | solution.py:301
  16.5 1.7 %collective-permute-done.4.refs_1_ = f32[2,40,128]{2,1,0:T(8,128)S(1)} collective-permute-done((f32[2,40,128]{2,1,0:T(8,128)S(1)}, f32[2,40,128]{2,1,0:T(8,128)S(1)}, u32[]{:S(2)}, u32[]{:S(2)}) %collective-permute-start.4) | collective-permute-done | bytes 40992 | tf_op jit(solution)/shard_map/ppermute | solution.py:301
  18.2 0.5 %collective-permute-start.5 = (f32[2,40,128]{2,1,0:T(8,128)S(1)}, f32[2,40,128]{2,1,0:T(8,128)S(1)}, u32[]{:S(2)}, u32[]{:S(2)}) collective-permute-start(f32[2,40,128]{2,1,0:T(8,128)S(1)} %collective-permute-done.4.refs_1_), channel_id=1, source_target_pairs={{0,2},{2,0},{4,6},{6,4},{8,10},{10,8},{12,14},{14,12},{16,18},{18,... | collective-permute-start | bytes 122888 | tf_op jit(solution)/shard_map/ppermute | solution.py:301
  18.7 0.6 %shard_map.74.refs_2_ = f32[8,2,320,128]{3,2,1,0:T(8,128)S(1)} custom-call(f32[8,128]{1,0:T(8,128)S(1)} %get-tuple-element.20.refs_0_, f32[2,40,128]{2,1,0:T(8,128)S(1)} %shard_map.72.first.refs_1_), custom_call_target="tpu_custom_call" | custom-call | flops 67108864 | bytes 4194304 | tf_op jit(solution)/shard_map/pallas_call | solution.py:312
  19.4 0.6 %shard_map.75.refs_2_ = f32[8,2,320,128]{3,2,1,0:T(8,128)S(1)} custom-call(f32[8,128]{1,0:T(8,128)S(1)} %get-tuple-element.20.refs_0_, f32[2,40,128]{2,1,0:T(8,128)S(1)} %collective-permute-done.3.second.refs_1_, f32[8,2,320,128]{3,2,1,0:T(8,128)S(1)} %shard_map.74.refs_2_), custom_call_target="tpu_custom_call", output_to_operand_aliasing={{}: (2, {})} | custom-call | flops 67108864 | bytes 4194304 | tf_op jit(solution)/shard_map/pallas_call | solution.py:312
  20.0 0.6 %shard_map.76.refs_2_ = f32[8,2,320,128]{3,2,1,0:T(8,128)S(1)} custom-call(f32[8,128]{1,0:T(8,128)S(1)} %get-tuple-element.20.refs_0_, f32[2,40,128]{2,1,0:T(8,128)S(1)} %collective-permute-done.4.refs_1_, f32[8,2,320,128]{3,2,1,0:T(8,128)S(1)} %shard_map.75.refs_2_), custom_call_target="tpu_custom_call", output_to_operand_aliasing={{}: (2, {})} | custom-call | flops 67108864 | bytes 4194304 | tf_op jit(solution)/shard_map/pallas_call | solution.py:312
  20.6 0.2 copy-done
  20.9 0.8 %shard_map.78.src_levels = f32[8,2,30,8,128]{4,3,2,1,0:T(8,128)S(1)} custom-call(f32[2,128,128]{2,1,0:T(8,128)S(1)} %bitcast.39, f32[2,128,128]{2,1,0:T(8,128)S(1)} %bitcast.42), custom_call_target="tpu_custom_call" | custom-call | flops 67108864 | bytes 4194304 | tf_op jit(solution)/shard_map/pallas_call | solution.py:312
  21.8 0.9 %shard_map.79.rec_levels = f32[8,2,30,8,128]{4,3,2,1,0:T(8,128)S(1)} custom-call(f32[2,128,128]{2,1,0:T(8,128)S(1)} %bitcast.40, f32[2,128,128]{2,1,0:T(8,128)S(1)} %bitcast.41), custom_call_target="tpu_custom_call" | custom-call | flops 67108864 | bytes 4194304 | tf_op jit(solution)/shard_map/pallas_call | solution.py:312
  22.6 0.6 %shard_map.77.coef_ref = f32[8,2,320,128]{3,2,1,0:T(8,128)S(1)} custom-call(f32[8,128]{1,0:T(8,128)S(1)} %get-tuple-element.20.refs_0_, f32[2,40,128]{2,1,0:T(8,128)S(1)} %collective-permute-done.5.refs_1_, f32[8,2,320,128]{3,2,1,0:T(8,128)S(1)} %shard_map.76.refs_2_), custom_call_target="tpu_custom_call", output_to_operand_aliasing={{}: (2, {})} | custom-call | flops 67108864 | bytes 4194304 | tf_op jit(solution)/shard_map/pallas_call | solution.py:312
  23.3 2.1 %shard_map.80 = (f32[128,128]{1,0:T(8,128)S(1)}, f32[128,128]{1,0:T(8,128)S(1)}, f32[4,16,8,128]{3,2,1,0:T(8,128)S(1)}) custom-call(f32[8,2,320,128]{3,2,1,0:T(8,128)S(1)} %shard_map.77.coef_ref, f32[8,2,30,8,128]{4,3,2,1,0:T(8,128)S(1)} %shard_map.78.src_levels, f32[8,2,30,8,128]{4,3,2,1,0:T(8,128)S(1)} %shard_map.79.rec_levels), custom_call_target="tpu_custom_call" | custom-call | tf_op jit(solution)/shard_map/pallas_call | solution.py:312
  25.4 1.2 %collective-permute-done.8 = f32[128,128]{1,0:T(8,128)S(1)} collective-permute-done((f32[128,128]{1,0:T(8,128)S(1)}, f32[128,128]{1,0:T(8,128)S(1)}, u32[]{:S(2)}, u32[]{:S(2)}) %collective-permute-start.8) | collective-permute-done | bytes 65568 | tf_op jit(solution)/shard_map/ppermute | solution.py:301
  26.7 1.4 %collective-permute-start.9 = (f32[4,16,128]{2,1,0:T(8,128)S(1)}, f32[4,16,128]{2,1,0:T(8,128)S(1)}, u32[]{:S(2)}, u32[]{:S(2)}) collective-permute-start(f32[4,16,128]{2,1,0:T(8,128)S(1)} %get-tuple-element.25), channel_id=1, source_target_pairs={{0,6},{2,4},{4,2},{6,0},{8,14},{10,12},{12,10},{14,8},{16,22},{18,... | collective-permute-start | bytes 98312 | tf_op jit(solution)/shard_map/ppermute | solution.py:301
  28.1 2.0 %collective-permute-done.9.came = f32[4,16,128]{2,1,0:T(8,128)S(1)} collective-permute-done((f32[4,16,128]{2,1,0:T(8,128)S(1)}, f32[4,16,128]{2,1,0:T(8,128)S(1)}, u32[]{:S(2)}, u32[]{:S(2)}) %collective-permute-start.9) | collective-permute-done | bytes 32800 | tf_op jit(solution)/shard_map/ppermute | solution.py:301
  30.1 1.5 %collective-permute-start.10 = (f32[2,16,128]{2,1,0:T(8,128)S(1)}, f32[2,16,128]{2,1,0:T(8,128)S(1)}, u32[]{:S(2)}, u32[]{:S(2)}) collective-permute-start(f32[2,16,128]{2,1,0:T(8,128)S(1)} %get-tuple-element.27), channel_id=1, source_target_pairs={{0,10},{2,8},{4,14},{6,12},{8,2},{10,0},{12,6},{14,4},{16,26},{18,... | collective-permute-start | bytes 49160 | tf_op jit(solution)/shard_map/ppermute | solution.py:301
  31.5 1.7 %collective-permute-done.10.came = f32[2,16,128]{2,1,0:T(8,128)S(1)} collective-permute-done((f32[2,16,128]{2,1,0:T(8,128)S(1)}, f32[2,16,128]{2,1,0:T(8,128)S(1)}, u32[]{:S(2)}, u32[]{:S(2)}) %collective-permute-start.10) | collective-permute-done | bytes 16416 | tf_op jit(solution)/shard_map/ppermute | solution.py:301
  33.2 2.5 %collective-permute-start.11 = (f32[1,16,128]{2,1,0:T(8,128)S(1)}, f32[1,16,128]{2,1,0:T(8,128)S(1)}, u32[]{:S(2)}, u32[]{:S(2)}) collective-permute-start(f32[1,16,128]{2,1,0:T(8,128)S(1)} %get-tuple-element.29), channel_id=1, source_target_pairs={{0,18},{2,16},{4,22},{6,20},{8,26},{10,24},{12,30},{14,28},{16,2},... | collective-permute-start | bytes 24584 | tf_op jit(solution)/shard_map/ppermute | solution.py:301
  35.7 0.7 %shard_map.85 = (f32[2,128,128]{2,1,0:T(8,128)}, f32[2,128,128]{2,1,0:T(8,128)}) custom-call(f32[4,16,8,128]{3,2,1,0:T(8,128)S(1)} %get-tuple-element.30.final_ref), custom_call_target="tpu_custom_call" | custom-call | flops 67108864 | bytes 4194304 | tf_op jit(solution)/shard_map/pallas_call | solution.py:312
  36.5 0.7 %collective-permute-done.11.came = f32[1,16,128]{2,1,0:T(8,128)S(1)} collective-permute-done((f32[1,16,128]{2,1,0:T(8,128)S(1)}, f32[1,16,128]{2,1,0:T(8,128)S(1)}, u32[]{:S(2)}, u32[]{:S(2)}) %collective-permute-start.11) | collective-permute-done | bytes 8224 | tf_op jit(solution)/shard_map/ppermute | solution.py:301
  37.2 0.7 %shard_map.84 = f32[2,16,64]{2,1,0:T(8,128)} custom-call(f32[1,16,128]{2,1,0:T(8,128)S(1)} %get-tuple-element.28.held, f32[1,16,128]{2,1,0:T(8,128)S(1)} %collective-permute-done.11.came), custom_call_target="tpu_custom_call" | custom-call | tf_op jit(solution)/shard_map/pallas_call | solution.py:312
  (14 shorter events, 0.1 us)
Async XLA Ops:
  0.6 1.6 %collective-permute-start = (f32[2,16,64]{2,1,0:T(8,128)}, f32[2,16,64]{2,1,0:T(8,128)S(1)}, u32[]{:S(2)}, u32[]{:S(2)}) collective-permute-start(f32[2,16,64]{2,1,0:T(8,128)} %param.5), channel_id=1, source_target_pairs={{0,2},{2,0},{4,6},{6,4},{8,10},{10,8},{12,14},{14,12},{16,18},{18,... | collective-permute-start | bytes 24584 | tf_op jit(solution)/shard_map/ppermute | solution.py:301
  2.3 4.4 %collective-permute-start.1 = (f32[8,128]{1,0:T(8,128)S(1)}, f32[8,128]{1,0:T(8,128)S(1)}, u32[]{:S(2)}, u32[]{:S(2)}) collective-permute-start(f32[8,128]{1,0:T(8,128)S(1)} %get-tuple-element.19), channel_id=1, source_target_pairs={{0,1},{1,0},{2,3},{3,2},{4,5},{5,4},{6,7},{7,6},{8,9},{9,8},{10,11... | collective-permute-start | bytes 12296 | tf_op jit(solution)/shard_map/ppermute | solution.py:294
  6.8 4.1 %collective-permute-start.2 = (f32[1,40,128]{2,1,0:T(8,128)S(1)}, f32[1,40,128]{2,1,0:T(8,128)S(1)}, u32[]{:S(2)}, u32[]{:S(2)}) collective-permute-start(f32[1,40,128]{2,1,0:T(8,128)S(1)} %bitcast.45), channel_id=1, source_target_pairs={{0,18},{2,16},{4,22},{6,20},{8,26},{10,24},{12,30},{14,28},{16,2},... | collective-permute-start | bytes 61448 | tf_op jit(solution)/shard_map/ppermute | solution.py:301
  8.5 12.2 %collective-permute-start.6 = (f32[1,2,16,1024]{3,2,1,0:T(8,128)}, f32[1,2,16,1024]{3,2,1,0:T(8,128)S(1)}, u32[]{:S(2)}, u32[]{:S(2)}) collective-permute-start(f32[1,2,16,1024]{3,2,1,0:T(8,128)} %param.6), channel_id=1, source_target_pairs={{0,1},{1,0},{2,3},{3,2},{4,5},{5,4},{6,7},{7,6},{8,9},{9,8},{10,11... | collective-permute-start | bytes 393224 | tf_op jit(solution)/shard_map/ppermute | solution.py:294
  10.0 11.8 %collective-permute-start.7 = (f32[1,2,16,1024]{3,2,1,0:T(8,128)}, f32[1,2,16,1024]{3,2,1,0:T(8,128)S(1)}, u32[]{:S(2)}, u32[]{:S(2)}) collective-permute-start(f32[1,2,16,1024]{3,2,1,0:T(8,128)} %param.7), channel_id=1, source_target_pairs={{0,1},{1,0},{2,3},{3,2},{4,5},{5,4},{6,7},{7,6},{8,9},{9,8},{10,11... | collective-permute-start | bytes 393224 | tf_op jit(solution)/shard_map/ppermute | solution.py:294
  10.9 3.5 %collective-permute-start.3 = (f32[2,40,128]{2,1,0:T(8,128)S(1)}, f32[2,40,128]{2,1,0:T(8,128)S(1)}, u32[]{:S(2)}, u32[]{:S(2)}) collective-permute-start(f32[2,40,128]{2,1,0:T(8,128)S(1)} %shard_map.72.first.refs_1_), channel_id=1, source_target_pairs={{0,10},{2,8},{4,14},{6,12},{8,2},{10,0},{12,6},{14,4},{16,26},{18,... | collective-permute-start | bytes 122888 | tf_op jit(solution)/shard_map/ppermute | solution.py:301
  14.4 3.8 %collective-permute-start.4 = (f32[2,40,128]{2,1,0:T(8,128)S(1)}, f32[2,40,128]{2,1,0:T(8,128)S(1)}, u32[]{:S(2)}, u32[]{:S(2)}) collective-permute-start(f32[2,40,128]{2,1,0:T(8,128)S(1)} %shard_map.73), channel_id=1, source_target_pairs={{0,6},{2,4},{4,2},{6,0},{8,14},{10,12},{12,10},{14,8},{16,22},{18,... | collective-permute-start | bytes 122888 | tf_op jit(solution)/shard_map/ppermute | solution.py:301
  18.2 4.4 %collective-permute-start.5 = (f32[2,40,128]{2,1,0:T(8,128)S(1)}, f32[2,40,128]{2,1,0:T(8,128)S(1)}, u32[]{:S(2)}, u32[]{:S(2)}) collective-permute-start(f32[2,40,128]{2,1,0:T(8,128)S(1)} %collective-permute-done.4.refs_1_), channel_id=1, source_target_pairs={{0,2},{2,0},{4,6},{6,4},{8,10},{10,8},{12,14},{14,12},{16,18},{18,... | collective-permute-start | bytes 122888 | tf_op jit(solution)/shard_map/ppermute | solution.py:301
  20.0 0.9 %copy-start = (f32[1,2,16,1024]{3,2,1,0:T(8,128)S(1)}, f32[1,2,16,1024]{3,2,1,0:T(8,128)}, u32[]{:S(2)}) copy-start(f32[1,2,16,1024]{3,2,1,0:T(8,128)} %param.6) | copy-start | bytes 393220
  20.0 1.8 %copy-start.1 = (f32[1,2,16,1024]{3,2,1,0:T(8,128)S(1)}, f32[1,2,16,1024]{3,2,1,0:T(8,128)}, u32[]{:S(2)}) copy-start(f32[1,2,16,1024]{3,2,1,0:T(8,128)} %param.7) | copy-start | bytes 393220
  25.3 1.3 %collective-permute-start.8 = (f32[128,128]{1,0:T(8,128)S(1)}, f32[128,128]{1,0:T(8,128)S(1)}, u32[]{:S(2)}, u32[]{:S(2)}) collective-permute-start(f32[128,128]{1,0:T(8,128)S(1)} %get-tuple-element.23), channel_id=1, source_target_pairs={{0,2},{2,0},{4,6},{6,4},{8,10},{10,8},{12,14},{14,12},{16,18},{18,... | collective-permute-start | bytes 196616 | tf_op jit(solution)/shard_map/ppermute | solution.py:301
  26.7 3.4 %collective-permute-start.9 = (f32[4,16,128]{2,1,0:T(8,128)S(1)}, f32[4,16,128]{2,1,0:T(8,128)S(1)}, u32[]{:S(2)}, u32[]{:S(2)}) collective-permute-start(f32[4,16,128]{2,1,0:T(8,128)S(1)} %get-tuple-element.25), channel_id=1, source_target_pairs={{0,6},{2,4},{4,2},{6,0},{8,14},{10,12},{12,10},{14,8},{16,22},{18,... | collective-permute-start | bytes 98312 | tf_op jit(solution)/shard_map/ppermute | solution.py:301
  30.1 3.2 %collective-permute-start.10 = (f32[2,16,128]{2,1,0:T(8,128)S(1)}, f32[2,16,128]{2,1,0:T(8,128)S(1)}, u32[]{:S(2)}, u32[]{:S(2)}) collective-permute-start(f32[2,16,128]{2,1,0:T(8,128)S(1)} %get-tuple-element.27), channel_id=1, source_target_pairs={{0,10},{2,8},{4,14},{6,12},{8,2},{10,0},{12,6},{14,4},{16,26},{18,... | collective-permute-start | bytes 49160 | tf_op jit(solution)/shard_map/ppermute | solution.py:301
  33.2 4.0 %collective-permute-start.11 = (f32[1,16,128]{2,1,0:T(8,128)S(1)}, f32[1,16,128]{2,1,0:T(8,128)S(1)}, u32[]{:S(2)}, u32[]{:S(2)}) collective-permute-start(f32[1,16,128]{2,1,0:T(8,128)S(1)} %get-tuple-element.29), channel_id=1, source_target_pairs={{0,18},{2,16},{4,22},{6,20},{8,26},{10,24},{12,30},{14,28},{16,2},... | collective-permute-start | bytes 24584 | tf_op jit(solution)/shard_map/ppermute | solution.py:301
